TPU v7x, 128 devices: a whole 4x4x4 slice. The times are simulated.
128 devices in a mesh: bins: 8 (over x_hi, y), tiles: 16 (over z, x_lo, core).
Axes of the slice: x: 4 (x_hi: 2, x_lo: 2; x = x_hi * 2 + x_lo), y: 4, z: 4, core: 2. Of those that a mesh axis runs over, the one named last changes fastest.
Arguments:
- spectrum: float32 [1152, 128, 1440], P('bins', 'tiles'), as said below
- sea_mask: int32 [128, 1440], P('tiles'), may hold values 0 or 1
- ice_mask: int32 [128, 1440], P('tiles'), may hold values 0 or 1
- friction: float32 [128, 1440], P('tiles'), may hold values from 0.2 to 1
- wind_dir: float32 [128, 1440], P('tiles'), may hold values from -3.140625 to 3.140625
- ocean_owner: int32 [16, 16], P('tiles'), may hold values from 0 to 7, as said below
Outputs:
- spectrum_next: float32 [1152, 128, 1440], P('bins', 'tiles')
- stokes_drift: float32 [2, 128, 16, 90], P(None, 'tiles', 'bins')
- wave_stress: float32 [2, 128, 16, 90], P(None, 'tiles', 'bins')
Inputs may be any that keep to these rules, and one draw needn't show every extreme that they name: The spectrum is positive everywhere. `ocean_owner`: in every row each owner index appears exactly 2 times.
All inputs are finite; a program needn't handle non-finite values. No bound on the sum of `sea_mask` or of `ice_mask` on one device may be relied on, other than what follows from the above.
Results may differ from a plain program's by a relative error of at most 0.0001.
Values sent between devices are 32-bit elements; how exact they have to be, the bound alone decides.
No kernel may reach another device: no remote copies, remote signals or barrier semaphores. Data moves between devices by JAX's collectives and lax.ppermute only.
A program may use at most 192 MiB of HBM per device.

v0:
```python
import math

import jax
import jax.numpy as jnp
from jax import lax
from jax.sharding import PartitionSpec as P

NDIR = 36
NFREQ = 32
LON_BLOCKS = 16
STEPS = 4


courant_max = 0.6
grid_step = 0.25 * math.pi / 180.0


def extended(cells, sides, width):
    for axis, dim in sides:
        count = lax.axis_size(axis)
        ends = count - 1
        head = lax.slice_in_dim(cells, 0, width, axis=dim)
        tail = lax.slice_in_dim(cells, cells.shape[dim] - width, cells.shape[dim], axis=dim)
        cells = jnp.concatenate(
            [
                lax.ppermute(tail, axis, [(i, (i + 1) % count) for i in range(ends)]),
                cells,
                lax.ppermute(head, axis, [((i + 1) % count, i) for i in range(ends)]),
            ],
            axis=dim,
        )
    return cells


def row_metric(first_row, count, lat_total):
    row_pos = (first_row + jnp.arange(count)).astype(jnp.float32)
    latitude = (row_pos - lat_total / 2 + 0.5) * grid_step
    edge_lat = (lat_total / 2 - 0.5) * grid_step
    return jnp.cos(jnp.asarray(edge_lat, jnp.float32)) / jnp.cos(latitude)


def advance(center, south_row, north_row, sea_open, courant_x, courant_y):
    west_cell = jnp.roll(center, 1, axis=2)
    east_cell = jnp.roll(center, -1, axis=2)
    result = center - jnp.maximum(courant_x, 0.0) * (center - west_cell)
    result = result - jnp.maximum(-courant_x, 0.0) * (center - east_cell)
    result = result - jnp.maximum(courant_y, 0.0) * (center - south_row)
    result = result - jnp.maximum(-courant_y, 0.0) * (center - north_row)
    return result * sea_open


def shards(spectrum, sea_mask, ice_mask, friction, wind_dir, ocean_owner):
    local_bins, lat_rows, lon_cells = spectrum.shape
    lat_total = lat_rows * lax.axis_size("tiles")
    first_row = lax.axis_index("tiles") * lat_rows
    bin_index = lax.axis_index("bins") * local_bins + jnp.arange(local_bins)
    freq_pos = (bin_index // NDIR).astype(jnp.float32)
    angles = ((bin_index % NDIR).astype(jnp.float32) + 0.5) * (2.0 * math.pi / NDIR)
    speed_ratio = jnp.power(1.1, -freq_pos)
    freq_weight = jnp.power(1.03, freq_pos - (NFREQ - 1))
    cos_dir = jnp.cos(angles)
    sin_dir = jnp.sin(angles)
    sea_open = sea_mask.astype(jnp.float32)
    courant_y = (courant_max * speed_ratio * sin_dir)[:, None, None]
    base_x = courant_max * speed_ratio * cos_dir
    spectral = spectrum * sea_open
    metric = row_metric(first_row, lat_rows, lat_total)
    courant_x = base_x[:, None, None] * metric[None, :, None]
    for sub_step in range(STEPS):
        padded = extended(spectral, (("tiles", 1),), 1)
        spectral = advance(spectral, padded[:, :-2], padded[:, 2:], sea_open, courant_x, courant_y)
    growth = (
        0.5
        * friction[None] ** 2
        * freq_weight[:, None, None]
        * jnp.maximum(jnp.cos(angles[:, None, None] - wind_dir[None]), 0.0)
    )
    source = growth * spectral
    updated = (spectral + source) * (1.0 - 0.5 * ice_mask.astype(jnp.float32))
    drift_weights = jnp.stack([freq_weight * cos_dir, freq_weight * sin_dir])
    stress_weights = jnp.stack([cos_dir, sin_dir])
    drift_terms = jnp.dot(
        drift_weights,
        updated.reshape(local_bins, -1),
        precision=lax.Precision.HIGHEST,
        preferred_element_type=jnp.float32,
    )
    stress_terms = jnp.dot(
        stress_weights,
        source.reshape(local_bins, -1),
        precision=lax.Precision.HIGHEST,
        preferred_element_type=jnp.float32,
    )
    ocean_order = jnp.argsort(ocean_owner[0], stable=True)
    block_cells = lon_cells // LON_BLOCKS
    drift_terms = jnp.take(
        drift_terms.reshape(2, lat_rows, LON_BLOCKS, block_cells), ocean_order, axis=2
    )
    stress_terms = jnp.take(
        stress_terms.reshape(2, lat_rows, LON_BLOCKS, block_cells), ocean_order, axis=2
    )
    drift_total, stress_total = lax.psum((drift_terms, stress_terms), "bins")
    owned = LON_BLOCKS // lax.axis_size("bins")
    offset = lax.axis_index("bins") * owned
    drift_out = lax.dynamic_slice_in_dim(drift_total, offset, owned, 2)
    stress_out = lax.dynamic_slice_in_dim(stress_total, offset, owned, 2)
    return (updated, drift_out, stress_out)


def solution(mesh):
    placed = (
        P("bins", "tiles", None),
        P("tiles", None),
        P("tiles", None),
        P("tiles", None),
        P("tiles", None),
        P("tiles", None),
    )
    return jax.shard_map(
        shards,
        mesh=mesh,
        in_specs=placed,
        out_specs=(
            P("bins", "tiles", None),
            P(None, "tiles", "bins", None),
            P(None, "tiles", "bins", None),
        ),
        check_vma=False,
    )
```

profile of v0, /device:TPU:0, one launch (start us, length us, event | category | flops | bytes accessed | tf_op | source)
XLA Modules:
  0.0 418.2 jit_solution(1800999815687901730)
XLA Ops:
  8.0 7.2 %copy_multiply_fusion = f32[144,8,1440]{2,0,1:T(8,128)S(1)} fusion(f32[144,8,1440]{2,1,0:T(8,128)} %param.8, f32[8,1440]{1,0:T(8,128)S(1)} %convert_element_type.79), kind=kLoop, calls=%fused_computation.66 | loop fusion | flops 1658880 | bytes 13317120 | tf_op jit(solution)/shard_map/mul | solution.py:66
  15.2 3.0 copy-done
  25.0 12.4 %fusion.78 = (f32[144,8,1439]{2,0,1:T(8,128)}, f32[144,8,1439]{2,0,1:T(8,128)}) fusion(f32[144,8,1440]{2,0,1:T(8,128)} %copy-done), kind=kLoop, calls=%fused_computation.125 | loop fusion | bytes 26523648 | tf_op jit(solution)/shard_map/jit(_roll_static)/slice | solution.py:44
  37.5 14.0 %fusion.28 = f32[144,8,1440]{2,0,1:T(8,128)S(1)} fusion(f32[144,8,1440]{2,0,1:T(8,128)} %copy-done, f32[144,1,1440]{2,0,1:T(8,128)} %collective-permute-done.1, f32[144,1,1440]{2,0,1:T(8,128)} %collective-permute-done, f32[144,8,1439]{2,0,1:T(8,128)} %get-tuple-element.41, f32[144,8,1]{2,0,1:T(8,128)S(1)} %get-tuple-element.43, ...), kind=kLoop, calls=%fused_computation.37 | loop fusion | flops 28200960 | bytes 28257408 | tf_op jit(solution)/shard_map/mul | solution.py:49
  51.6 2.8 copy-done.1
  54.6 8.8 %collective-permute-start.2 = (f32[144,1,1440]{2,0,1:T(8,128)S(1)}, f32[144,1,1440]{2,0,1:T(8,128)}, u32[]{:S(2)}, u32[]{:S(2)}) collective-permute-start(f32[144,1,1440]{2,0,1:T(8,128)S(1)} %get-tuple-element.38), channel_id=1, source_target_pairs={{0,1},{1,2},{2,3},{3,4},{4,5},{5,6},{6,7},{7,8},{8,9},{9,10},{10,1... | collective-permute-start | bytes 2488328 | tf_op jit(solution)/shard_map/ppermute | solution.py:26
  64.9 12.5 %fusion.75 = (f32[144,8,1439]{2,0,1:T(8,128)}, f32[144,8,1439]{2,0,1:T(8,128)}) fusion(f32[144,8,1440]{2,0,1:T(8,128)} %copy-done.1), kind=kLoop, calls=%fused_computation.122 | loop fusion | bytes 26523648 | tf_op jit(solution)/shard_map/jit(_roll_static)/slice | solution.py:44
  77.4 14.0 %fusion.21 = f32[144,8,1440]{2,0,1:T(8,128)S(1)} fusion(f32[144,8,1440]{2,0,1:T(8,128)} %copy-done.1, f32[144,1,1440]{2,0,1:T(8,128)} %collective-permute-done.3, f32[144,1,1440]{2,0,1:T(8,128)} %collective-permute-done.2, f32[144,8,1439]{2,0,1:T(8,128)} %get-tuple-element.35, f32[144,8,1]{2,0,1:T(8,128)S(1)} %get-tuple-element.37, ...), kind=kLoop, calls=%fused_computation.28 | loop fusion | flops 28200960 | bytes 28257408 | tf_op jit(solution)/shard_map/mul | solution.py:49
  94.6 9.2 %collective-permute-start.4 = (f32[144,1,1440]{2,0,1:T(8,128)S(1)}, f32[144,1,1440]{2,0,1:T(8,128)}, u32[]{:S(2)}, u32[]{:S(2)}) collective-permute-start(f32[144,1,1440]{2,0,1:T(8,128)S(1)} %get-tuple-element.32), channel_id=1, source_target_pairs={{0,1},{1,2},{2,3},{3,4},{4,5},{5,6},{6,7},{7,8},{8,9},{9,10},{10,1... | collective-permute-start | bytes 2488328 | tf_op jit(solution)/shard_map/ppermute | solution.py:26
  105.0 12.5 %fusion.72 = (f32[144,8,1439]{2,0,1:T(8,128)}, f32[144,8,1439]{2,0,1:T(8,128)}) fusion(f32[144,8,1440]{2,0,1:T(8,128)} %copy-done.2), kind=kLoop, calls=%fused_computation.119 | loop fusion | bytes 26523648 | tf_op jit(solution)/shard_map/jit(_roll_static)/slice | solution.py:44
  117.5 14.0 %fusion.14 = f32[144,8,1440]{2,0,1:T(8,128)S(1)} fusion(f32[144,8,1440]{2,0,1:T(8,128)} %copy-done.2, f32[144,1,1440]{2,0,1:T(8,128)} %collective-permute-done.5, f32[144,1,1440]{2,0,1:T(8,128)} %collective-permute-done.4, f32[144,8,1439]{2,0,1:T(8,128)} %get-tuple-element.29, f32[144,8,1]{2,0,1:T(8,128)S(1)} %get-tuple-element.31, ...), kind=kLoop, calls=%fused_computation.19 | loop fusion | flops 28200960 | bytes 28257408 | tf_op jit(solution)/shard_map/mul | solution.py:49
  134.6 9.8 %collective-permute-start.6 = (f32[144,1,1440]{2,0,1:T(8,128)S(1)}, f32[144,1,1440]{2,0,1:T(8,128)}, u32[]{:S(2)}, u32[]{:S(2)}) collective-permute-start(f32[144,1,1440]{2,0,1:T(8,128)S(1)} %get-tuple-element.26), channel_id=1, source_target_pairs={{0,1},{1,2},{2,3},{3,4},{4,5},{5,6},{6,7},{7,8},{8,9},{9,10},{10,1... | collective-permute-start | bytes 2488328 | tf_op jit(solution)/shard_map/ppermute | solution.py:26
  146.2 12.5 %fusion.70 = (f32[144,8,1439]{2,0,1:T(8,128)}, f32[144,8,1439]{2,0,1:T(8,128)}) fusion(f32[144,8,1440]{2,0,1:T(8,128)} %copy-done.3), kind=kLoop, calls=%fused_computation.117 | loop fusion | bytes 26523648 | tf_op jit(solution)/shard_map/jit(_roll_static)/slice | solution.py:43
  158.7 33.0 %multiply_multiply_fusion = (f32[144,8,1440]{2,0,1:T(8,128)}, f32[144,8,1440]{2,0,1:T(8,128)S(1)}) fusion(f32[8,1440]{1,0:T(8,128)S(1)} %copy-done.4, f32[144]{0:T(256)S(1)} %get-tuple-element.51, f32[144]{0:T(256)S(1)} %get-tuple-element.50, f32[8,1440]{1,0:T(8,128)S(1)} %multiply_multiply_fusion.1, f32[8,1440]{1,0:T(8,128)S(1)} %convert_element_type.79, ...), kind=kLoop, calls=%fused_computation.68 | loop fusion | flops 36495360 | bytes 34986240 | tf_op jit(solution)/shard_map/mul | solution.py:78
  191.7 24.2 %add_multiply_fusion = f32[144,8,1440]{2,0,1:T(8,128)S(1)} fusion(f32[144,8,1440]{2,0,1:T(8,128)S(1)} %get-tuple-element.21, f32[8,1440]{1,0:T(8,128)S(1)} %multiply_subtract_fusion, f32[8,1440]{1,0:T(8,128)S(1)} %copy-done.4, f32[144]{0:T(256)S(1)} %get-tuple-element.51, f32[144]{0:T(256)S(1)} %get-tuple-element.50, f32[8,1440]{1,0:T(8,128)S(1)} %multiply_multiply_fusion.1), kind=kLoop, calls=%fused_computation.67 | loop fusion | flops 11612160 | bytes 13410432 | tf_op jit(solution)/shard_map/mul | solution.py:79
  216.0 7.1 %copy.26 = f32[144,8,1440]{2,1,0:T(8,128)} copy(f32[144,8,1440]{2,0,1:T(8,128)S(1)} %add_multiply_fusion) | data formatting | bytes 13271040
  223.0 8.7 %reshape.219 = f32[144,11520]{1,0:T(8,128)} reshape(f32[144,8,1440]{2,1,0:T(8,128)} %copy.26) | data formatting | bytes 13271040 | tf_op jit(solution)/shard_map/reshape | solution.py:84
  231.7 18.7 %dot_general.15 = f32[8,16,90,144]{2,1,0,3:T(8,128)} reshape(f32[11520,144]{0,1:T(8,128)} %bitcast.22) | data formatting | bytes 13271040 | tf_op jit(solution)/shard_map/dot_general | solution.py:82
  250.5 10.0 %copy.24 = f32[144,8,1440]{2,1,0:T(8,128)} copy(f32[144,8,1440]{2,0,1:T(8,128)} %get-tuple-element.20) | data formatting | bytes 13271040 | tf_op jit(solution)/shard_map/mul | solution.py:78
  260.5 8.7 %reshape.220 = f32[144,11520]{1,0:T(8,128)} reshape(f32[144,8,1440]{2,1,0:T(8,128)} %copy.24) | data formatting | bytes 13271040 | tf_op jit(solution)/shard_map/reshape | solution.py:90
  269.2 19.0 %dot_general.18 = f32[8,16,90,144]{2,1,0,3:T(8,128)} reshape(f32[11520,144]{0,1:T(8,128)} %bitcast.21) | data formatting | bytes 13271040 | tf_op jit(solution)/shard_map/dot_general | solution.py:88
  288.2 13.6 %fusion.2 = f32[2,8,16,90]{3,0,2,1:T(2,128)S(1)} fusion(f32[8,16,90,144]{2,1,0,3:T(8,128)} %dot_general.15, f32[1,144]{1,0:T(1,128)S(1)} %get-tuple-element.56, f32[1,144]{1,0:T(1,128)S(1)} %get-tuple-element.57), kind=kOutput, calls=%fused_computation.4 | convolution fusion | flops 39813408 | bytes 6728832 | tf_op jit(solution)/shard_map/dot_general | solution.py:82
  302.6 13.9 %fusion = f32[2,8,16,90]{3,0,2,1:T(2,128)S(1)} fusion(f32[8,16,90,144]{2,1,0,3:T(8,128)} %dot_general.18, f32[1,144]{1,0:T(1,128)S(1)} %get-tuple-element.54, f32[1,144]{1,0:T(1,128)S(1)} %get-tuple-element.55), kind=kOutput, calls=%fused_computation.2 | convolution fusion | flops 39813408 | bytes 6728832 | tf_op jit(solution)/shard_map/dot_general | solution.py:88
  318.1 90.1 %all-reduce.3.cloned.1.call-done = (f32[2,8,16,90]{3,0,1,2:T(2,128)}, f32[2,8,16,90]{3,0,1,2:T(2,128)}) async-done(((f32[2,8,16,90]{3,0,1,2:T(2,128)}, f32[2,8,16,90]{3,0,1,2:T(2,128)}), (f32[2,8,16,90]{3,0,1,2:T(2,128)}, f32[2,8,16,90]{3,0,1,2:T(2,128)})) %all-reduce.3.cloned.1.call-update) | async-done | bytes 184336 | tf_op jit(solution)/shard_map/psum | solution.py:102
  (59 shorter events, 23.9 us)
Async XLA Ops:
  7.2 401.0 %all-reduce.3.cloned.1.call-start = ((), (), s32[]{:S(2)}) async-start(), calls=%async_computation | async-start | bytes 524288 | tf_op jit(solution)/shard_map/psum | solution.py:102
  8.0 15.5 %copy-start.7 = (s32[1,16]{1,0:T(1,128)S(1)}, s32[1,16]{1,0:T(1,128)}, u32[]{:S(2)}) copy-start(s32[1,16]{1,0:T(1,128)} %param.13) | copy-start | bytes 196
  8.0 16.9 %copy-start.5 = (f32[8,1440]{1,0:T(8,128)S(1)}, f32[8,1440]{1,0:T(8,128)}, u32[]{:S(2)}) copy-start(f32[8,1440]{1,0:T(8,128)} %param.11) | copy-start | bytes 138244
  8.0 16.9 %copy-start.6 = (s32[8,1440]{1,0:T(8,128)S(1)}, s32[8,1440]{1,0:T(8,128)}, u32[]{:S(2)}) copy-start(s32[8,1440]{1,0:T(8,128)} %param.10) | copy-start | bytes 138244
  15.2 3.0 copy-start
  18.3 19.2 %collective-permute-start = (f32[144,1,1440]{2,0,1:T(8,128)S(1)}, f32[144,1,1440]{2,0,1:T(8,128)}, u32[]{:S(2)}, u32[]{:S(2)}) collective-permute-start(f32[144,1,1440]{2,0,1:T(8,128)S(1)} %get-tuple-element.44), channel_id=1, source_target_pairs={{0,1},{1,2},{2,3},{3,4},{4,5},{5,6},{6,7},{7,8},{8,9},{9,10},{10,1... | collective-permute-start | bytes 2488328 | tf_op jit(solution)/shard_map/ppermute | solution.py:26
  20.5 17.0 %collective-permute-start.1 = (f32[144,1,1440]{2,0,1:T(8,128)S(1)}, f32[144,1,1440]{2,0,1:T(8,128)}, u32[]{:S(2)}, u32[]{:S(2)}) collective-permute-start(f32[144,1,1440]{2,0,1:T(8,128)S(1)} %get-tuple-element.45), channel_id=1, source_target_pairs={{1,0},{2,1},{3,2},{4,3},{5,4},{6,5},{7,6},{8,7},{9,8},{10,9},{11,1... | collective-permute-start | bytes 2488328 | tf_op jit(solution)/shard_map/ppermute | solution.py:28
  51.4 3.0 copy-start.1
  54.6 22.8 %collective-permute-start.2 = (f32[144,1,1440]{2,0,1:T(8,128)S(1)}, f32[144,1,1440]{2,0,1:T(8,128)}, u32[]{:S(2)}, u32[]{:S(2)}) collective-permute-start(f32[144,1,1440]{2,0,1:T(8,128)S(1)} %get-tuple-element.38), channel_id=1, source_target_pairs={{0,1},{1,2},{2,3},{3,4},{4,5},{5,6},{6,7},{7,8},{8,9},{9,10},{10,1... | collective-permute-start | bytes 2488328 | tf_op jit(solution)/shard_map/ppermute | solution.py:26
  63.4 14.0 %collective-permute-start.3 = (f32[144,1,1440]{2,0,1:T(8,128)S(1)}, f32[144,1,1440]{2,0,1:T(8,128)}, u32[]{:S(2)}, u32[]{:S(2)}) collective-permute-start(f32[144,1,1440]{2,0,1:T(8,128)S(1)} %get-tuple-element.39), channel_id=1, source_target_pairs={{1,0},{2,1},{3,2},{4,3},{5,4},{6,5},{7,6},{8,7},{9,8},{10,9},{11,1... | collective-permute-start | bytes 2488328 | tf_op jit(solution)/shard_map/ppermute | solution.py:28
  91.4 3.0 copy-start.2
  94.6 22.9 %collective-permute-start.4 = (f32[144,1,1440]{2,0,1:T(8,128)S(1)}, f32[144,1,1440]{2,0,1:T(8,128)}, u32[]{:S(2)}, u32[]{:S(2)}) collective-permute-start(f32[144,1,1440]{2,0,1:T(8,128)S(1)} %get-tuple-element.32), channel_id=1, source_target_pairs={{0,1},{1,2},{2,3},{3,4},{4,5},{5,6},{6,7},{7,8},{8,9},{9,10},{10,1... | collective-permute-start | bytes 2488328 | tf_op jit(solution)/shard_map/ppermute | solution.py:26
  103.7 13.7 %collective-permute-start.5 = (f32[144,1,1440]{2,0,1:T(8,128)S(1)}, f32[144,1,1440]{2,0,1:T(8,128)}, u32[]{:S(2)}, u32[]{:S(2)}) collective-permute-start(f32[144,1,1440]{2,0,1:T(8,128)S(1)} %get-tuple-element.33), channel_id=1, source_target_pairs={{1,0},{2,1},{3,2},{4,3},{5,4},{6,5},{7,6},{8,7},{9,8},{10,9},{11,1... | collective-permute-start | bytes 2488328 | tf_op jit(solution)/shard_map/ppermute | solution.py:28
  131.4 3.0 copy-start.3
  134.6 24.1 %collective-permute-start.6 = (f32[144,1,1440]{2,0,1:T(8,128)S(1)}, f32[144,1,1440]{2,0,1:T(8,128)}, u32[]{:S(2)}, u32[]{:S(2)}) collective-permute-start(f32[144,1,1440]{2,0,1:T(8,128)S(1)} %get-tuple-element.26), channel_id=1, source_target_pairs={{0,1},{1,2},{2,3},{3,4},{4,5},{5,6},{6,7},{7,8},{8,9},{9,10},{10,1... | collective-permute-start | bytes 2488328 | tf_op jit(solution)/shard_map/ppermute | solution.py:26
  144.4 14.3 %copy-start.4 = (f32[8,1440]{1,0:T(8,128)S(1)}, f32[8,1440]{1,0:T(8,128)}, u32[]{:S(2)}) copy-start(f32[8,1440]{1,0:T(8,128)} %param.12) | copy-start | bytes 138244
  144.4 14.3 %collective-permute-start.7 = (f32[144,1,1440]{2,0,1:T(8,128)S(1)}, f32[144,1,1440]{2,0,1:T(8,128)}, u32[]{:S(2)}, u32[]{:S(2)}) collective-permute-start(f32[144,1,1440]{2,0,1:T(8,128)S(1)} %get-tuple-element.27), channel_id=1, source_target_pairs={{1,0},{2,1},{3,2},{4,3},{5,4},{6,5},{7,6},{8,7},{9,8},{10,9},{11,1... | collective-permute-start | bytes 2488328 | tf_op jit(solution)/shard_map/ppermute | solution.py:28
Sparse Core Ops, SparseCore 0:
  318.3 89.8 all-reduce.2
where the time goes:
time: 426 us; the launch traced here: 418 us
  local copies, waits for them, and re-layouts  140 us (33%)
  other arithmetic  110 us (26%)
  waiting for transfers between devices  90.1 us (21%)
  starting transfers between devices  35.9 us (8%)
  matrix products  27.5 us (6%)
  between operations  14.7 us (3%)
    psum x1, waiting for transfers between devices, shards(): drift_total, stress_total = lax.psum((drift_terms, stress_terms), 'bins')  90.1 us
    mul x3, other arithmetic, advance(): return result * sea_open  41.9 us
    slice x6, local copies, waits for them, and re-layouts, advance(): east_cell = jnp.roll(center, -1, axis=2)  39.3 us
    mul x1, other arithmetic, shards(): source = growth * spectral  33 us
    ppermute x4, starting transfers between devices, extended(): lax.ppermute(tail, axis, [(i, (i + 1) % count) for i in range(ends)])  30 us
    mul x1, other arithmetic, shards(): updated = (spectral + source) * (1.0 - 0.5 * ice_mask.astype(jnp.float32))  24.2 us
    unnamed x19, local copies, waits for them, and re-layouts  19.8 us
    dot_general x1, local copies, waits for them, and re-layouts, shards(): jnp.dot(stress_weights, source.reshape(local_bins, -1), precision=lax.Pre...  19 us
  transfers between devices with their start and end apart: 9, of which 1 were waited for; matrix products, arithmetic and copies ran while one was open for 13% of the time, Pallas kernels for 0%

commit v1 on v0

v1 whole, which is shorter than its diff:
```python
import math

import jax
import jax.numpy as jnp
from jax import lax
from jax.experimental import pallas as pl
from jax.experimental.pallas import tpu as pltpu
from jax.sharding import PartitionSpec as P

NDIR = 36
NFREQ = 32
LON_BLOCKS = 16
STEPS = 4
COURANT_MAX = 0.6
GRID_STEP = 0.25 * math.pi / 180.0

ROWS = 8
NLON = 1440
BLK = 90
LANES = 128
TILES = 12
TAIL = NLON - (TILES - 1) * LANES
NF = 4
GROUPS = 9
G1 = 7
G2 = GROUPS - G1
TPG = NF * (TILES - 1) + 1

F32 = jnp.float32
OFF_BX = 0
OFF_BY = NF * NDIR
OFF_COS = 2 * NF * NDIR
OFF_SIN = OFF_COS + NDIR
OFF_P = OFF_SIN + NDIR


def lane_iota():
    return lax.broadcasted_iota(jnp.int32, (ROWS, LANES), 1)


def sub_iota():
    return lax.broadcasted_iota(jnp.int32, (ROWS, LANES), 0)


def pack_group(src_ref, mask_ref, out_ref, upward, lane, low):
    def pair(j, i):
        cols = pl.ds(i * LANES, LANES)
        first = src_ref[j, 0, :, cols]
        second = src_ref[j, 1, :, cols]
        mask = mask_ref[:, cols].astype(F32)
        first = first * mask
        second = second * mask
        if upward:
            return jnp.where(low, pltpu.roll(first, 4, 0), second)
        return jnp.where(low, first, pltpu.roll(second, 4, 0))

    for i in range(TILES - 1):
        for j in range(NF):
            out_ref[0, j * (TILES - 1) + i] = pair(j, i)
    tail = pair(0, TILES - 1)
    for j in range(1, NF):
        moved = pltpu.roll(pair(j, TILES - 1), TAIL * j, 1)
        tail = jnp.where(lane >= TAIL * j, moved, tail)
    out_ref[0, TPG - 1] = tail


def pack_kernel(with_mask, south_ref, north_ref, mask_ref, up_ref, dn_ref):
    lane = lane_iota()
    low = sub_iota() < 4
    pack_group(south_ref, mask_ref, up_ref, True, lane, low)
    pack_group(north_ref, mask_ref, dn_ref, False, lane, low)
    if with_mask:
        start = jnp.minimum(pl.program_id(0), TILES // 2 - 1) * (2 * LANES)
        start = pl.multiple_of(start, 2 * LANES)
        first = mask_ref[:, pl.ds(start, LANES)].astype(F32)
        second = mask_ref[:, pl.ds(start + LANES, LANES)].astype(F32)
        up_ref[0, TPG] = jnp.where(low, pltpu.roll(first, 4, 0), second)
        dn_ref[0, TPG] = jnp.where(low, first, pltpu.roll(second, 4, 0))


def pack(spectral, sea_mask, base, groups, with_mask):
    tiles = TPG + 1 if with_mask else TPG
    block = (NF, 2, ROWS, TILES * LANES)
    out = jax.ShapeDtypeStruct((groups, tiles, ROWS, LANES), F32)
    out_spec = pl.BlockSpec((1, tiles, ROWS, LANES), lambda g: (g, 0, 0, 0))
    return pl.pallas_call(
        lambda *refs: pack_kernel(with_mask, *refs),
        grid=(groups,),
        in_specs=[
            pl.BlockSpec(block, lambda g: (0, base + g, 0, 0)),
            pl.BlockSpec(block, lambda g: (0, 2 * GROUPS - 1 - base - g, 0, 0)),
            pl.BlockSpec((ROWS, TILES * LANES), lambda g: (0, 0)),
        ],
        out_specs=[out_spec, out_spec],
        out_shape=[out, out],
        name="pack%d" % base,
    )(spectral, spectral, sea_mask)


def fill_wrap(tiles, west, lane):
    last = tiles[-1]
    if west:
        moved = pltpu.roll(last, LANES - TAIL, 1)
    else:
        moved = pltpu.roll(tiles[0], TAIL, 1)
    return tiles[:-1] + [jnp.where(lane < TAIL, last, moved)]


def advance(tiles, mask_at, alpha, cx, cy, west, south, lane):
    shift = 1 if west else LANES - 1
    edge = (lane == 0) if west else (lane == LANES - 1)
    for step in range(STEPS):
        moved = [pltpu.roll(t, shift, 1) for t in tiles]
        new = []
        for i in range(TILES):
            near = moved[i - 1] if west else moved[(i + 1) % TILES]
            x = jnp.where(edge, near, moved[i])
            y = pltpu.roll(tiles[i], 1 if south else ROWS - 1, 0)
            new.append((alpha * tiles[i] + cx * x + cy * y) * mask_at(i))
        tiles = new
    return tiles


def variants(dp, dd, body):
    direction = 2 * dp + dd
    is_south = dp < GROUPS
    is_west = jnp.logical_or(direction < NDIR // 4, direction >= NDIR - NDIR // 4)
    for south in (True, False):
        for west in (True, False):
            cond = jnp.logical_and(is_south == south, is_west == west)
            pl.when(cond)(lambda west=west, south=south: body(west, south))


def own_kernel(tab_ref, met_ref, mask_ref, src_ref, out_ref):
    dp = pl.program_id(0)
    lane = lane_iota()
    low = sub_iota() < 4
    for dd in range(2):

        def body(west, south, dd=dd):
            def one(j, carry):
                index = j * NDIR + 2 * dp + dd
                cy = tab_ref[OFF_BY + index]
                cx = tab_ref[OFF_BX + index] * met_ref[0]
                alpha = 1.0 - cx - cy
                start = [
                    src_ref[j, dd, :, pl.ds(i * LANES, LANES)] for i in range(TILES)
                ]
                start = fill_wrap(start, west, lane)
                start = [t * mask_ref[i] for i, t in enumerate(start)]
                done = advance(
                    start, lambda i: mask_ref[i], alpha, cx, cy, west, south, lane
                )
                for i in range(TILES):
                    if south:
                        kept = jnp.where(low, start[i], done[i])
                    else:
                        kept = jnp.where(low, done[i], start[i])
                    out_ref[0, dd, j, i] = kept
                return carry

            lax.fori_loop(0, NF, one, 0)

        variants(dp, dd, body)


def own_rows(spectral, table, metric, mask):
    whole = pl.BlockSpec(memory_space=pltpu.VMEM)
    return pl.pallas_call(
        own_kernel,
        grid=(2 * GROUPS,),
        in_specs=[
            pl.BlockSpec(memory_space=pltpu.SMEM),
            whole,
            whole,
            pl.BlockSpec((NF, 2, ROWS, TILES * LANES), lambda d: (0, d, 0, 0)),
        ],
        out_specs=pl.BlockSpec(
            (1, 2, NF, TILES, ROWS, LANES), lambda d: (d, 0, 0, 0, 0, 0)
        ),
        out_shape=jax.ShapeDtypeStruct((2 * GROUPS, 2, NF, TILES, ROWS, LANES), F32),
        name="own",
    )(table, metric, mask, spectral)


def finish_kernel(
    dp_of,
    first,
    tab_ref,
    met_ref,
    mask_ref,
    wind_ref,
    own_ref,
    up_ref,
    dn_ref,
    prev_ref,
    old_ref,
    out_ref,
    acc_ref,
    e_ref,
):
    step = pl.program_id(0)
    dp = dp_of(step)
    lane = lane_iota()
    low = sub_iota() < 4

    @pl.when(step == 0)
    def _():
        if first:
            acc_ref[...] = jnp.zeros_like(acc_ref)
        else:
            acc_ref[...] = prev_ref[...]

    for dd in range(2):

        def body(west, south, dd=dd):
            halo_ref = up_ref if south else dn_ref
            side = 0 if south else 1
            swap = (dd == 0) if south else (dd == 1)

            def one(j, carry):
                index = j * NDIR + 2 * dp + dd
                cy = tab_ref[OFF_BY + index]
                cx = tab_ref[OFF_BX + index] * met_ref[1 + side]
                alpha = 1.0 - cx - cy
                start = []
                own = []
                for i in range(TILES):
                    if i < TILES - 1:
                        halo = halo_ref[0, j * (TILES - 1) + i]
                    else:
                        halo = pltpu.roll(
                            halo_ref[0, TPG - 1], (LANES - TAIL * j) % LANES, 1
                        )
                    if swap:
                        halo = pltpu.roll(halo, 4, 0)
                    mine = own_ref[0, dd, j, i]
                    own.append(mine)
                    if south:
                        start.append(jnp.where(low, mine, halo))
                    else:
                        start.append(jnp.where(low, halo, mine))
                start = fill_wrap(start, west, lane)
                done = advance(
                    start,
                    lambda i: mask_ref[side, i],
                    alpha,
                    cx,
                    cy,
                    west,
                    south,
                    lane,
                )
                for i in range(TILES):
                    if south:
                        e_ref[j, i] = jnp.where(low, done[i], own_ref[0, dd, j, i])
                    else:
                        e_ref[j, i] = jnp.where(low, own_ref[0, dd, j, i], done[i])
                return carry

            lax.fori_loop(0, NF, one, 0)

        variants(dp, dd, body)
        cos_d = tab_ref[OFF_COS + 2 * dp + dd]
        sin_d = tab_ref[OFF_SIN + 2 * dp + dd]
        weight = [tab_ref[OFF_P + j] for j in range(NF)]
        for i in range(TILES):
            h = jnp.maximum(cos_d * wind_ref[0, i] + sin_d * wind_ref[1, i], 0.0)
            ice = wind_ref[2, i]
            for j in range(NF):
                e = e_ref[j, i]
                x = weight[j] * e
                out_ref[j, dd, :, pl.ds(i * LANES, LANES)] = (e + h * x) * ice
                y = weight[j] * x
                sum_x = x if j == 0 else sum_x + x
                sum_y = y if j == 0 else sum_y + y
            source = h * sum_x
            drift = ice * (sum_x + h * sum_y)
            acc_ref[0, i] += cos_d * drift
            acc_ref[1, i] += sin_d * drift
            acc_ref[2, i] += cos_d * source
            acc_ref[3, i] += sin_d * source


def finish(table, metric, masks, wind, own, up, dn, prev, old, base):
    first = prev is None
    groups = up.shape[0]
    if first:
        dp_of = lambda i: jnp.where(i < groups, i, i + 2 * (GROUPS - groups))
    else:
        dp_of = lambda i: i + base
    tiles = up.shape[1]
    whole = pl.BlockSpec(memory_space=pltpu.VMEM)
    anywhere = pl.BlockSpec(memory_space=pl.ANY)
    acc = jax.ShapeDtypeStruct((4, TILES, ROWS, LANES), F32)
    out = jax.ShapeDtypeStruct((NF, NDIR, ROWS, NLON), F32)
    in_specs = [
        pl.BlockSpec(memory_space=pltpu.SMEM),
        whole,
        whole,
        whole,
        pl.BlockSpec(
            (1, 2, NF, TILES, ROWS, LANES), lambda i: (dp_of(i), 0, 0, 0, 0, 0)
        ),
        pl.BlockSpec(
            (1, tiles, ROWS, LANES), lambda i: (jnp.minimum(i, groups - 1), 0, 0, 0)
        ),
        pl.BlockSpec(
            (1, tiles, ROWS, LANES),
            lambda i: (jnp.minimum(2 * groups - 1 - i, groups - 1), 0, 0, 0),
        ),
    ]
    args = [table, metric, masks, wind, own, up, dn]
    aliases = {}
    if first:
        kernel = lambda *r: finish_kernel(dp_of, True, *r[:7], None, None, *r[7:])
    else:
        kernel = lambda *r: finish_kernel(dp_of, False, *r)
        in_specs += [whole, anywhere]
        args += [prev, old]
        aliases = {8: 0}
    return pl.pallas_call(
        kernel,
        grid=(2 * groups,),
        in_specs=in_specs,
        out_specs=[
            pl.BlockSpec(
                (NF, 2, ROWS, TILES * LANES), lambda i: (0, dp_of(i), 0, 0)
            ),
            pl.BlockSpec((4, TILES, ROWS, LANES), lambda i: (0, 0, 0, 0)),
        ],
        out_shape=[out, acc],
        scratch_shapes=[pltpu.VMEM((NF, TILES, ROWS, LANES), F32)],
        input_output_aliases=aliases,
        name="finish%d" % base,
    )(*args)


def slots_kernel(order_ref, acc_ref, out_ref):
    lane = lane_iota()

    def owner(k, carry):
        rests = []
        for c in range(4):
            parts = []
            for s in range(2):
                column = order_ref[2 * k + s] * BLK
                tile = column // LANES
                shift = column % LANES
                back = (LANES - shift) % LANES
                here = pltpu.roll(acc_ref[c, tile], back, 1)
                after = pltpu.roll(acc_ref[c, jnp.minimum(tile + 1, TILES - 1)], back, 1)
                parts.append(jnp.where(lane < LANES - shift, here, after))
            moved = pltpu.roll(parts[1], BLK, 1)
            out_ref[k, c] = jnp.where(lane < BLK, parts[0], moved)
            rests.append(moved)
        for c in range(2):
            other = pltpu.roll(rests[2 * c + 1], LANES // 2, 1)
            both = jnp.where(lane < LANES // 2, rests[2 * c], other)
            used = lane % (LANES // 2) < 2 * BLK - LANES
            out_ref[k, 4 + c] = jnp.where(used, both, 0.0)
        return carry

    lax.fori_loop(0, LON_BLOCKS // 2, owner, 0)


def pick_slots(order, acc):
    return pl.pallas_call(
        slots_kernel,
        in_specs=[
            pl.BlockSpec(memory_space=pltpu.SMEM),
            pl.BlockSpec(memory_space=pltpu.VMEM),
        ],
        out_specs=pl.BlockSpec(memory_space=pltpu.VMEM),
        out_shape=jax.ShapeDtypeStruct((LON_BLOCKS // 2, 6, ROWS, LANES), F32),
        name="slots",
    )(order, acc)


def as_tiles(field):
    return field.reshape(ROWS, TILES, LANES).transpose(1, 0, 2)


def with_wrap(field):
    side = (TILES * LANES - NLON) // 2
    return jnp.concatenate([field, field[:, :side], field[:, NLON - side :]], axis=1)


def edge_mask(received):
    tiles = received[: TILES // 2, TPG].reshape(TILES, 4, LANES)
    return tiles.transpose(1, 0, 2).reshape(4, TILES * LANES)[:, :NLON]


def row_metric(row_pos, lat_total):
    latitude = (row_pos.astype(F32) - lat_total / 2 + 0.5) * GRID_STEP
    edge_lat = (lat_total / 2 - 0.5) * GRID_STEP
    return jnp.cos(jnp.asarray(edge_lat, F32)) / jnp.cos(latitude)


def shards(spectrum, sea_mask, ice_mask, friction, wind_dir, ocean_owner):
    count = lax.axis_size("tiles")
    first_row = lax.axis_index("tiles") * ROWS
    up_pairs = [(i, i + 1) for i in range(count - 1)]
    dn_pairs = [(i + 1, i) for i in range(count - 1)]
    spectral = spectrum.reshape(NF, NDIR, ROWS, NLON)

    up1, dn1 = pack(spectral, sea_mask, 0, G1, True)
    up1 = lax.ppermute(up1, "tiles", up_pairs)
    dn1 = lax.ppermute(dn1, "tiles", dn_pairs)
    up2, dn2 = pack(spectral, sea_mask, G1, G2, False)
    up2 = lax.ppermute(up2, "tiles", up_pairs)
    dn2 = lax.ppermute(dn2, "tiles", dn_pairs)

    freq_pos = (lax.axis_index("bins") * NF + jnp.arange(NF)).astype(F32)
    speed_ratio = jnp.power(1.1, -freq_pos)
    freq_weight = jnp.power(1.03, freq_pos - (NFREQ - 1))
    angles = (jnp.arange(NDIR).astype(F32) + 0.5) * (2.0 * math.pi / NDIR)
    cos_dir = jnp.cos(angles)
    sin_dir = jnp.sin(angles)
    courant = (COURANT_MAX * speed_ratio)[:, None]
    table = jnp.concatenate(
        [
            (courant * jnp.abs(cos_dir)).reshape(-1),
            (courant * jnp.abs(sin_dir)).reshape(-1),
            cos_dir,
            sin_dir,
            freq_weight,
        ]
    )
    sub = jnp.arange(ROWS)
    rows = jnp.stack(
        [sub, jnp.where(sub < 4, sub, sub - ROWS), jnp.where(sub < 4, sub + ROWS, sub)]
    )
    metric = row_metric(first_row + rows, ROWS * count)
    metric = jnp.broadcast_to(metric[:, :, None], (3, ROWS, LANES))

    sea = sea_mask.astype(F32)
    mask = as_tiles(with_wrap(sea))
    strength = 0.5 * friction**2
    wind = jnp.stack(
        [
            strength * jnp.cos(wind_dir),
            strength * jnp.sin(wind_dir),
            1.0 - 0.5 * ice_mask.astype(F32),
        ]
    )
    wind = jnp.pad(wind, ((0, 0), (0, 0), (0, TILES * LANES - NLON)))
    wind = wind.reshape(3, ROWS, TILES, LANES).transpose(0, 2, 1, 3)
    order = jnp.argsort(ocean_owner[0], stable=True).astype(jnp.int32)

    own = own_rows(spectral, table, metric, mask)

    south = jnp.concatenate([sea[:4], edge_mask(up1)], axis=0)
    north = jnp.concatenate([edge_mask(dn1), sea[4:]], axis=0)
    masks = jnp.stack([as_tiles(with_wrap(south)), as_tiles(with_wrap(north))])

    out, acc = finish(table, metric, masks, wind, own, up1, dn1, None, None, 0)
    out, acc = finish(table, metric, masks, wind, own, up2, dn2, acc, out, G1)

    sent = pick_slots(order, acc)
    got = lax.all_to_all(sent, "bins", 0, 0, tiled=True)
    total = got.sum(0)
    rest = total[4:].reshape(2, ROWS, 2, LANES // 2).transpose(0, 2, 1, 3)
    rest = rest.reshape(4, ROWS, LANES // 2)[:, :, : 2 * BLK - LANES]
    fields = jnp.concatenate([total[:4], rest], axis=2).reshape(4, ROWS, 2, BLK)
    return out.reshape(spectrum.shape), fields[:2], fields[2:]


def solution(mesh):
    field = P("tiles", None)
    blocks = P(None, "tiles", "bins", None)
    whole = P("bins", "tiles", None)
    return jax.shard_map(
        shards,
        mesh=mesh,
        in_specs=(whole, field, field, field, field, field),
        out_specs=(whole, blocks, blocks),
        check_vma=False,
    )
```

time: 426 us -> 173 us (0.41)
  the two profiles are of different devices: /device:TPU:0 before, /device:TPU:32 now
where the time goes in v1:
time: 173 us; the launch traced here: 172 us
  Pallas kernels  134 us (77%)
  blocking collectives  15.4 us (9%)
  starting transfers between devices  13 us (8%)
  local copies, waits for them, and re-layouts  5.01 us (3%)
  other arithmetic  4.31 us (2%)
    pallas_call x2, Pallas kernels, finish(): pl.pallas_call(kernel, grid=(2 * groups,), in_specs=in_specs, out_specs=[...  66.8 us
    pallas_call x1, Pallas kernels, own_rows(): pl.pallas_call(own_kernel, grid=(2 * GROUPS,), in_specs=[pl.BlockSpec(mem...  55.2 us
    all_to_all x1, blocking collectives, shards(): got = lax.all_to_all(sent, 'bins', 0, 0, tiled=True)  15.4 us
    pallas_call x2, Pallas kernels, pack(): pl.pallas_call(lambda *refs: pack_kernel(with_mask, *refs), grid=(groups,...  8.52 us
    ppermute x1, starting transfers between devices, shards(): dn1 = lax.ppermute(dn1, 'tiles', dn_pairs)  4.67 us
    ppermute x1, starting transfers between devices, shards(): dn2 = lax.ppermute(dn2, 'tiles', dn_pairs)  4.54 us
  transfers between devices with their start and end apart: 4, of which 0 were waited for; matrix products, arithmetic and copies ran while one was open for 4% of the time, Pallas kernels for 63%

profile of v1, /device:TPU:32, one launch (start us, length us, event | category | flops | bytes accessed | tf_op | source)
XLA Modules:
  0.0 172.4 jit_solution(1928106544972582300)
XLA Ops:
  0.6 6.3 %pack0.1 = (f32[7,46,8,128]{3,2,1,0:T(8,128)}, f32[7,46,8,128]{3,2,1,0:T(8,128)}) custom-call(f32[4,36,8,1440]{3,2,1,0:T(8,128)} %bitcast.40, f32[4,36,8,1440]{3,2,1,0:T(8,128)} %bitcast.41, s32[8,1440]{1,0:T(8,128)} %refs_2_.3), custom_call_target="tpu_custom_call" | custom-call | tf_op jit(solution)/shard_map/pack0/pallas_call | solution.py:86
  6.9 1.9 %collective-permute-start = (f32[7,46,8,128]{3,2,1,0:T(8,128)}, f32[7,46,8,128]{3,2,1,0:T(8,128)S(1)}, u32[]{:S(2)}, u32[]{:S(2)}) collective-permute-start(f32[7,46,8,128]{3,2,1,0:T(8,128)} %get-tuple-element.12), channel_id=1, source_target_pairs={{0,1},{1,2},{2,3},{3,4},{4,5},{5,6},{6,7},{7,8},{8,9},{9,10},{10,1... | collective-permute-start | bytes 3956744 | tf_op jit(solution)/shard_map/ppermute | solution.py:408
  8.9 4.7 %collective-permute-start.1 = (f32[7,46,8,128]{3,2,1,0:T(8,128)}, f32[7,46,8,128]{3,2,1,0:T(8,128)S(1)}, u32[]{:S(2)}, u32[]{:S(2)}) collective-permute-start(f32[7,46,8,128]{3,2,1,0:T(8,128)} %get-tuple-element.13), channel_id=1, source_target_pairs={{1,0},{2,1},{3,2},{4,3},{5,4},{6,5},{7,6},{8,7},{9,8},{10,9},{11,1... | collective-permute-start | bytes 3956744 | tf_op jit(solution)/shard_map/ppermute | solution.py:409
  13.5 2.2 %pack7.1 = (f32[2,45,8,128]{3,2,1,0:T(8,128)}, f32[2,45,8,128]{3,2,1,0:T(8,128)}) custom-call(f32[4,36,8,1440]{3,2,1,0:T(8,128)} %bitcast.42, f32[4,36,8,1440]{3,2,1,0:T(8,128)} %bitcast.43, s32[8,1440]{1,0:T(8,128)} %refs_2_.3), custom_call_target="tpu_custom_call" | custom-call | tf_op jit(solution)/shard_map/pack7/pallas_call | solution.py:86
  15.8 1.9 %collective-permute-start.2 = (f32[2,45,8,128]{3,2,1,0:T(8,128)}, f32[2,45,8,128]{3,2,1,0:T(8,128)S(1)}, u32[]{:S(2)}, u32[]{:S(2)}) collective-permute-start(f32[2,45,8,128]{3,2,1,0:T(8,128)} %get-tuple-element.14), channel_id=1, source_target_pairs={{0,1},{1,2},{2,3},{3,4},{4,5},{5,6},{6,7},{7,8},{8,9},{9,10},{10,1... | collective-permute-start | bytes 1105928 | tf_op jit(solution)/shard_map/ppermute | solution.py:411
  17.7 4.5 %collective-permute-start.3 = (f32[2,45,8,128]{3,2,1,0:T(8,128)}, f32[2,45,8,128]{3,2,1,0:T(8,128)S(1)}, u32[]{:S(2)}, u32[]{:S(2)}) collective-permute-start(f32[2,45,8,128]{3,2,1,0:T(8,128)} %get-tuple-element.15), channel_id=1, source_target_pairs={{1,0},{2,1},{3,2},{4,3},{5,4},{6,5},{7,6},{8,7},{9,8},{10,9},{11,1... | collective-permute-start | bytes 1105928 | tf_op jit(solution)/shard_map/ppermute | solution.py:412
  22.5 0.1 mul.90
  22.7 0.7 concatenate.33
  23.4 1.2 sort.17
  24.7 0.7 concatenate.28.tab_ref.r_0_
  25.4 0.7 broadcast_in_dim.2.met_ref.r_1_
  26.1 55.2 %own.1.r_4_ = f32[18,2,4,12,8,128]{5,4,3,2,1,0:T(8,128)} custom-call(f32[364]{0:T(512)} %concatenate.28.tab_ref.r_0_, f32[3,8,128]{2,1,0:T(8,128)} %broadcast_in_dim.2.met_ref.r_1_, f32[12,8,128]{2,1,0:T(8,128)} %bitcast.50, f32[4,36,8,1440]{3,2,1,0:T(8,128)} %bitcast.44), custom_call_target="tpu_custom_call" | custom-call | tf_op jit(solution)/shard_map/own/pallas_call | solution.py:169
  81.3 1.0 multiply_bitcast_fusion.1
  82.3 0.7 fusion.r_3_
  83.3 1.0 pad_maximum_fusion.r_2_
  84.3 0.2 copy-done.1
  84.5 51.9 %finish0.1 = (f32[4,36,8,1440]{3,2,1,0:T(8,128)}, f32[4,12,8,128]{3,2,1,0:T(8,128)}) custom-call(f32[364]{0:T(512)} %concatenate.28.tab_ref.r_0_, f32[3,8,128]{2,1,0:T(8,128)} %broadcast_in_dim.2.met_ref.r_1_, f32[2,12,8,128]{3,2,1,0:T(8,128)} %pad_maximum_fusion.r_2_, f32[3,12,8,128]{3,2,1,0:T(8,128)} %fusion.r_3_, f32[18,2,4,12,8,128]{5,4,3,2,1,0:T(8,128)} %own.1.r_4_, ...), custom_call_target="tpu_custom_call" | custom-call | tf_op jit(solution)/shard_map/finish0/pallas_call | solution.py:322
  136.4 0.7 copy-done.3
  137.1 0.1 copy-done.4
  137.3 14.9 %finish7.1 = (f32[4,36,8,1440]{3,2,1,0:T(8,128)}, f32[4,12,8,128]{3,2,1,0:T(8,128)}) custom-call(f32[364]{0:T(512)} %concatenate.28.tab_ref.r_0_, f32[3,8,128]{2,1,0:T(8,128)} %broadcast_in_dim.2.met_ref.r_1_, f32[2,12,8,128]{3,2,1,0:T(8,128)} %pad_maximum_fusion.r_2_, f32[3,12,8,128]{3,2,1,0:T(8,128)} %fusion.r_3_, ...), custom_call_target="tpu_custom_call", output_to_operand_aliasing={{0}: (8, {})} | custom-call | tf_op jit(solution)/shard_map/finish7/pallas_call | solution.py:322
  152.2 3.3 %slots.1 = f32[8,6,8,128]{3,2,1,0:T(8,128)} custom-call(s32[16]{0:T(128)} %get-tuple-element.19.order_ref, f32[4,12,8,128]{3,2,1,0:T(8,128)} %get-tuple-element.20.acc_ref), custom_call_target="tpu_custom_call" | custom-call | tf_op jit(solution)/shard_map/slots/pallas_call | solution.py:368
  155.5 15.4 %all_to_all.5 = f32[8,6,8,128]{3,2,1,0:T(8,128)S(1)} all-to-all(f32[8,6,8,128]{3,2,1,0:T(8,128)} %slots.1), channel_id=1, replica_groups=mesh['bins'=8,'tiles'=16] {'bins'}, dimensions={0} | all-to-all | bytes 393216 | tf_op jit(solution)/shard_map/all_to_all | solution.py:461
  171.0 0.7 slice.80
  171.7 0.7 slice.82
  (42 shorter events, 0.8 us)
Async XLA Ops:
  6.9 76.0 %collective-permute-start = (f32[7,46,8,128]{3,2,1,0:T(8,128)}, f32[7,46,8,128]{3,2,1,0:T(8,128)S(1)}, u32[]{:S(2)}, u32[]{:S(2)}) collective-permute-start(f32[7,46,8,128]{3,2,1,0:T(8,128)} %get-tuple-element.12), channel_id=1, source_target_pairs={{0,1},{1,2},{2,3},{3,4},{4,5},{5,6},{6,7},{7,8},{8,9},{9,10},{10,1... | collective-permute-start | bytes 3956744 | tf_op jit(solution)/shard_map/ppermute | solution.py:408
  8.8 13.4 %copy-start.2 = (s32[8,1440]{1,0:T(8,128)S(1)}, s32[8,1440]{1,0:T(8,128)}, u32[]{:S(2)}) copy-start(s32[8,1440]{1,0:T(8,128)} %refs_2_.3) | copy-start | bytes 138244
  8.9 14.6 %copy-start.7 = (s32[1,16]{1,0:T(1,128)S(1)}, s32[1,16]{1,0:T(1,128)}, u32[]{:S(2)}) copy-start(s32[1,16]{1,0:T(1,128)} %param.11) | copy-start | bytes 196
  8.9 74.1 %collective-permute-start.1 = (f32[7,46,8,128]{3,2,1,0:T(8,128)}, f32[7,46,8,128]{3,2,1,0:T(8,128)S(1)}, u32[]{:S(2)}, u32[]{:S(2)}) collective-permute-start(f32[7,46,8,128]{3,2,1,0:T(8,128)} %get-tuple-element.13), channel_id=1, source_target_pairs={{1,0},{2,1},{3,2},{4,3},{5,4},{6,5},{7,6},{8,7},{9,8},{10,9},{11,1... | collective-permute-start | bytes 3956744 | tf_op jit(solution)/shard_map/ppermute | solution.py:409
  15.8 120.6 %collective-permute-start.2 = (f32[2,45,8,128]{3,2,1,0:T(8,128)}, f32[2,45,8,128]{3,2,1,0:T(8,128)S(1)}, u32[]{:S(2)}, u32[]{:S(2)}) collective-permute-start(f32[2,45,8,128]{3,2,1,0:T(8,128)} %get-tuple-element.14), channel_id=1, source_target_pairs={{0,1},{1,2},{2,3},{3,4},{4,5},{5,6},{6,7},{7,8},{8,9},{9,10},{10,1... | collective-permute-start | bytes 1105928 | tf_op jit(solution)/shard_map/ppermute | solution.py:411
  17.7 118.7 %collective-permute-start.3 = (f32[2,45,8,128]{3,2,1,0:T(8,128)}, f32[2,45,8,128]{3,2,1,0:T(8,128)S(1)}, u32[]{:S(2)}, u32[]{:S(2)}) collective-permute-start(f32[2,45,8,128]{3,2,1,0:T(8,128)} %get-tuple-element.15), channel_id=1, source_target_pairs={{1,0},{2,1},{3,2},{4,3},{5,4},{6,5},{7,6},{8,7},{9,8},{10,9},{11,1... | collective-permute-start | bytes 1105928 | tf_op jit(solution)/shard_map/ppermute | solution.py:412
  26.1 55.2 %copy-start.5 = (s32[8,1440]{1,0:T(8,128)S(1)}, s32[8,1440]{1,0:T(8,128)}, u32[]{:S(2)}) copy-start(s32[8,1440]{1,0:T(8,128)} %param.8) | copy-start | bytes 138244
  26.1 55.2 %copy-start.6 = (f32[8,1440]{1,0:T(8,128)S(1)}, f32[8,1440]{1,0:T(8,128)}, u32[]{:S(2)}) copy-start(f32[8,1440]{1,0:T(8,128)} %param.10) | copy-start | bytes 138244
  83.0 1.3 copy-start
  83.0 1.5 copy-start.1
  136.4 0.7 copy-start.3
  136.4 0.8 copy-start.4

commit v2 on v1

--- a/solution.py
+++ b/solution.py
@@ -27,6 +27,7 @@
 TPG = NF * (TILES - 1) + 1
 
 F32 = jnp.float32
+LIMIT = 12 << 20
 OFF_BX = 0
 OFF_BY = NF * NDIR
 OFF_COS = 2 * NF * NDIR
@@ -42,7 +43,7 @@
     return lax.broadcasted_iota(jnp.int32, (ROWS, LANES), 0)
 
 
-def pack_group(src_ref, mask_ref, out_ref, upward, lane, low):
+def pack_group(src_ref, mask_ref, out_ref, g, upward, lane, low):
     def pair(j, i):
         cols = pl.ds(i * LANES, LANES)
         first = src_ref[j, 0, :, cols]
@@ -56,33 +57,34 @@
 
     for i in range(TILES - 1):
         for j in range(NF):
-            out_ref[0, j * (TILES - 1) + i] = pair(j, i)
+            out_ref[g, j * (TILES - 1) + i] = pair(j, i)
     tail = pair(0, TILES - 1)
     for j in range(1, NF):
         moved = pltpu.roll(pair(j, TILES - 1), TAIL * j, 1)
         tail = jnp.where(lane >= TAIL * j, moved, tail)
-    out_ref[0, TPG - 1] = tail
+    out_ref[g, TPG - 1] = tail
 
 
 def pack_kernel(with_mask, south_ref, north_ref, mask_ref, up_ref, dn_ref):
+    g = pl.program_id(0)
     lane = lane_iota()
     low = sub_iota() < 4
-    pack_group(south_ref, mask_ref, up_ref, True, lane, low)
-    pack_group(north_ref, mask_ref, dn_ref, False, lane, low)
+    pack_group(south_ref, mask_ref, up_ref, g, True, lane, low)
+    pack_group(north_ref, mask_ref, dn_ref, g, False, lane, low)
     if with_mask:
-        start = jnp.minimum(pl.program_id(0), TILES // 2 - 1) * (2 * LANES)
+        start = jnp.minimum(g, TILES // 2 - 1) * (2 * LANES)
         start = pl.multiple_of(start, 2 * LANES)
         first = mask_ref[:, pl.ds(start, LANES)].astype(F32)
         second = mask_ref[:, pl.ds(start + LANES, LANES)].astype(F32)
-        up_ref[0, TPG] = jnp.where(low, pltpu.roll(first, 4, 0), second)
-        dn_ref[0, TPG] = jnp.where(low, first, pltpu.roll(second, 4, 0))
+        up_ref[g, TPG] = jnp.where(low, pltpu.roll(first, 4, 0), second)
+        dn_ref[g, TPG] = jnp.where(low, first, pltpu.roll(second, 4, 0))
 
 
 def pack(spectral, sea_mask, base, groups, with_mask):
     tiles = TPG + 1 if with_mask else TPG
     block = (NF, 2, ROWS, TILES * LANES)
-    out = jax.ShapeDtypeStruct((groups, tiles, ROWS, LANES), F32)
-    out_spec = pl.BlockSpec((1, tiles, ROWS, LANES), lambda g: (g, 0, 0, 0))
+    out = pltpu.VMEM((groups, tiles, ROWS, LANES), F32)
+    out_spec = pl.BlockSpec(memory_space=pltpu.VMEM)
     return pl.pallas_call(
         lambda *refs: pack_kernel(with_mask, *refs),
         grid=(groups,),
@@ -93,6 +95,7 @@
         ],
         out_specs=[out_spec, out_spec],
         out_shape=[out, out],
+        compiler_params=pltpu.CompilerParams(vmem_limit_bytes=LIMIT),
         name="pack%d" % base,
     )(spectral, spectral, sea_mask)
 
@@ -106,19 +109,23 @@
     return tiles[:-1] + [jnp.where(lane < TAIL, last, moved)]
 
 
-def advance(tiles, mask_at, alpha, cx, cy, west, south, lane):
+def advance(bins, mask_at, west, south, lane):
     shift = 1 if west else LANES - 1
     edge = (lane == 0) if west else (lane == LANES - 1)
+    fields = [b[0] for b in bins]
     for step in range(STEPS):
-        moved = [pltpu.roll(t, shift, 1) for t in tiles]
+        moved = [[pltpu.roll(t, shift, 1) for t in tiles] for tiles in fields]
         new = []
-        for i in range(TILES):
-            near = moved[i - 1] if west else moved[(i + 1) % TILES]
-            x = jnp.where(edge, near, moved[i])
-            y = pltpu.roll(tiles[i], 1 if south else ROWS - 1, 0)
-            new.append((alpha * tiles[i] + cx * x + cy * y) * mask_at(i))
-        tiles = new
-    return tiles
+        for tiles, shifted, (_, alpha, cx, cy) in zip(fields, moved, bins):
+            done = []
+            for i in range(TILES):
+                near = shifted[i - 1] if west else shifted[(i + 1) % TILES]
+                x = jnp.where(edge, near, shifted[i])
+                y = pltpu.roll(tiles[i], 1 if south else ROWS - 1, 0)
+                done.append((alpha * tiles[i] + cx * x + cy * y) * mask_at(i))
+            new.append(done)
+        fields = new
+    return fields
 
 
 def variants(dp, dd, body):
@@ -138,28 +145,24 @@
     for dd in range(2):
 
         def body(west, south, dd=dd):
-            def one(j, carry):
+            bins = []
+            for j in range(NF):
                 index = j * NDIR + 2 * dp + dd
                 cy = tab_ref[OFF_BY + index]
                 cx = tab_ref[OFF_BX + index] * met_ref[0]
-                alpha = 1.0 - cx - cy
                 start = [
                     src_ref[j, dd, :, pl.ds(i * LANES, LANES)] for i in range(TILES)
                 ]
                 start = fill_wrap(start, west, lane)
                 start = [t * mask_ref[i] for i, t in enumerate(start)]
-                done = advance(
-                    start, lambda i: mask_ref[i], alpha, cx, cy, west, south, lane
-                )
+                bins.append((start, 1.0 - cx - cy, cx, cy))
+            fields = advance(bins, lambda i: mask_ref[i], west, south, lane)
+            for j in range(NF):
                 for i in range(TILES):
-                    if south:
-                        kept = jnp.where(low, start[i], done[i])
-                    else:
-                        kept = jnp.where(low, done[i], start[i])
-                    out_ref[0, dd, j, i] = kept
-                return carry
-
-            lax.fori_loop(0, NF, one, 0)
+                    first, last = bins[j][0][i], fields[j][i]
+                    if not south:
+                        first, last = last, first
+                    out_ref[dp, dd, j, i] = jnp.where(low, first, last)
 
         variants(dp, dd, body)
 
@@ -175,10 +178,9 @@
             whole,
             pl.BlockSpec((NF, 2, ROWS, TILES * LANES), lambda d: (0, d, 0, 0)),
         ],
-        out_specs=pl.BlockSpec(
-            (1, 2, NF, TILES, ROWS, LANES), lambda d: (d, 0, 0, 0, 0, 0)
-        ),
-        out_shape=jax.ShapeDtypeStruct((2 * GROUPS, 2, NF, TILES, ROWS, LANES), F32),
+        out_specs=whole,
+        out_shape=pltpu.VMEM((2 * GROUPS, 2, NF, TILES, ROWS, LANES), F32),
+        compiler_params=pltpu.CompilerParams(vmem_limit_bytes=LIMIT),
         name="own",
     )(table, metric, mask, spectral)
 
@@ -201,6 +203,8 @@
 ):
     step = pl.program_id(0)
     dp = dp_of(step)
+    groups = up_ref.shape[0]
+    group = jnp.where(step < groups, step, 2 * groups - 1 - step)
     lane = lane_iota()
     low = sub_iota() < 4
 
@@ -218,47 +222,35 @@
             side = 0 if south else 1
             swap = (dd == 0) if south else (dd == 1)
 
-            def one(j, carry):
+            bins = []
+            for j in range(NF):
                 index = j * NDIR + 2 * dp + dd
                 cy = tab_ref[OFF_BY + index]
                 cx = tab_ref[OFF_BX + index] * met_ref[1 + side]
-                alpha = 1.0 - cx - cy
                 start = []
-                own = []
                 for i in range(TILES):
                     if i < TILES - 1:
-                        halo = halo_ref[0, j * (TILES - 1) + i]
+                        halo = halo_ref[group, j * (TILES - 1) + i]
                     else:
-                        halo = pltpu.roll(
-                            halo_ref[0, TPG - 1], (LANES - TAIL * j) % LANES, 1
-                        )
+                        halo = halo_ref[group, TPG - 1]
+                        if j > 0:
+                            halo = pltpu.roll(halo, LANES - TAIL * j, 1)
                     if swap:
                         halo = pltpu.roll(halo, 4, 0)
-                    mine = own_ref[0, dd, j, i]
-                    own.append(mine)
+                    mine = own_ref[dp, dd, j, i]
                     if south:
                         start.append(jnp.where(low, mine, halo))
                     else:
                         start.append(jnp.where(low, halo, mine))
                 start = fill_wrap(start, west, lane)
-                done = advance(
-                    start,
-                    lambda i: mask_ref[side, i],
-                    alpha,
-                    cx,
-                    cy,
-                    west,
-                    south,
-                    lane,
-                )
+                bins.append((start, 1.0 - cx - cy, cx, cy))
+            fields = advance(bins, lambda i: mask_ref[side, i], west, south, lane)
+            for j in range(NF):
                 for i in range(TILES):
-                    if south:
-                        e_ref[j, i] = jnp.where(low, done[i], own_ref[0, dd, j, i])
-                    else:
-                        e_ref[j, i] = jnp.where(low, own_ref[0, dd, j, i], done[i])
-                return carry
-
-            lax.fori_loop(0, NF, one, 0)
+                    first, last = fields[j][i], own_ref[dp, dd, j, i]
+                    if not south:
+                        first, last = last, first
+                    e_ref[j, i] = jnp.where(low, first, last)
 
         variants(dp, dd, body)
         cos_d = tab_ref[OFF_COS + 2 * dp + dd]
@@ -282,6 +274,10 @@
             acc_ref[3, i] += sin_d * source
 
 
+def in_vmem(x):
+    return pltpu.with_memory_space_constraint(x, pltpu.VMEM)
+
+
 def finish(table, metric, masks, wind, own, up, dn, prev, old, base):
     first = prev is None
     groups = up.shape[0]
@@ -289,28 +285,20 @@
         dp_of = lambda i: jnp.where(i < groups, i, i + 2 * (GROUPS - groups))
     else:
         dp_of = lambda i: i + base
-    tiles = up.shape[1]
     whole = pl.BlockSpec(memory_space=pltpu.VMEM)
     anywhere = pl.BlockSpec(memory_space=pl.ANY)
-    acc = jax.ShapeDtypeStruct((4, TILES, ROWS, LANES), F32)
+    acc = pltpu.VMEM((4, TILES, ROWS, LANES), F32)
     out = jax.ShapeDtypeStruct((NF, NDIR, ROWS, NLON), F32)
     in_specs = [
         pl.BlockSpec(memory_space=pltpu.SMEM),
         whole,
         whole,
         whole,
-        pl.BlockSpec(
-            (1, 2, NF, TILES, ROWS, LANES), lambda i: (dp_of(i), 0, 0, 0, 0, 0)
-        ),
-        pl.BlockSpec(
-            (1, tiles, ROWS, LANES), lambda i: (jnp.minimum(i, groups - 1), 0, 0, 0)
-        ),
-        pl.BlockSpec(
-            (1, tiles, ROWS, LANES),
-            lambda i: (jnp.minimum(2 * groups - 1 - i, groups - 1), 0, 0, 0),
-        ),
+        whole,
+        whole,
+        whole,
     ]
-    args = [table, metric, masks, wind, own, up, dn]
+    args = [table, metric, masks, wind, in_vmem(own), in_vmem(up), in_vmem(dn)]
     aliases = {}
     if first:
         kernel = lambda *r: finish_kernel(dp_of, True, *r[:7], None, None, *r[7:])
@@ -327,11 +315,12 @@
             pl.BlockSpec(
                 (NF, 2, ROWS, TILES * LANES), lambda i: (0, dp_of(i), 0, 0)
             ),
-            pl.BlockSpec((4, TILES, ROWS, LANES), lambda i: (0, 0, 0, 0)),
+            whole,
         ],
         out_shape=[out, acc],
         scratch_shapes=[pltpu.VMEM((NF, TILES, ROWS, LANES), F32)],
         input_output_aliases=aliases,
+        compiler_params=pltpu.CompilerParams(vmem_limit_bytes=LIMIT),
         name="finish%d" % base,
     )(*args)
 
@@ -339,7 +328,7 @@
 def slots_kernel(order_ref, acc_ref, out_ref):
     lane = lane_iota()
 
-    def owner(k, carry):
+    for k in range(LON_BLOCKS // 2):
         rests = []
         for c in range(4):
             parts = []
@@ -359,9 +348,6 @@
             both = jnp.where(lane < LANES // 2, rests[2 * c], other)
             used = lane % (LANES // 2) < 2 * BLK - LANES
             out_ref[k, 4 + c] = jnp.where(used, both, 0.0)
-        return carry
-
-    lax.fori_loop(0, LON_BLOCKS // 2, owner, 0)
 
 
 def pick_slots(order, acc):
@@ -372,7 +358,8 @@
             pl.BlockSpec(memory_space=pltpu.VMEM),
         ],
         out_specs=pl.BlockSpec(memory_space=pltpu.VMEM),
-        out_shape=jax.ShapeDtypeStruct((LON_BLOCKS // 2, 6, ROWS, LANES), F32),
+        out_shape=pltpu.VMEM((LON_BLOCKS // 2, 6, ROWS, LANES), F32),
+        compiler_params=pltpu.CompilerParams(vmem_limit_bytes=LIMIT),
         name="slots",
     )(order, acc)
 

time: 173 us -> 94 us (0.54)
  Pallas kernels: 134 us -> 42 us
  local copies, waits for them, and re-layouts: 5.01 us -> 18.6 us
    pallas_call x2, Pallas kernels: 66.8 us -> 21.6 us  [finish(): pl.pallas_call(kernel, grid=(2 * groups,), in_specs=in_specs, out_specs=[...]
    pallas_call x1, Pallas kernels: 55.2 us -> 15.7 us  [own_rows(): pl.pallas_call(own_kernel, grid=(2 * GROUPS,), in_specs=[pl.BlockSpec(mem...]
    unnamed x16 -> x20, local copies, waits for them, and re-layouts: 1.1 us -> 12.8 us
    pallas_call x2, Pallas kernels: 8.52 us -> 3.67 us  [pack(): pl.pallas_call(lambda *refs: pack_kernel(with_mask, *refs), grid=(groups,...]
    pallas_call x1, Pallas kernels: 3.34 us -> 1.04 us  [pick_slots(): pl.pallas_call(slots_kernel, in_specs=[pl.BlockSpec(memory_space=pltpu.SM...]
    concatenate x3, local copies, waits for them, and re-layouts: 0.85 us -> 3.05 us  [with_wrap(): jnp.concatenate([field, field[:, :side], field[:, NLON - side:]], axis=1)]
  transfers between devices with their start and end apart: 4 -> 4, of which waited for: 0 -> 0; matrix products, arithmetic and copies ran while one was open for 4% -> 9% of each run, Pallas kernels for 63% -> 36%
where the time goes in v2:
time: 94 us; the launch traced here: 93.4 us
  Pallas kernels  42 us (45%)
  local copies, waits for them, and re-layouts  18.6 us (20%)
  blocking collectives  15.2 us (16%)
  starting transfers between devices  12.9 us (14%)
  other arithmetic  3.92 us (4%)
    pallas_call x2, Pallas kernels, finish(): pl.pallas_call(kernel, grid=(2 * groups,), in_specs=in_specs, out_specs=[...  21.6 us
    pallas_call x1, Pallas kernels, own_rows(): pl.pallas_call(own_kernel, grid=(2 * GROUPS,), in_specs=[pl.BlockSpec(mem...  15.7 us
    all_to_all x1, blocking collectives, shards(): got = lax.all_to_all(sent, 'bins', 0, 0, tiled=True)  15.2 us
    unnamed x20, local copies, waits for them, and re-layouts  12.8 us
    ppermute x1, starting transfers between devices, shards(): dn2 = lax.ppermute(dn2, 'tiles', dn_pairs)  4.54 us
    ppermute x1, starting transfers between devices, shards(): dn1 = lax.ppermute(dn1, 'tiles', dn_pairs)  4.54 us
    pallas_call x2, Pallas kernels, pack(): pl.pallas_call(lambda *refs: pack_kernel(with_mask, *refs), grid=(groups,...  3.67 us
    concatenate x3, local copies, waits for them, and re-layouts, with_wrap(): jnp.concatenate([field, field[:, :side], field[:, NLON - side:]], axis=1)  3.05 us
  transfers between devices with their start and end apart: 4, of which 0 were waited for; matrix products, arithmetic and copies ran while one was open for 9% of the time, Pallas kernels for 36%

profile of v2, /device:TPU:32, one launch (start us, length us, event | category | flops | bytes accessed | tf_op | source)
XLA Modules:
  0.0 93.4 jit_solution(7231605854084177306)
XLA Ops:
  0.6 3.0 %copy-done = f32[144,8,1440]{2,1,0:T(8,128)S(1)} copy-done((f32[144,8,1440]{2,1,0:T(8,128)S(1)}, f32[144,8,1440]{2,1,0:T(8,128)}, u32[]{:S(2)}) %copy-start) | copy-done | bytes 6635544
  3.6 0.8 copy-done.4
  4.4 2.5 %pack0.1 = (f32[7,46,8,128]{3,2,1,0:T(8,128)}, f32[7,46,8,128]{3,2,1,0:T(8,128)}) custom-call(f32[4,36,8,1440]{3,2,1,0:T(8,128)S(1)} %bitcast.40, f32[4,36,8,1440]{3,2,1,0:T(8,128)S(1)} %bitcast.41, s32[8,1440]{1,0:T(8,128)S(1)} %copy-done.4), custom_call_target="tpu_custom_call" | custom-call | tf_op jit(solution)/shard_map/pack0/pallas_call | solution.py:88
  6.9 1.9 %collective-permute-start = (f32[7,46,8,128]{3,2,1,0:T(8,128)}, f32[7,46,8,128]{3,2,1,0:T(8,128)S(1)}, u32[]{:S(2)}, u32[]{:S(2)}) collective-permute-start(f32[7,46,8,128]{3,2,1,0:T(8,128)} %get-tuple-element.12), channel_id=1, source_target_pairs={{0,1},{1,2},{2,3},{3,4},{4,5},{5,6},{6,7},{7,8},{8,9},{9,10},{10,1... | collective-permute-start | bytes 3956744 | tf_op jit(solution)/shard_map/ppermute | solution.py:395
  8.8 4.5 %collective-permute-start.1 = (f32[7,46,8,128]{3,2,1,0:T(8,128)}, f32[7,46,8,128]{3,2,1,0:T(8,128)S(1)}, u32[]{:S(2)}, u32[]{:S(2)}) collective-permute-start(f32[7,46,8,128]{3,2,1,0:T(8,128)} %get-tuple-element.13), channel_id=1, source_target_pairs={{1,0},{2,1},{3,2},{4,3},{5,4},{6,5},{7,6},{8,7},{9,8},{10,9},{11,1... | collective-permute-start | bytes 3956744 | tf_op jit(solution)/shard_map/ppermute | solution.py:396
  13.4 1.2 %pack7.1 = (f32[2,45,8,128]{3,2,1,0:T(8,128)}, f32[2,45,8,128]{3,2,1,0:T(8,128)}) custom-call(f32[4,36,8,1440]{3,2,1,0:T(8,128)S(1)} %bitcast.42, f32[4,36,8,1440]{3,2,1,0:T(8,128)S(1)} %bitcast.43, s32[8,1440]{1,0:T(8,128)S(1)} %copy-done.4), custom_call_target="tpu_custom_call" | custom-call | tf_op jit(solution)/shard_map/pack7/pallas_call | solution.py:88
  14.6 1.9 %collective-permute-start.2 = (f32[2,45,8,128]{3,2,1,0:T(8,128)}, f32[2,45,8,128]{3,2,1,0:T(8,128)S(1)}, u32[]{:S(2)}, u32[]{:S(2)}) collective-permute-start(f32[2,45,8,128]{3,2,1,0:T(8,128)} %get-tuple-element.14), channel_id=1, source_target_pairs={{0,1},{1,2},{2,3},{3,4},{4,5},{5,6},{6,7},{7,8},{8,9},{9,10},{10,1... | collective-permute-start | bytes 1105928 | tf_op jit(solution)/shard_map/ppermute | solution.py:398
  16.5 4.5 %collective-permute-start.3 = (f32[2,45,8,128]{3,2,1,0:T(8,128)}, f32[2,45,8,128]{3,2,1,0:T(8,128)S(1)}, u32[]{:S(2)}, u32[]{:S(2)}) collective-permute-start(f32[2,45,8,128]{3,2,1,0:T(8,128)} %get-tuple-element.15), channel_id=1, source_target_pairs={{1,0},{2,1},{3,2},{4,3},{5,4},{6,5},{7,6},{8,7},{9,8},{10,9},{11,1... | collective-permute-start | bytes 1105928 | tf_op jit(solution)/shard_map/ppermute | solution.py:399
  21.6 1.2 %sort.17 = (s32[16]{0:T(128)}, s32[16]{0:T(128)S(1)}) sort(s32[16]{0:T(128)S(1)} %bitcast.54, s32[16]{0:T(128)S(1)} %iota.43), dimensions={0}, to_apply=%region_0.1 | sort | flops 64 | bytes 256 | tf_op jit(solution)/shard_map/jit(argsort)/sort | solution.py:436
  23.1 3.0 %copy-done.1 = f32[144,8,1440]{2,1,0:T(8,128)S(1)} copy-done((f32[144,8,1440]{2,1,0:T(8,128)S(1)}, f32[144,8,1440]{2,1,0:T(8,128)}, u32[]{:S(2)}) %copy-start.1) | copy-done | bytes 6635544
  26.1 15.7 %own.1.r_4_ = f32[18,2,4,12,8,128]{5,4,3,2,1,0:T(8,128)S(1)} custom-call(f32[364]{0:T(512)S(1)} %concatenate.28.tab_ref.r_0_, f32[3,8,128]{2,1,0:T(8,128)S(1)} %broadcast_in_dim.2.met_ref.r_1_, f32[12,8,128]{2,1,0:T(8,128)S(1)} %bitcast.45, f32[4,36,8,1440]{3,2,1,0:T(8,128)S(1)} %bitcast.44), custom_call_target="tpu_custom_call" | custom-call | tf_op jit(solution)/shard_map/own/pallas_call | solution.py:172
  41.8 3.0 %copy-done.2 = f32[18,2,4,12,8,128]{5,4,3,2,1,0:T(8,128)} copy-done((f32[18,2,4,12,8,128]{5,4,3,2,1,0:T(8,128)}, f32[18,2,4,12,8,128]{5,4,3,2,1,0:T(8,128)S(1)}, u32[]{:S(2)}) %copy-start.2) | copy-done | bytes 7077912
  45.1 0.9 fusion.16
  46.7 0.7 pad_maximum_fusion.1
  47.3 1.5 %concatenate.30 = f32[8,1536]{1,0:T(8,128)} concatenate(f32[8,1440]{1,0:T(8,128)} %get-tuple-element.43, f32[8,48]{1,0:T(8,128)S(1)} %get-tuple-element.45, f32[8,48]{1,0:T(8,128)} %get-tuple-element.46), dimensions={1} | concatenate | bytes 98304 | tf_op jit(solution)/shard_map/concatenate | solution.py:373
  48.8 1.5 %concatenate.32 = f32[8,1536]{1,0:T(8,128)} concatenate(f32[8,1440]{1,0:T(8,128)} %get-tuple-element.44, f32[8,48]{1,0:T(8,128)S(1)} %get-tuple-element.30, f32[8,48]{1,0:T(8,128)S(1)} %get-tuple-element.29), dimensions={1} | concatenate | bytes 98304 | tf_op jit(solution)/shard_map/concatenate | solution.py:373
  50.3 0.8 pad_maximum_fusion.r_2_
  51.1 3.0 %copy-done.3 = f32[18,2,4,12,8,128]{5,4,3,2,1,0:T(8,128)S(1)} copy-done((f32[18,2,4,12,8,128]{5,4,3,2,1,0:T(8,128)S(1)}, f32[18,2,4,12,8,128]{5,4,3,2,1,0:T(8,128)}, u32[]{:S(2)}) %copy-start.3) | copy-done | bytes 7077912
  54.1 16.3 %finish0.1 = (f32[4,36,8,1440]{3,2,1,0:T(8,128)}, f32[4,12,8,128]{3,2,1,0:T(8,128)S(1)}) custom-call(f32[364]{0:T(512)S(1)} %concatenate.28.tab_ref.r_0_, f32[3,8,128]{2,1,0:T(8,128)S(1)} %broadcast_in_dim.2.met_ref.r_1_, f32[2,12,8,128]{3,2,1,0:T(8,128)S(1)} %pad_maximum_fusion.r_2_, f32[3,12,8,128]{3,2,1,0:T(8,128)S(1)} %fusion.r_3_, ...), custom_call_target="tpu_custom_call" | custom-call | tf_op jit(solution)/shard_map/finish0/pallas_call | solution.py:310
  70.4 5.3 %finish7.1 = (f32[4,36,8,1440]{3,2,1,0:T(8,128)}, f32[4,12,8,128]{3,2,1,0:T(8,128)S(1)}) custom-call(f32[364]{0:T(512)S(1)} %concatenate.28.tab_ref.r_0_, f32[3,8,128]{2,1,0:T(8,128)S(1)} %broadcast_in_dim.2.met_ref.r_1_, f32[2,12,8,128]{3,2,1,0:T(8,128)S(1)} %pad_maximum_fusion.r_2_, ...), custom_call_target="tpu_custom_call", output_to_operand_aliasing={{0}: (8, {})} | custom-call | tf_op jit(solution)/shard_map/finish7/pallas_call | solution.py:310
  75.7 1.0 %slots.1 = f32[8,6,8,128]{3,2,1,0:T(8,128)S(1)} custom-call(s32[16]{0:T(128)S(1)} %get-tuple-element.19.order_ref, f32[4,12,8,128]{3,2,1,0:T(8,128)S(1)} %get-tuple-element.20.acc_ref), custom_call_target="tpu_custom_call" | custom-call | tf_op jit(solution)/shard_map/slots/pallas_call | solution.py:354
  76.8 15.2 %all_to_all.5 = f32[8,6,8,128]{3,2,1,0:T(8,128)S(1)} all-to-all(f32[8,6,8,128]{3,2,1,0:T(8,128)S(1)} %slots.1), channel_id=1, replica_groups=mesh['bins'=8,'tiles'=16] {'bins'}, dimensions={0} | all-to-all | bytes 393216 | tf_op jit(solution)/shard_map/all_to_all | solution.py:448
  92.0 0.7 slice.80
  92.7 0.7 slice.82
  (46 shorter events, 1.8 us)
Async XLA Ops:
  0.6 3.0 %copy-start = (f32[144,8,1440]{2,1,0:T(8,128)S(1)}, f32[144,8,1440]{2,1,0:T(8,128)}, u32[]{:S(2)}) copy-start(f32[144,8,1440]{2,1,0:T(8,128)} %param.6) | copy-start | bytes 19906564
  3.6 0.8 copy-start.4
  6.9 39.0 %collective-permute-start = (f32[7,46,8,128]{3,2,1,0:T(8,128)}, f32[7,46,8,128]{3,2,1,0:T(8,128)S(1)}, u32[]{:S(2)}, u32[]{:S(2)}) collective-permute-start(f32[7,46,8,128]{3,2,1,0:T(8,128)} %get-tuple-element.12), channel_id=1, source_target_pairs={{0,1},{1,2},{2,3},{3,4},{4,5},{5,6},{6,7},{7,8},{8,9},{9,10},{10,1... | collective-permute-start | bytes 3956744 | tf_op jit(solution)/shard_map/ppermute | solution.py:395
  8.8 12.8 %copy-start.9 = (s32[1,16]{1,0:T(1,128)S(1)}, s32[1,16]{1,0:T(1,128)}, u32[]{:S(2)}) copy-start(s32[1,16]{1,0:T(1,128)} %param.11) | copy-start | bytes 196
  8.8 37.1 %collective-permute-start.1 = (f32[7,46,8,128]{3,2,1,0:T(8,128)}, f32[7,46,8,128]{3,2,1,0:T(8,128)S(1)}, u32[]{:S(2)}, u32[]{:S(2)}) collective-permute-start(f32[7,46,8,128]{3,2,1,0:T(8,128)} %get-tuple-element.13), channel_id=1, source_target_pairs={{1,0},{2,1},{3,2},{4,3},{5,4},{6,5},{7,6},{8,7},{9,8},{10,9},{11,1... | collective-permute-start | bytes 3956744 | tf_op jit(solution)/shard_map/ppermute | solution.py:396
  14.6 55.8 %collective-permute-start.2 = (f32[2,45,8,128]{3,2,1,0:T(8,128)}, f32[2,45,8,128]{3,2,1,0:T(8,128)S(1)}, u32[]{:S(2)}, u32[]{:S(2)}) collective-permute-start(f32[2,45,8,128]{3,2,1,0:T(8,128)} %get-tuple-element.14), channel_id=1, source_target_pairs={{0,1},{1,2},{2,3},{3,4},{4,5},{5,6},{6,7},{7,8},{8,9},{9,10},{10,1... | collective-permute-start | bytes 1105928 | tf_op jit(solution)/shard_map/ppermute | solution.py:398
  16.5 53.9 %collective-permute-start.3 = (f32[2,45,8,128]{3,2,1,0:T(8,128)}, f32[2,45,8,128]{3,2,1,0:T(8,128)S(1)}, u32[]{:S(2)}, u32[]{:S(2)}) collective-permute-start(f32[2,45,8,128]{3,2,1,0:T(8,128)} %get-tuple-element.15), channel_id=1, source_target_pairs={{1,0},{2,1},{3,2},{4,3},{5,4},{6,5},{7,6},{8,7},{9,8},{10,9},{11,1... | collective-permute-start | bytes 1105928 | tf_op jit(solution)/shard_map/ppermute | solution.py:399
  21.1 20.8 %copy-start.5 = (f32[8,1440]{1,0:T(8,128)}, f32[8,1440]{1,0:T(8,128)S(1)}, u32[]{:S(2)}) copy-start(f32[8,1440]{1,0:T(8,128)S(1)} %convert_element_type.41) | copy-start | bytes 138244
  23.1 3.0 %copy-start.1 = (f32[144,8,1440]{2,1,0:T(8,128)S(1)}, f32[144,8,1440]{2,1,0:T(8,128)}, u32[]{:S(2)}) copy-start(f32[144,8,1440]{2,1,0:T(8,128)} %param.6) | copy-start | bytes 19906564
  26.1 18.7 %copy-start.6 = (s32[8,1440]{1,0:T(8,128)S(1)}, s32[8,1440]{1,0:T(8,128)}, u32[]{:S(2)}) copy-start(s32[8,1440]{1,0:T(8,128)} %param.8) | copy-start | bytes 138244
  26.1 18.7 %copy-start.7 = (f32[8,1440]{1,0:T(8,128)S(1)}, f32[8,1440]{1,0:T(8,128)}, u32[]{:S(2)}) copy-start(f32[8,1440]{1,0:T(8,128)} %param.10) | copy-start | bytes 138244
  26.1 18.7 %copy-start.8 = (f32[8,1440]{1,0:T(8,128)S(1)}, f32[8,1440]{1,0:T(8,128)}, u32[]{:S(2)}) copy-start(f32[8,1440]{1,0:T(8,128)} %param.9) | copy-start | bytes 138244
  41.8 3.0 %copy-start.2 = (f32[18,2,4,12,8,128]{5,4,3,2,1,0:T(8,128)}, f32[18,2,4,12,8,128]{5,4,3,2,1,0:T(8,128)S(1)}, u32[]{:S(2)}) copy-start(f32[18,2,4,12,8,128]{5,4,3,2,1,0:T(8,128)S(1)} %own.1.r_4_) | copy-start | bytes 21233668
  51.1 3.0 %copy-start.3 = (f32[18,2,4,12,8,128]{5,4,3,2,1,0:T(8,128)S(1)}, f32[18,2,4,12,8,128]{5,4,3,2,1,0:T(8,128)}, u32[]{:S(2)}) copy-start(f32[18,2,4,12,8,128]{5,4,3,2,1,0:T(8,128)} %copy-done.2) | copy-start | bytes 21233668

commit v3 on v2

v3 whole, which is shorter than its diff:
```python
import math

import jax
import jax.numpy as jnp
from jax import lax
from jax.experimental import pallas as pl
from jax.experimental.pallas import tpu as pltpu
from jax.sharding import PartitionSpec as P

NDIR = 36
NFREQ = 32
LON_BLOCKS = 16
STEPS = 4
COURANT_MAX = 0.6
GRID_STEP = 0.25 * math.pi / 180.0

ROWS = 8
NLON = 1440
BLK = 90
LANES = 128
TILES = 12
TAIL = NLON - (TILES - 1) * LANES
NF = 4
GROUPS = 9
G1 = 6
G2 = GROUPS - G1
TPG = NF * (TILES - 1) + 1

F32 = jnp.float32
PER_STEP = 2
LIMIT = 16 << 20
OFF_BX = 0
OFF_BY = NF * NDIR
OFF_COS = 2 * NF * NDIR
OFF_SIN = OFF_COS + NDIR
OFF_P = OFF_SIN + NDIR


def lane_iota():
    return lax.broadcasted_iota(jnp.int32, (ROWS, LANES), 1)


def sub_iota():
    return lax.broadcasted_iota(jnp.int32, (ROWS, LANES), 0)


def pack_group(src_ref, local, mask_ref, out_ref, group, upward, lane, low):
    def pair(j, i):
        cols = pl.ds(i * LANES, LANES)
        mask = mask_ref[:, cols].astype(F32)
        first = src_ref[j, 2 * local, :, cols] * mask
        second = src_ref[j, 2 * local + 1, :, cols] * mask
        if upward:
            return jnp.where(low, pltpu.roll(first, 4, 0), second)
        return jnp.where(low, first, pltpu.roll(second, 4, 0))

    for i in range(TILES - 1):
        for j in range(NF):
            out_ref[group, j * (TILES - 1) + i] = pair(j, i)
    tail = pair(0, TILES - 1)
    for j in range(1, NF):
        moved = pltpu.roll(pair(j, TILES - 1), TAIL * j, 1)
        tail = jnp.where(lane >= TAIL * j, moved, tail)
    out_ref[group, TPG - 1] = tail


def pack_kernel(width, with_mask, south_ref, north_ref, mask_ref, up_ref, dn_ref):
    lane = lane_iota()
    low = sub_iota() < 4
    for u in range(width):
        g = pl.program_id(0) * width + u
        pack_group(south_ref, u, mask_ref, up_ref, g, True, lane, low)
        pack_group(north_ref, width - 1 - u, mask_ref, dn_ref, g, False, lane, low)
        if with_mask:
            start = jnp.minimum(g, TILES // 2 - 1) * (2 * LANES)
            start = pl.multiple_of(start, 2 * LANES)
            first = mask_ref[:, pl.ds(start, LANES)].astype(F32)
            second = mask_ref[:, pl.ds(start + LANES, LANES)].astype(F32)
            up_ref[g, TPG] = jnp.where(low, pltpu.roll(first, 4, 0), second)
            dn_ref[g, TPG] = jnp.where(low, first, pltpu.roll(second, 4, 0))


def pack(spectral, sea_mask, base, groups, width, with_mask):
    tiles = TPG + 1 if with_mask else TPG
    block = (NF, 2 * width, ROWS, TILES * LANES)
    last = (2 * GROUPS - base) // width - 1
    whole = pl.BlockSpec(memory_space=pltpu.VMEM)
    out = pltpu.VMEM((groups, tiles, ROWS, LANES), F32)
    return pl.pallas_call(
        lambda *refs: pack_kernel(width, with_mask, *refs),
        grid=(groups // width,),
        in_specs=[
            pl.BlockSpec(block, lambda g: (0, base // width + g, 0, 0)),
            pl.BlockSpec(block, lambda g: (0, last - g, 0, 0)),
            pl.BlockSpec((ROWS, TILES * LANES), lambda g: (0, 0)),
        ],
        out_specs=[whole, whole],
        out_shape=[out, out],
        compiler_params=pltpu.CompilerParams(vmem_limit_bytes=LIMIT),
        name="pack%d" % base,
    )(spectral, spectral, sea_mask)


WEST, EAST, BOTH = 0, 1, 2


def fill_wrap(tiles, lane):
    last = tiles[-1]
    after = pltpu.roll(tiles[0], TAIL, 1)
    before = pltpu.roll(last, LANES - TAIL, 1)
    filled = jnp.where(lane < LANES - TAIL, after, before)
    return tiles[:-1] + [jnp.where(lane < TAIL, last, filled)]


def shift_lanes(tiles, west, lane):
    if west:
        moved = [pltpu.roll(t, 1, 1) for t in tiles]
        return [jnp.where(lane == 0, moved[i - 1], moved[i]) for i in range(TILES)]
    moved = [pltpu.roll(t, LANES - 1, 1) for t in tiles]
    return [
        jnp.where(lane == LANES - 1, moved[(i + 1) % TILES], moved[i])
        for i in range(TILES)
    ]


def x_side(direction):
    west = direction < NDIR // 4 or direction >= NDIR - NDIR // 4
    return WEST if west else EAST


def pair_side(dp):
    first, second = x_side(2 * dp), x_side(2 * dp + 1)
    return first if first == second else BOTH


def run_cases(index, values, south_below, side_of, body):
    found = {}
    for v in values:
        found.setdefault((v < south_below, side_of(v)), []).append(v)
    for (south, side), members in sorted(found.items()):
        cond = index == members[0]
        for m in members[1:]:
            cond = jnp.logical_or(cond, index == m)
        pl.when(cond)(lambda south=south, side=side: body(south, side))


def chunk_dps(base, groups):
    south = [base + g for g in range(groups)]
    return south + [2 * GROUPS - 1 - d for d in reversed(south)]


def block_at(base, groups, width, step):
    first = base // width
    if base + groups == GROUPS:
        return first + step
    skip = 2 * (GROUPS - base - groups) // width
    return jnp.where(step < groups // width, first + step, first + skip + step)


def load_tiles(ref):
    return [ref[:, pl.ds(i * LANES, LANES)].astype(F32) for i in range(TILES)]


def own_kernel(
    tab_ref,
    met_ref,
    sea_ref,
    ice_ref,
    friction_ref,
    wind_ref,
    src_ref,
    out_ref,
    mask_ref,
    force_ref,
):
    step = pl.program_id(0)
    lane = lane_iota()
    sub = sub_iota()

    @pl.when(step == 0)
    def _():
        sea = fill_wrap(load_tiles(sea_ref), lane)
        ice = load_tiles(ice_ref)
        friction = load_tiles(friction_ref)
        wind = load_tiles(wind_ref)
        for i in range(TILES):
            strength = 0.5 * friction[i] * friction[i]
            mask_ref[i] = sea[i]
            force_ref[0, i] = strength * jnp.cos(wind[i])
            force_ref[1, i] = strength * jnp.sin(wind[i])
            force_ref[2, i] = 1.0 - 0.5 * ice[i]

    def one(local, carry):
        direction = 2 * PER_STEP * step + local

        def body(south, side):
            west = side == WEST
            inflow = sub > 0 if south else sub < ROWS - 1
            fields = []
            coefs = []
            for j in range(NF):
                cy = tab_ref[OFF_BY + j * NDIR + direction]
                cx = tab_ref[OFF_BX + j * NDIR + direction] * met_ref[0]
                alpha = 1.0 - cx - cy
                coefs.append((alpha, cx, jnp.where(inflow, cy, 0.0)))
                tiles = [
                    src_ref[j, local, :, pl.ds(i * LANES, LANES)] for i in range(TILES)
                ]
                tiles = fill_wrap(tiles, lane)
                fields.append([t * mask_ref[i] for i, t in enumerate(tiles)])
            for sub_step in range(STEPS):
                new = []
                for tiles, (alpha, cx, cy) in zip(fields, coefs):
                    xs = shift_lanes(tiles, west, lane)
                    done = []
                    for i in range(TILES):
                        y = pltpu.roll(tiles[i], 1 if south else ROWS - 1, 0)
                        total = alpha * tiles[i] + cx * xs[i] + cy * y
                        done.append(total * mask_ref[i])
                    new.append(done)
                fields = new
            for j in range(NF):
                for i in range(TILES):
                    out_ref[local // 2, local % 2, j, i] = fields[j][i]

        run_cases(direction, range(NDIR), NDIR // 2, x_side, body)
        return carry

    lax.fori_loop(0, 2 * PER_STEP, one, 0)


def own_rows(spectral, table, metric, sea_mask, ice_mask, friction, wind_dir):
    whole = pl.BlockSpec(memory_space=pltpu.VMEM)
    field = pl.BlockSpec((ROWS, TILES * LANES), lambda i: (0, 0))
    return pl.pallas_call(
        own_kernel,
        grid=(2 * GROUPS // PER_STEP,),
        in_specs=[
            pl.BlockSpec(memory_space=pltpu.SMEM),
            whole,
            field,
            field,
            field,
            field,
            pl.BlockSpec(
                (NF, 2 * PER_STEP, ROWS, TILES * LANES), lambda i: (0, i, 0, 0)
            ),
        ],
        out_specs=[
            pl.BlockSpec(
                (PER_STEP, 2, NF, TILES, ROWS, LANES), lambda i: (i, 0, 0, 0, 0, 0)
            ),
            whole,
            whole,
        ],
        out_shape=[
            jax.ShapeDtypeStruct((2 * GROUPS, 2, NF, TILES, ROWS, LANES), F32),
            pltpu.VMEM((TILES, ROWS, LANES), F32),
            pltpu.VMEM((3, TILES, ROWS, LANES), F32),
        ],
        compiler_params=pltpu.CompilerParams(vmem_limit_bytes=LIMIT),
        name="own",
    )(table, metric, sea_mask, ice_mask, friction, wind_dir, spectral)


def window_masks(mask_ref, up_ref, dn_ref, out_ref, lane, low):
    for side, halo_ref in enumerate((up_ref, dn_ref)):
        rows = []
        for i in range(TILES):
            edge = halo_ref[i // 2, 0]
            if i % 2 != side:
                edge = pltpu.roll(edge, 4, 0)
            mine = pltpu.roll(mask_ref[i], 4, 0)
            if side == 0:
                rows.append(jnp.where(low, edge, mine))
            else:
                rows.append(jnp.where(low, mine, edge))
        rows = fill_wrap(rows, lane)
        for k in range(1, STEPS + 1):
            first = k if side == 0 else 4 - k
            for i in range(TILES):
                window = rows[i]
                if first > 0:
                    window = pltpu.roll(window, ROWS - first, 0)
                out_ref[side, k - 1, i] = jnp.where(
                    low, window, pltpu.roll(window, 4, 0)
                )


def finish_kernel(
    base,
    groups,
    width,
    tab_ref,
    met_ref,
    mask_ref,
    wind_ref,
    own_ref,
    up_ref,
    dn_ref,
    up_mask_ref,
    dn_mask_ref,
    prev_ref,
    old_ref,
    out_ref,
    acc_ref,
    win_ref,
    c_ref,
):
    step = pl.program_id(0)
    dps = chunk_dps(base, groups)
    lane = lane_iota()
    sub = sub_iota()
    low = sub < 4

    @pl.when(step == 0)
    def _():
        if prev_ref is None:
            acc_ref[...] = jnp.zeros_like(acc_ref)
            window_masks(mask_ref, up_mask_ref, dn_mask_ref, win_ref, lane, low)
        else:
            acc_ref[...] = prev_ref[...]

    windows = win_ref if prev_ref is None else mask_ref

    def one(local, carry):
        dp = block_at(base, groups, width, step) * width + local

        def contribution(south, side):
            halo_ref = up_ref if south else dn_ref
            row = 0 if south else 1
            group = local if south else width - 1 - local
            fields = []
            scalars = []
            for j in range(NF):
                index = j * NDIR + 2 * dp
                bx = jnp.where(low, tab_ref[OFF_BX + index], tab_ref[OFF_BX + index + 1])
                cy = jnp.where(low, tab_ref[OFF_BY + index], tab_ref[OFF_BY + index + 1])
                inside = sub % 4 < 3 if south else sub % 4 > 0
                scalars.append((bx, cy, jnp.where(inside, 1.0 - cy, 0.0)))
                tiles = [halo_ref[group, j * (TILES - 1) + i] for i in range(TILES - 1)]
                last = halo_ref[group, TPG - 1]
                if j > 0:
                    last = pltpu.roll(last, LANES - TAIL * j, 1)
                fields.append(fill_wrap(tiles + [last], lane))
            for k in range(STEPS):
                new = []
                for tiles, (bx, cy, rest) in zip(fields, scalars):
                    cx = bx * met_ref[1 + row * STEPS + k]
                    alpha = rest - cx
                    ahead = [pltpu.roll(t, ROWS - 1 if south else 1, 0) for t in tiles]
                    if side == BOTH:
                        west = shift_lanes(ahead, True, lane)
                        east = shift_lanes(ahead, False, lane)
                        here = low if south else jnp.logical_not(low)
                        xs = [jnp.where(here, w, e) for w, e in zip(west, east)]
                    else:
                        xs = shift_lanes(ahead, side == WEST, lane)
                    new.append(
                        [
                            (alpha * ahead[i] + cx * xs[i] + cy * tiles[i])
                            * windows[row, k, i]
                            for i in range(TILES)
                        ]
                    )
                fields = new
            for j in range(NF):
                for i in range(TILES):
                    c_ref[j, i] = fields[j][i]

        run_cases(dp, dps, GROUPS, pair_side, contribution)

        def combine(south, side):
            weight = [tab_ref[OFF_P + j] for j in range(NF)]
            angle = [
                (tab_ref[OFF_COS + 2 * dp + dd], tab_ref[OFF_SIN + 2 * dp + dd])
                for dd in range(2)
            ]
            target = low if south else jnp.logical_not(low)
            for i in range(TILES):
                ice = wind_ref[2, i]
                parts = []
                for j in range(NF):
                    c = c_ref[j, i]
                    turned = pltpu.roll(c, 4, 0)
                    parts.append((c, turned) if south else (turned, c))
                total = [acc_ref[n, i] for n in range(4)]
                for dd in range(2):
                    cos_d, sin_d = angle[dd]
                    h = cos_d * wind_ref[0, i] + sin_d * wind_ref[1, i]
                    h = jnp.maximum(h, 0.0)
                    for j in range(NF):
                        e = own_ref[local, dd, j, i] + jnp.where(target, parts[j][dd], 0.0)
                        x = weight[j] * e
                        out_ref[j, 2 * local + dd, :, pl.ds(i * LANES, LANES)] = (e + h * x) * ice
                        y = weight[j] * x
                        sum_x = x if j == 0 else sum_x + x
                        sum_y = y if j == 0 else sum_y + y
                    source = h * sum_x
                    drift = ice * (sum_x + h * sum_y)
                    total[0] += cos_d * drift
                    total[1] += sin_d * drift
                    total[2] += cos_d * source
                    total[3] += sin_d * source
                for n in range(4):
                    acc_ref[n, i] = total[n]

        run_cases(dp, dps, GROUPS, lambda d: WEST, combine)
        return carry

    lax.fori_loop(0, width, one, 0)


def in_vmem(x):
    return pltpu.with_memory_space_constraint(x, pltpu.VMEM)


def in_hbm(x):
    return pltpu.with_memory_space_constraint(x, pltpu.HBM)


def finish(table, metric, mask, wind, own, up, dn, prev, old, base, width):
    groups = up.shape[0]
    tiles = up.shape[1]
    steps = groups // width
    whole = pl.BlockSpec(memory_space=pltpu.VMEM)
    acc = pltpu.VMEM((4, TILES, ROWS, LANES), F32)
    out = jax.ShapeDtypeStruct((NF, NDIR, ROWS, NLON), F32)
    halo = (width, tiles, ROWS, LANES)
    block = lambda i: block_at(base, groups, width, i)
    in_specs = [
        pl.BlockSpec(memory_space=pltpu.SMEM),
        whole,
        whole,
        whole,
        pl.BlockSpec(
            (width, 2, NF, TILES, ROWS, LANES), lambda i: (block(i), 0, 0, 0, 0, 0)
        ),
        pl.BlockSpec(halo, lambda i: (jnp.minimum(i, steps - 1), 0, 0, 0)),
        pl.BlockSpec(
            halo, lambda i: (jnp.minimum(2 * steps - 1 - i, steps - 1), 0, 0, 0)
        ),
    ]
    args = [table, metric, in_vmem(mask), in_vmem(wind), own, in_hbm(up), in_hbm(dn)]
    out_specs = [
        pl.BlockSpec(
            (NF, 2 * width, ROWS, TILES * LANES), lambda i: (0, block(i), 0, 0)
        ),
        whole,
    ]
    out_shape = [out, acc]
    aliases = {}
    setting = (base, groups, width)
    if prev is None:
        kernel = lambda *r: finish_kernel(*setting, *r[:9], None, None, *r[9:])
        edges = pl.BlockSpec((TILES // 2, 1, ROWS, LANES), lambda i: (0, TPG, 0, 0))
        in_specs += [edges, edges]
        args += args[5:7]
        out_specs.append(whole)
        out_shape.append(pltpu.VMEM((2, STEPS, TILES, ROWS, LANES), F32))
    else:
        kernel = lambda *r: finish_kernel(
            *setting, *r[:7], None, None, *r[7:11], None, *r[11:]
        )
        in_specs += [whole, pl.BlockSpec(memory_space=pl.ANY)]
        args += [in_vmem(prev), old]
        aliases = {8: 0}
    return pl.pallas_call(
        kernel,
        grid=(2 * steps,),
        in_specs=in_specs,
        out_specs=out_specs,
        out_shape=out_shape,
        scratch_shapes=[pltpu.VMEM((NF, TILES, ROWS, LANES), F32)],
        input_output_aliases=aliases,
        compiler_params=pltpu.CompilerParams(vmem_limit_bytes=LIMIT),
        name="finish%d" % base,
    )(*args)


def slots_kernel(owner_ref, acc_ref, out_ref, order_ref, count_ref):
    lane = lane_iota()
    for k in range(LON_BLOCKS // 2):
        count_ref[k] = 0
    for block in range(LON_BLOCKS):
        owner = owner_ref[0, block]
        seen = count_ref[owner]
        order_ref[2 * owner + seen] = block
        count_ref[owner] = seen + 1

    for k in range(LON_BLOCKS // 2):
        rests = []
        for c in range(4):
            parts = []
            for s in range(2):
                column = order_ref[2 * k + s] * BLK
                tile = column // LANES
                shift = column % LANES
                back = (LANES - shift) % LANES
                here = pltpu.roll(acc_ref[c, tile], back, 1)
                after = pltpu.roll(acc_ref[c, jnp.minimum(tile + 1, TILES - 1)], back, 1)
                parts.append(jnp.where(lane < LANES - shift, here, after))
            moved = pltpu.roll(parts[1], BLK, 1)
            out_ref[k, c] = jnp.where(lane < BLK, parts[0], moved)
            rests.append(moved)
        for c in range(2):
            other = pltpu.roll(rests[2 * c + 1], LANES // 2, 1)
            both = jnp.where(lane < LANES // 2, rests[2 * c], other)
            used = lane % (LANES // 2) < 2 * BLK - LANES
            out_ref[k, 4 + c] = jnp.where(used, both, 0.0)


def pick_slots(owner, acc):
    return pl.pallas_call(
        slots_kernel,
        in_specs=[
            pl.BlockSpec(memory_space=pltpu.SMEM),
            pl.BlockSpec(memory_space=pltpu.VMEM),
        ],
        out_specs=pl.BlockSpec(memory_space=pltpu.VMEM),
        out_shape=pltpu.VMEM((LON_BLOCKS // 2, 6, ROWS, LANES), F32),
        scratch_shapes=[
            pltpu.SMEM((LON_BLOCKS,), jnp.int32),
            pltpu.SMEM((LON_BLOCKS // 2,), jnp.int32),
        ],
        compiler_params=pltpu.CompilerParams(vmem_limit_bytes=LIMIT),
        name="slots",
    )(owner, acc)


def row_metric(row_pos, lat_total):
    latitude = (row_pos.astype(F32) - lat_total / 2 + 0.5) * GRID_STEP
    edge_lat = (lat_total / 2 - 0.5) * GRID_STEP
    return jnp.cos(jnp.asarray(edge_lat, F32)) / jnp.cos(latitude)


def shards(spectrum, sea_mask, ice_mask, friction, wind_dir, ocean_owner):
    count = lax.axis_size("tiles")
    first_row = lax.axis_index("tiles") * ROWS
    up_pairs = [(i, i + 1) for i in range(count - 1)]
    dn_pairs = [(i + 1, i) for i in range(count - 1)]
    spectral = spectrum.reshape(NF, NDIR, ROWS, NLON)
    spectral = pltpu.with_memory_space_constraint(spectral, pltpu.HBM)

    up1, dn1 = pack(spectral, sea_mask, 0, G1, 2, True)
    sea_later, _, _ = lax.optimization_barrier((sea_mask, up1, dn1))
    up1 = lax.ppermute(up1, "tiles", up_pairs)
    dn1 = lax.ppermute(dn1, "tiles", dn_pairs)
    up2, dn2 = pack(spectral, sea_later, G1, G2, G2, False)
    up2 = lax.ppermute(up2, "tiles", up_pairs)
    dn2 = lax.ppermute(dn2, "tiles", dn_pairs)

    freq_pos = (lax.axis_index("bins") * NF + jnp.arange(NF)).astype(F32)
    speed_ratio = jnp.power(1.1, -freq_pos)
    freq_weight = jnp.power(1.03, freq_pos - (NFREQ - 1))
    angles = (jnp.arange(NDIR).astype(F32) + 0.5) * (2.0 * math.pi / NDIR)
    cos_dir = jnp.cos(angles)
    sin_dir = jnp.sin(angles)
    courant = (COURANT_MAX * speed_ratio)[:, None]
    table = jnp.concatenate(
        [
            (courant * jnp.abs(cos_dir)).reshape(-1),
            (courant * jnp.abs(sin_dir)).reshape(-1),
            cos_dir,
            sin_dir,
            freq_weight,
        ]
    )
    sub = jnp.arange(ROWS)
    part = sub % 4
    rows = [sub]
    keep = [jnp.ones_like(sub)]
    for k in range(1, STEPS + 1):
        rows.append(part - 4 + k)
        keep.append(part < 3)
    for k in range(1, STEPS + 1):
        rows.append(part + ROWS - k)
        keep.append(part > 0)
    metric = row_metric(first_row + jnp.stack(rows), ROWS * count)
    metric = metric * jnp.stack(keep).astype(F32)
    metric = jnp.broadcast_to(metric[:, :, None], (1 + 2 * STEPS, ROWS, LANES))

    own, mask, wind = own_rows(
        spectral, table, metric, sea_mask, ice_mask, friction, wind_dir
    )
    out, acc, windows = finish(
        table, metric, mask, wind, own, up1, dn1, None, None, 0, PER_STEP
    )
    out, acc = finish(table, metric, windows, wind, own, up2, dn2, acc, out, G1, 1)

    sent = pick_slots(ocean_owner, acc)
    got = lax.all_to_all(sent, "bins", 0, 0, tiled=True)
    total = got.sum(0)
    rest = total[4:].reshape(2, ROWS, 2, LANES // 2).transpose(0, 2, 1, 3)
    rest = rest.reshape(4, ROWS, LANES // 2)[:, :, : 2 * BLK - LANES]
    fields = jnp.concatenate([total[:4], rest], axis=2).reshape(4, ROWS, 2, BLK)
    return out.reshape(spectrum.shape), fields[:2], fields[2:]


def solution(mesh):
    field = P("tiles", None)
    blocks = P(None, "tiles", "bins", None)
    whole = P("bins", "tiles", None)
    return jax.shard_map(
        shards,
        mesh=mesh,
        in_specs=(whole, field, field, field, field, field),
        out_specs=(whole, blocks, blocks),
        check_vma=False,
    )
```

time: 94 us -> 73.4 us (0.78)
  local copies, waits for them, and re-layouts: 18.6 us -> 2.69 us
  other arithmetic: 3.92 us -> 0.3 us
  Pallas kernels: 42 us -> 40.8 us
    unnamed x20 -> x12, local copies, waits for them, and re-layouts: 12.8 us -> 0.83 us
    concatenate x3 -> x0, local copies, waits for them, and re-layouts: 3.05 us -> none  [with_wrap(): jnp.concatenate([field, field[:, :side], field[:, NLON - side:]], axis=1)]
    concatenate x3 -> x1, other arithmetic: 1.36 us -> 0.01 us  [the longest x1 0.68 us: shards(): south = jnp.concatenate([sea[:4], edge_mask(up1)], axis=0)]
    sort x1 -> x0, other arithmetic: 1.25 us -> none  [shards(): order = jnp.argsort(ocean_owner[0], stable=True).astype(jnp.int32)]
    pallas_call x5, Pallas kernels: 40.9 us -> 39.8 us  [the longest x2 17.2 us: finish(): pl.pallas_call(kernel, grid=(2 * steps,), in_specs=in_specs, out_specs=ou...]
    another operation x3 -> x0, other arithmetic: 1.03 us -> none  [the longest x1 0.83 us: shards(): masks = jnp.stack([as_tiles(with_wrap(south)), as_tiles(with_wrap(north))])]
    slice x5 -> x1, local copies, waits for them, and re-layouts: 1.04 us -> 0.07 us  [the longest x1 0.88 us: shards(): south = jnp.concatenate([sea[:4], edge_mask(up1)], axis=0)]
  transfers between devices with their start and end apart: 4 -> 4, of which waited for: 0 -> 0; matrix products, arithmetic and copies ran while one was open for 9% -> 1% of each run, Pallas kernels for 36% -> 41%
where the time goes in v3:
time: 73.4 us; the launch traced here: 72.9 us
  Pallas kernels  40.8 us (56%)
  blocking collectives  15.2 us (21%)
  starting transfers between devices  13 us (18%)
  local copies, waits for them, and re-layouts  2.69 us (4%)
  between operations  0.84 us (1%)
    pallas_call x2, Pallas kernels, finish(): pl.pallas_call(kernel, grid=(2 * steps,), in_specs=in_specs, out_specs=ou...  17.2 us
    pallas_call x1, Pallas kernels, own_rows(): pl.pallas_call(own_kernel, grid=(2 * GROUPS // PER_STEP,), in_specs=[pl.B...  16.9 us
    all_to_all x1, blocking collectives, shards(): got = lax.all_to_all(sent, 'bins', 0, 0, tiled=True)  15.2 us
    pallas_call x2, Pallas kernels, pack(): pl.pallas_call(lambda *refs: pack_kernel(width, with_mask, *refs), grid=(...  5.69 us
    ppermute x1, starting transfers between devices, shards(): dn1 = lax.ppermute(dn1, 'tiles', dn_pairs)  4.67 us
    ppermute x1, starting transfers between devices, shards(): dn2 = lax.ppermute(dn2, 'tiles', dn_pairs)  4.54 us
    ppermute x1, starting transfers between devices, shards(): up1 = lax.ppermute(up1, 'tiles', up_pairs)  1.92 us
    ppermute x1, starting transfers between devices, shards(): up2 = lax.ppermute(up2, 'tiles', up_pairs)  1.91 us
  transfers between devices with their start and end apart: 4, of which 0 were waited for; matrix products, arithmetic and copies ran while one was open for 1% of the time, Pallas kernels for 41%

profile of v3, /device:TPU:32, one launch (start us, length us, event | category | flops | bytes accessed | tf_op | source)
XLA Modules:
  0.0 72.9 jit_solution(630719802008795546)
XLA Ops:
  0.6 0.0 copy-start
  0.6 0.8 %copy-done = s32[8,1440]{1,0:T(8,128)S(1)} copy-done((s32[8,1440]{1,0:T(8,128)S(1)}, s32[8,1440]{1,0:T(8,128)}, u32[]{:S(2)}) %copy-start) | copy-done | bytes 46104
  1.4 3.1 %pack0.1 = (f32[6,46,8,128]{3,2,1,0:T(8,128)S(1)}, f32[6,46,8,128]{3,2,1,0:T(8,128)S(1)}) custom-call(f32[4,36,8,1440]{3,2,1,0:T(8,128)} %bitcast.4, f32[4,36,8,1440]{3,2,1,0:T(8,128)} %bitcast.5, s32[8,1440]{1,0:T(8,128)S(1)} %copy-done), custom_call_target="tpu_custom_call" | custom-call | tf_op jit(solution)/shard_map/pack0/pallas_call | solution.py:89
  4.5 1.9 %collective-permute-start = (f32[6,46,8,128]{3,2,1,0:T(8,128)S(1)}, f32[6,46,8,128]{3,2,1,0:T(8,128)}, u32[]{:S(2)}, u32[]{:S(2)}) collective-permute-start(f32[6,46,8,128]{3,2,1,0:T(8,128)S(1)} %get-tuple-element.19), channel_id=1, source_target_pairs={{0,1},{1,2},{2,3},{3,4},{4,5},{5,6},{6,7},{7,8},{8,9},{9,10},{10,1... | collective-permute-start | bytes 3391496 | tf_op jit(solution)/shard_map/ppermute | solution.py:547
  6.5 0.0 copy-start.1
  6.5 0.0 copy-start.2
  6.5 4.7 %collective-permute-start.1 = (f32[6,46,8,128]{3,2,1,0:T(8,128)S(1)}, f32[6,46,8,128]{3,2,1,0:T(8,128)}, u32[]{:S(2)}, u32[]{:S(2)}) collective-permute-start(f32[6,46,8,128]{3,2,1,0:T(8,128)S(1)} %get-tuple-element.20), channel_id=1, source_target_pairs={{1,0},{2,1},{3,2},{4,3},{5,4},{6,5},{7,6},{8,7},{9,8},{10,9},{11,1... | collective-permute-start | bytes 3391496 | tf_op jit(solution)/shard_map/ppermute | solution.py:548
  11.2 2.6 %pack6.1 = (f32[3,45,8,128]{3,2,1,0:T(8,128)}, f32[3,45,8,128]{3,2,1,0:T(8,128)S(1)}) custom-call(f32[4,36,8,1440]{3,2,1,0:T(8,128)} %bitcast.6, f32[4,36,8,1440]{3,2,1,0:T(8,128)} %bitcast.7, s32[8,1440]{1,0:T(8,128)S(1)} %copy-done), custom_call_target="tpu_custom_call" | custom-call | tf_op jit(solution)/shard_map/pack6/pallas_call | solution.py:89
  13.8 1.9 %collective-permute-start.2 = (f32[3,45,8,128]{3,2,1,0:T(8,128)}, f32[3,45,8,128]{3,2,1,0:T(8,128)}, u32[]{:S(2)}, u32[]{:S(2)}) collective-permute-start(f32[3,45,8,128]{3,2,1,0:T(8,128)} %get-tuple-element.23), channel_id=1, source_target_pairs={{0,1},{1,2},{2,3},{3,4},{4,5},{5,6},{6,7},{7,8},{8,9},{9,10},{10,1... | collective-permute-start | bytes 1658888 | tf_op jit(solution)/shard_map/ppermute | solution.py:550
  15.7 4.5 %collective-permute-start.3 = (f32[3,45,8,128]{3,2,1,0:T(8,128)S(1)}, f32[3,45,8,128]{3,2,1,0:T(8,128)}, u32[]{:S(2)}, u32[]{:S(2)}) collective-permute-start(f32[3,45,8,128]{3,2,1,0:T(8,128)S(1)} %get-tuple-element.24), channel_id=1, source_target_pairs={{1,0},{2,1},{3,2},{4,3},{5,4},{6,5},{7,6},{8,7},{9,8},{10,9},{11,1... | collective-permute-start | bytes 1658888 | tf_op jit(solution)/shard_map/ppermute | solution.py:551
  20.3 0.1 broadcast_multiply_fusion
  20.4 0.1 mul.91
  20.5 0.1 mul.88
  20.7 0.1 concatenate.17.tab_ref.r_0_
  20.8 0.1 convert_multiply_fusion
  20.9 0.1 broadcast_in_dim.2.met_ref.r_1_
  21.0 16.9 %own.1 = (f32[18,2,4,12,8,128]{5,4,3,2,1,0:T(8,128)S(1)}, f32[12,8,128]{2,1,0:T(8,128)S(1)}, f32[3,12,8,128]{3,2,1,0:T(8,128)S(1)}) custom-call(f32[364]{0:T(512)S(1)} %concatenate.17.tab_ref.r_0_, f32[9,8,128]{2,1,0:T(8,128)S(1)} %broadcast_in_dim.2.met_ref.r_1_, s32[8,1440]{1,0:T(8,128)S(1)} %copy-done.1, s32[8,1440]{1,0:T(8,128)S(1)} %copy-done.2, ...), custom_call_target="tpu_custom_call" | custom-call | tf_op jit(solution)/shard_map/own/pallas_call | solution.py:235
  38.0 10.6 %finish0.1 = (f32[4,36,8,1440]{3,2,1,0:T(8,128)}, f32[4,12,8,128]{3,2,1,0:T(8,128)S(1)}, f32[2,4,12,8,128]{4,3,2,1,0:T(8,128)S(1)}) custom-call(f32[364]{0:T(512)S(1)} %concatenate.17.tab_ref.r_0_, f32[9,8,128]{2,1,0:T(8,128)S(1)} %broadcast_in_dim.2.met_ref.r_1_, f32[12,8,128]{2,1,0:T(8,128)S(1)} %get-tuple-element.16.r_2_, ...), custom_call_target="tpu_custom_call" | custom-call | tf_op jit(solution)/shard_map/finish0/pallas_call | solution.py:468
  48.6 6.6 %finish6.1 = (f32[4,36,8,1440]{3,2,1,0:T(8,128)}, f32[4,12,8,128]{3,2,1,0:T(8,128)S(1)}) custom-call(f32[364]{0:T(512)S(1)} %concatenate.17.tab_ref.r_0_, f32[9,8,128]{2,1,0:T(8,128)S(1)} %broadcast_in_dim.2.met_ref.r_1_, f32[2,4,12,8,128]{4,3,2,1,0:T(8,128)S(1)} %get-tuple-element.21.r_2_, ...), custom_call_target="tpu_custom_call", output_to_operand_aliasing={{0}: (8, {})} | custom-call | tf_op jit(solution)/shard_map/finish6/pallas_call | solution.py:468
  55.2 1.0 %slots.1 = f32[8,6,8,128]{3,2,1,0:T(8,128)S(1)} custom-call(s32[1,16]{1,0:T(1,128)S(1)} %copy-done.5, f32[4,12,8,128]{3,2,1,0:T(8,128)S(1)} %get-tuple-element.28.acc_ref), custom_call_target="tpu_custom_call" | custom-call | tf_op jit(solution)/shard_map/slots/pallas_call | solution.py:514
  56.2 15.2 %all_to_all.5 = f32[8,6,8,128]{3,2,1,0:T(8,128)S(1)} all-to-all(f32[8,6,8,128]{3,2,1,0:T(8,128)S(1)} %slots.1), channel_id=1, replica_groups=mesh['bins'=8,'tiles'=16] {'bins'}, dimensions={0} | all-to-all | bytes 393216 | tf_op jit(solution)/shard_map/all_to_all | solution.py:592
  71.4 0.1 fusion.5
  71.5 0.7 slice.34
  72.2 0.7 slice.32
  (29 shorter events, 0.3 us)
Async XLA Ops:
  0.6 0.8 %copy-start = (s32[8,1440]{1,0:T(8,128)S(1)}, s32[8,1440]{1,0:T(8,128)}, u32[]{:S(2)}) copy-start(s32[8,1440]{1,0:T(8,128)} %refs_2_.2) | copy-start | bytes 138244
  4.5 33.4 %collective-permute-start = (f32[6,46,8,128]{3,2,1,0:T(8,128)S(1)}, f32[6,46,8,128]{3,2,1,0:T(8,128)}, u32[]{:S(2)}, u32[]{:S(2)}) collective-permute-start(f32[6,46,8,128]{3,2,1,0:T(8,128)S(1)} %get-tuple-element.19), channel_id=1, source_target_pairs={{0,1},{1,2},{2,3},{3,4},{4,5},{5,6},{6,7},{7,8},{8,9},{9,10},{10,1... | collective-permute-start | bytes 3391496 | tf_op jit(solution)/shard_map/ppermute | solution.py:547
  6.5 14.5 %copy-start.1 = (s32[8,1440]{1,0:T(8,128)S(1)}, s32[8,1440]{1,0:T(8,128)}, u32[]{:S(2)}) copy-start(s32[8,1440]{1,0:T(8,128)} %refs_2_.2) | copy-start | bytes 138244
  6.5 14.5 %copy-start.2 = (s32[8,1440]{1,0:T(8,128)S(1)}, s32[8,1440]{1,0:T(8,128)}, u32[]{:S(2)}) copy-start(s32[8,1440]{1,0:T(8,128)} %ice_ref.1) | copy-start | bytes 138244
  6.5 14.5 %copy-start.3 = (f32[8,1440]{1,0:T(8,128)S(1)}, f32[8,1440]{1,0:T(8,128)}, u32[]{:S(2)}) copy-start(f32[8,1440]{1,0:T(8,128)} %friction_ref.1) | copy-start | bytes 138244
  6.5 14.5 %copy-start.4 = (f32[8,1440]{1,0:T(8,128)S(1)}, f32[8,1440]{1,0:T(8,128)}, u32[]{:S(2)}) copy-start(f32[8,1440]{1,0:T(8,128)} %wind_ref.1) | copy-start | bytes 138244
  6.5 31.5 %collective-permute-start.1 = (f32[6,46,8,128]{3,2,1,0:T(8,128)S(1)}, f32[6,46,8,128]{3,2,1,0:T(8,128)}, u32[]{:S(2)}, u32[]{:S(2)}) collective-permute-start(f32[6,46,8,128]{3,2,1,0:T(8,128)S(1)} %get-tuple-element.20), channel_id=1, source_target_pairs={{1,0},{2,1},{3,2},{4,3},{5,4},{6,5},{7,6},{8,7},{9,8},{10,9},{11,1... | collective-permute-start | bytes 3391496 | tf_op jit(solution)/shard_map/ppermute | solution.py:548
  13.8 34.8 %collective-permute-start.2 = (f32[3,45,8,128]{3,2,1,0:T(8,128)}, f32[3,45,8,128]{3,2,1,0:T(8,128)}, u32[]{:S(2)}, u32[]{:S(2)}) collective-permute-start(f32[3,45,8,128]{3,2,1,0:T(8,128)} %get-tuple-element.23), channel_id=1, source_target_pairs={{0,1},{1,2},{2,3},{3,4},{4,5},{5,6},{6,7},{7,8},{8,9},{9,10},{10,1... | collective-permute-start | bytes 1658888 | tf_op jit(solution)/shard_map/ppermute | solution.py:550
  15.7 32.9 %collective-permute-start.3 = (f32[3,45,8,128]{3,2,1,0:T(8,128)S(1)}, f32[3,45,8,128]{3,2,1,0:T(8,128)}, u32[]{:S(2)}, u32[]{:S(2)}) collective-permute-start(f32[3,45,8,128]{3,2,1,0:T(8,128)S(1)} %get-tuple-element.24), channel_id=1, source_target_pairs={{1,0},{2,1},{3,2},{4,3},{5,4},{6,5},{7,6},{8,7},{9,8},{10,9},{11,1... | collective-permute-start | bytes 1658888 | tf_op jit(solution)/shard_map/ppermute | solution.py:551
  48.6 6.6 %copy-start.5 = (s32[1,16]{1,0:T(1,128)S(1)}, s32[1,16]{1,0:T(1,128)}, u32[]{:S(2)}) copy-start(s32[1,16]{1,0:T(1,128)} %owner_ref.1) | copy-start | bytes 196

commit v4 on v3

v4 whole, which is shorter than its diff:
```python
import math

import jax
import jax.numpy as jnp
import numpy as np
from jax import lax
from jax.experimental import pallas as pl
from jax.experimental.pallas import tpu as pltpu
from jax.sharding import PartitionSpec as P

NDIR = 36
NFREQ = 32
LON_BLOCKS = 16
STEPS = 4
COURANT_MAX = 0.6
GRID_STEP = 0.25 * math.pi / 180.0

ROWS = 8
NLON = 1440
BLK = 90
LANES = 128
TILES = 12
TAIL = NLON - (TILES - 1) * LANES
NF = 4
GROUPS = 9
G1 = 6
G2 = GROUPS - G1
TPG = NF * (TILES - 1) + 1

F32 = jnp.float32
PER_STEP = 2
LIMIT = 16 << 20
ANGLES = (np.arange(NDIR, dtype=np.float32) + 0.5) * np.float32(2.0 * math.pi / NDIR)
TRIG = np.concatenate([np.cos(ANGLES), np.sin(ANGLES)]).astype(np.float32)


def lane_iota():
    return lax.broadcasted_iota(jnp.int32, (ROWS, LANES), 1)


def sub_iota():
    return lax.broadcasted_iota(jnp.int32, (ROWS, LANES), 0)


def pack_group(src_ref, local, mask_ref, out_ref, group, upward, lane, low):
    def pair(j, i):
        cols = pl.ds(i * LANES, LANES)
        mask = mask_ref[:, cols].astype(F32)
        first = src_ref[j, 2 * local, :, cols] * mask
        second = src_ref[j, 2 * local + 1, :, cols] * mask
        if upward:
            return jnp.where(low, pltpu.roll(first, 4, 0), second)
        return jnp.where(low, first, pltpu.roll(second, 4, 0))

    for i in range(TILES - 1):
        for j in range(NF):
            out_ref[group, j * (TILES - 1) + i] = pair(j, i)
    tail = pair(0, TILES - 1)
    for j in range(1, NF):
        moved = pltpu.roll(pair(j, TILES - 1), TAIL * j, 1)
        tail = jnp.where(lane >= TAIL * j, moved, tail)
    out_ref[group, TPG - 1] = tail


def pack_kernel(base, width, with_mask, up_ref, src_ref, mask_ref, out_ref):
    lane = lane_iota()
    low = sub_iota() < 4
    upward = up_ref[0] == 1

    def fill(is_up):
        for u in range(width):
            g = pl.program_id(0) * width + u
            local = u if is_up else width - 1 - u
            pack_group(src_ref, local, mask_ref, out_ref, g, is_up, lane, low)
            if with_mask:
                start = jnp.minimum(g, TILES // 2 - 1) * (2 * LANES)
                start = pl.multiple_of(start, 2 * LANES)
                first = mask_ref[:, pl.ds(start, LANES)].astype(F32)
                second = mask_ref[:, pl.ds(start + LANES, LANES)].astype(F32)
                if is_up:
                    first = pltpu.roll(first, 4, 0)
                else:
                    second = pltpu.roll(second, 4, 0)
                out_ref[g, TPG] = jnp.where(low, first, second)

    pl.when(upward)(lambda: fill(True))
    pl.when(jnp.logical_not(upward))(lambda: fill(False))


def block_of(base, width, step, south):
    last = (2 * GROUPS - base) // width - 1
    return jnp.where(south == 1, base // width + step, last - step)


def pack(upward, spectral, sea_mask, base, groups, width, with_mask, name):
    tiles = TPG + 1 if with_mask else TPG
    block = (NF, 2 * width, ROWS, TILES * LANES)
    return pl.pallas_call(
        lambda *refs: pack_kernel(base, width, with_mask, *refs),
        grid_spec=pltpu.PrefetchScalarGridSpec(
            num_scalar_prefetch=1,
            grid=(groups // width,),
            in_specs=[
                pl.BlockSpec(
                    block, lambda g, up: (0, block_of(base, width, g, up[0]), 0, 0)
                ),
                pl.BlockSpec((ROWS, TILES * LANES), lambda g, up: (0, 0)),
            ],
            out_specs=pl.BlockSpec(memory_space=pltpu.VMEM),
        ),
        out_shape=pltpu.VMEM((groups, tiles, ROWS, LANES), F32),
        compiler_params=pltpu.CompilerParams(vmem_limit_bytes=LIMIT),
        name=name,
    )(upward, spectral, sea_mask)


WEST, EAST, BOTH = 0, 1, 2


def fill_wrap(tiles, lane):
    last = tiles[-1]
    after = pltpu.roll(tiles[0], TAIL, 1)
    before = pltpu.roll(last, LANES - TAIL, 1)
    filled = jnp.where(lane < LANES - TAIL, after, before)
    return tiles[:-1] + [jnp.where(lane < TAIL, last, filled)]


def shift_lanes(tiles, west, lane):
    if west:
        moved = [pltpu.roll(t, 1, 1) for t in tiles]
        return [jnp.where(lane == 0, moved[i - 1], moved[i]) for i in range(TILES)]
    moved = [pltpu.roll(t, LANES - 1, 1) for t in tiles]
    return [
        jnp.where(lane == LANES - 1, moved[(i + 1) % TILES], moved[i])
        for i in range(TILES)
    ]


def x_side(direction):
    west = direction < NDIR // 4 or direction >= NDIR - NDIR // 4
    return WEST if west else EAST


def pair_side(dp):
    first, second = x_side(2 * dp), x_side(2 * dp + 1)
    return first if first == second else BOTH


def run_cases(index, values, south_below, side_of, body):
    found = {}
    for v in values:
        found.setdefault((v < south_below, side_of(v)), []).append(v)
    for (south, side), members in sorted(found.items()):
        cond = index == members[0]
        for m in members[1:]:
            cond = jnp.logical_or(cond, index == m)
        pl.when(cond)(lambda south=south, side=side: body(south, side))


def load_tiles(ref):
    return [ref[:, pl.ds(i * LANES, LANES)].astype(F32) for i in range(TILES)]


def fill_metric(first_row, lat_total, out_ref):
    sub = sub_iota()
    part = sub % 4
    rows = [(sub, sub >= 0)]
    rows += [(part - 4 + k, part < 3) for k in range(1, STEPS + 1)]
    rows += [(part + ROWS - k, part > 0) for k in range(1, STEPS + 1)]
    edge = math.cos((lat_total / 2 - 0.5) * GRID_STEP)
    for n, (row, inside) in enumerate(rows):
        row = (first_row + row).astype(F32)
        latitude = (row - lat_total / 2 + 0.5) * GRID_STEP
        out_ref[n] = jnp.where(inside, edge / jnp.cos(latitude), 0.0)


def own_kernel(
    lat_total,
    tab_ref,
    trig_ref,
    row_ref,
    sea_ref,
    ice_ref,
    friction_ref,
    wind_ref,
    src_ref,
    out_ref,
    mask_ref,
    force_ref,
    met_ref,
):
    step = pl.program_id(0)
    lane = lane_iota()
    sub = sub_iota()

    @pl.when(step == 0)
    def _():
        sea = fill_wrap(load_tiles(sea_ref), lane)
        ice = load_tiles(ice_ref)
        friction = load_tiles(friction_ref)
        wind = load_tiles(wind_ref)
        for i in range(TILES):
            strength = 0.5 * friction[i] * friction[i]
            mask_ref[i] = sea[i]
            force_ref[0, i] = strength * jnp.cos(wind[i])
            force_ref[1, i] = strength * jnp.sin(wind[i])
            force_ref[2, i] = 1.0 - 0.5 * ice[i]
        fill_metric(row_ref[0], lat_total, met_ref)

    def one(local, carry):
        direction = 2 * PER_STEP * step + local

        def body(south, side):
            west = side == WEST
            inflow = sub > 0 if south else sub < ROWS - 1
            fields = []
            coefs = []
            for j in range(NF):
                cy = tab_ref[j] * jnp.abs(trig_ref[NDIR + direction])
                cx = tab_ref[j] * jnp.abs(trig_ref[direction]) * met_ref[0]
                alpha = 1.0 - cx - cy
                coefs.append((alpha, cx, jnp.where(inflow, cy, 0.0)))
                tiles = [
                    src_ref[j, local, :, pl.ds(i * LANES, LANES)] for i in range(TILES)
                ]
                tiles = fill_wrap(tiles, lane)
                fields.append([t * mask_ref[i] for i, t in enumerate(tiles)])
            for sub_step in range(STEPS):
                new = []
                for tiles, (alpha, cx, cy) in zip(fields, coefs):
                    xs = shift_lanes(tiles, west, lane)
                    done = []
                    for i in range(TILES):
                        y = pltpu.roll(tiles[i], 1 if south else ROWS - 1, 0)
                        total = alpha * tiles[i] + cx * xs[i] + cy * y
                        done.append(total * mask_ref[i])
                    new.append(done)
                fields = new
            for j in range(NF):
                for i in range(TILES):
                    out_ref[local // 2, local % 2, j, i] = fields[j][i]

        run_cases(direction, range(NDIR), NDIR // 2, x_side, body)
        return carry

    lax.fori_loop(0, 2 * PER_STEP, one, 0)


def own_rows(
    spectral, table, trig, first_row, lat_total, sea_mask, ice_mask, friction, wind_dir
):
    whole = pl.BlockSpec(memory_space=pltpu.VMEM)
    field = pl.BlockSpec((ROWS, TILES * LANES), lambda i: (0, 0))
    return pl.pallas_call(
        lambda *refs: own_kernel(lat_total, *refs),
        grid=(2 * GROUPS // PER_STEP,),
        in_specs=[
            pl.BlockSpec(memory_space=pltpu.SMEM),
            pl.BlockSpec(memory_space=pltpu.SMEM),
            pl.BlockSpec(memory_space=pltpu.SMEM),
            field,
            field,
            field,
            field,
            pl.BlockSpec(
                (NF, 2 * PER_STEP, ROWS, TILES * LANES), lambda i: (0, i, 0, 0)
            ),
        ],
        out_specs=[
            pl.BlockSpec(
                (PER_STEP, 2, NF, TILES, ROWS, LANES), lambda i: (i, 0, 0, 0, 0, 0)
            ),
            whole,
            whole,
            whole,
        ],
        out_shape=[
            jax.ShapeDtypeStruct((2 * GROUPS, 2, NF, TILES, ROWS, LANES), F32),
            pltpu.VMEM((TILES, ROWS, LANES), F32),
            pltpu.VMEM((3, TILES, ROWS, LANES), F32),
            pltpu.VMEM((1 + 2 * STEPS, ROWS, LANES), F32),
        ],
        compiler_params=pltpu.CompilerParams(vmem_limit_bytes=LIMIT),
        name="own",
    )(table, trig, first_row, sea_mask, ice_mask, friction, wind_dir, spectral)


def window_masks(south, mask_ref, halo_ref, out_ref, lane, low):
    rows = []
    for i in range(TILES):
        edge = halo_ref[i // 2, 0]
        if (i % 2 == 0) != south:
            edge = pltpu.roll(edge, 4, 0)
        mine = pltpu.roll(mask_ref[i], 4, 0)
        if south:
            rows.append(jnp.where(low, edge, mine))
        else:
            rows.append(jnp.where(low, mine, edge))
    rows = fill_wrap(rows, lane)
    for k in range(1, STEPS + 1):
        first = k if south else 4 - k
        for i in range(TILES):
            window = rows[i]
            if first > 0:
                window = pltpu.roll(window, ROWS - first, 0)
            out_ref[k - 1, i] = jnp.where(low, window, pltpu.roll(window, 4, 0))


def finish_kernel(
    base,
    groups,
    width,
    south_ref,
    tab_ref,
    trig_ref,
    met_ref,
    mask_ref,
    wind_ref,
    own_ref,
    halo_ref,
    edge_ref,
    prev_ref,
    old_ref,
    out_ref,
    acc_ref,
    win_ref,
    c_ref,
):
    step = pl.program_id(0)
    is_south = south_ref[0] == 1
    dps = [base + g for g in range(groups)]
    dps = dps + [2 * GROUPS - 1 - d for d in dps]
    lane = lane_iota()
    sub = sub_iota()
    low = sub < 4

    @pl.when(step == 0)
    def _():
        if prev_ref is None:
            acc_ref[...] = jnp.zeros_like(acc_ref)
        else:
            acc_ref[...] = prev_ref[...]

    if edge_ref is not None:
        for south in (True, False):
            mine = jnp.logical_and(step == 0, is_south == south)
            pl.when(mine)(
                lambda south=south: window_masks(
                    south, mask_ref, edge_ref, win_ref, lane, low
                )
            )

    windows = mask_ref if edge_ref is None else win_ref

    def one(u, carry):
        local = jnp.where(is_south, u, width - 1 - u)
        group = base + step * width + u
        dp = jnp.where(is_south, group, 2 * GROUPS - 1 - group)

        def contribution(south, side):
            row = 0 if south else 1
            fields = []
            scalars = []
            for j in range(NF):
                courant = tab_ref[j]
                bx = courant * jnp.abs(
                    jnp.where(low, trig_ref[2 * dp], trig_ref[2 * dp + 1])
                )
                cy = courant * jnp.abs(
                    jnp.where(low, trig_ref[NDIR + 2 * dp], trig_ref[NDIR + 2 * dp + 1])
                )
                inside = sub % 4 < 3 if south else sub % 4 > 0
                scalars.append((bx, cy, jnp.where(inside, 1.0 - cy, 0.0)))
                tiles = [halo_ref[u, j * (TILES - 1) + i] for i in range(TILES - 1)]
                last = halo_ref[u, TPG - 1]
                if j > 0:
                    last = pltpu.roll(last, LANES - TAIL * j, 1)
                fields.append(fill_wrap(tiles + [last], lane))
            for k in range(STEPS):
                new = []
                for tiles, (bx, cy, rest) in zip(fields, scalars):
                    cx = bx * met_ref[1 + row * STEPS + k]
                    alpha = rest - cx
                    ahead = [pltpu.roll(t, ROWS - 1 if south else 1, 0) for t in tiles]
                    if side == BOTH:
                        west = shift_lanes(ahead, True, lane)
                        east = shift_lanes(ahead, False, lane)
                        here = low if south else jnp.logical_not(low)
                        xs = [jnp.where(here, w, e) for w, e in zip(west, east)]
                    else:
                        xs = shift_lanes(ahead, side == WEST, lane)
                    new.append(
                        [
                            (alpha * ahead[i] + cx * xs[i] + cy * tiles[i])
                            * windows[k, i]
                            for i in range(TILES)
                        ]
                    )
                fields = new
            for j in range(NF):
                for i in range(TILES):
                    c_ref[j, i] = fields[j][i]

        run_cases(dp, dps, GROUPS, pair_side, contribution)

        def combine(south, side):
            weight = [tab_ref[NF + j] for j in range(NF)]
            angle = [
                (trig_ref[2 * dp + dd], trig_ref[NDIR + 2 * dp + dd]) for dd in range(2)
            ]
            target = low if south else jnp.logical_not(low)
            for first in range(0, TILES, 2):
                held = []
                for i in (first, first + 1):
                    held.append(
                        (
                            [wind_ref[n, i] for n in range(3)],
                            [c_ref[j, i] for j in range(NF)],
                            [acc_ref[n, i] for n in range(4)],
                            [
                                [own_ref[local, dd, j, i] for j in range(NF)]
                                for dd in range(2)
                            ],
                        )
                    )
                results = []
                for (east, north, ice), parts, total, own in held:
                    made = []
                    for dd in range(2):
                        cos_d, sin_d = angle[dd]
                        h = jnp.maximum(cos_d * east + sin_d * north, 0.0)
                        for j in range(NF):
                            c = parts[j]
                            if (dd == 0) != south:
                                c = pltpu.roll(c, 4, 0)
                            e = own[dd][j] + jnp.where(target, c, 0.0)
                            x = weight[j] * e
                            made.append((e + h * x) * ice)
                            y = weight[j] * x
                            sum_x = x if j == 0 else sum_x + x
                            sum_y = y if j == 0 else sum_y + y
                        source = h * sum_x
                        drift = ice * (sum_x + h * sum_y)
                        total = [
                            total[0] + cos_d * drift,
                            total[1] + sin_d * drift,
                            total[2] + cos_d * source,
                            total[3] + sin_d * source,
                        ]
                    results.append((made, total))
                for i, (made, total) in zip((first, first + 1), results):
                    cols = pl.ds(i * LANES, LANES)
                    for dd in range(2):
                        for j in range(NF):
                            out_ref[j, 2 * local + dd, :, cols] = made[dd * NF + j]
                    for n in range(4):
                        acc_ref[n, i] = total[n]

        run_cases(dp, dps, GROUPS, lambda d: WEST, combine)
        return carry

    lax.fori_loop(0, width, one, 0)


def in_vmem(x):
    return pltpu.with_memory_space_constraint(x, pltpu.VMEM)


def in_hbm(x):
    return pltpu.with_memory_space_constraint(x, pltpu.HBM)


def finish(south, table, trig, metric, mask, wind, own, halo, prev, old, base, width, name):
    groups, tiles = halo.shape[:2]
    whole = pl.BlockSpec(memory_space=pltpu.VMEM)
    block = lambda i, s: block_of(base, width, i, s[0])
    in_specs = [
        pl.BlockSpec(memory_space=pltpu.SMEM),
        pl.BlockSpec(memory_space=pltpu.SMEM),
        whole,
        whole,
        whole,
        pl.BlockSpec(
            (width, 2, NF, TILES, ROWS, LANES),
            lambda i, s: (block(i, s), 0, 0, 0, 0, 0),
        ),
        pl.BlockSpec((width, tiles, ROWS, LANES), lambda i, s: (i, 0, 0, 0)),
    ]
    halo = in_hbm(halo)
    args = [south, table, trig, in_vmem(metric), in_vmem(mask), in_vmem(wind)]
    args += [own, halo]
    out_specs = [
        pl.BlockSpec(
            (NF, 2 * width, ROWS, TILES * LANES), lambda i, s: (0, block(i, s), 0, 0)
        ),
        whole,
    ]
    out_shape = [
        jax.ShapeDtypeStruct((NF, NDIR, ROWS, NLON), F32),
        pltpu.VMEM((4, TILES, ROWS, LANES), F32),
    ]
    with_edge = tiles > TPG
    with_prev = prev is not None
    aliases = {}
    if with_edge:
        in_specs.append(
            pl.BlockSpec((TILES // 2, 1, ROWS, LANES), lambda i, s: (0, TPG, 0, 0))
        )
        args.append(halo)
        out_specs.append(whole)
        out_shape.append(pltpu.VMEM((STEPS, TILES, ROWS, LANES), F32))
    if with_prev:
        in_specs += [whole, pl.BlockSpec(memory_space=pl.ANY)]
        args += [in_vmem(prev), old]
        aliases = {len(args) - 1: 0}

    def kernel(*refs):
        refs = list(refs)
        fixed, refs = refs[:8], refs[8:]
        edge = refs.pop(0) if with_edge else None
        before = refs.pop(0) if with_prev else None
        former = refs.pop(0) if with_prev else None
        result, acc = refs.pop(0), refs.pop(0)
        windows = refs.pop(0) if with_edge else None
        finish_kernel(
            base,
            groups,
            width,
            *fixed,
            edge,
            before,
            former,
            result,
            acc,
            windows,
            *refs,
        )

    return pl.pallas_call(
        kernel,
        grid_spec=pltpu.PrefetchScalarGridSpec(
            num_scalar_prefetch=1,
            grid=(groups // width,),
            in_specs=in_specs,
            out_specs=out_specs,
            scratch_shapes=[pltpu.VMEM((NF, TILES, ROWS, LANES), F32)],
        ),
        out_shape=out_shape,
        input_output_aliases=aliases,
        compiler_params=pltpu.CompilerParams(vmem_limit_bytes=LIMIT),
        name=name,
    )(*args)


def slots_kernel(owner_ref, acc_ref, out_ref, order_ref, count_ref):
    lane = lane_iota()
    for k in range(LON_BLOCKS // 2):
        count_ref[k] = 0
    for block in range(LON_BLOCKS):
        owner = owner_ref[0, block]
        seen = count_ref[owner]
        order_ref[2 * owner + seen] = block
        count_ref[owner] = seen + 1

    for k in range(LON_BLOCKS // 2):
        rests = []
        for c in range(4):
            parts = []
            for s in range(2):
                column = order_ref[2 * k + s] * BLK
                tile = column // LANES
                shift = column % LANES
                back = (LANES - shift) % LANES
                here = pltpu.roll(acc_ref[c, tile], back, 1)
                after = pltpu.roll(acc_ref[c, jnp.minimum(tile + 1, TILES - 1)], back, 1)
                parts.append(jnp.where(lane < LANES - shift, here, after))
            moved = pltpu.roll(parts[1], BLK, 1)
            out_ref[k, c] = jnp.where(lane < BLK, parts[0], moved)
            rests.append(moved)
        for c in range(2):
            other = pltpu.roll(rests[2 * c + 1], LANES // 2, 1)
            both = jnp.where(lane < LANES // 2, rests[2 * c], other)
            used = lane % (LANES // 2) < 2 * BLK - LANES
            out_ref[k, 4 + c] = jnp.where(used, both, 0.0)


def pick_slots(owner, acc):
    return pl.pallas_call(
        slots_kernel,
        in_specs=[
            pl.BlockSpec(memory_space=pltpu.SMEM),
            pl.BlockSpec(memory_space=pltpu.VMEM),
        ],
        out_specs=pl.BlockSpec(memory_space=pltpu.VMEM),
        out_shape=pltpu.VMEM((LON_BLOCKS // 2, 6, ROWS, LANES), F32),
        scratch_shapes=[
            pltpu.SMEM((LON_BLOCKS,), jnp.int32),
            pltpu.SMEM((LON_BLOCKS // 2,), jnp.int32),
        ],
        compiler_params=pltpu.CompilerParams(vmem_limit_bytes=LIMIT),
        name="slots",
    )(owner, acc)


def shards(spectrum, sea_mask, ice_mask, friction, wind_dir, ocean_owner):
    count = lax.axis_size("tiles")
    first_row = (lax.axis_index("tiles") * ROWS).astype(jnp.int32).reshape(1)
    spectral = in_hbm(spectrum.reshape(NF, NDIR, ROWS, NLON))
    sea = in_hbm(sea_mask)
    odd = lax.axis_index("tiles") % 2
    odd = odd.astype(jnp.int32).reshape(1)
    even = 1 - odd

    def swap(x, start):
        pairs = [(i, i + 1) for i in range(start, count - 1, 2)]
        return lax.ppermute(x, "tiles", pairs + [(j, i) for i, j in pairs])

    far1 = pack(odd, spectral, sea, 0, G1, 2, True, "far1")
    sea, _ = lax.optimization_barrier((sea, far1))
    far1 = swap(far1, 1)
    near = pack(even, spectral, sea, 0, GROUPS, 3, True, "near")
    sea, _ = lax.optimization_barrier((sea, near))
    near = swap(near, 0)
    far2 = pack(odd, spectral, sea, G1, G2, G2, False, "far2")
    far2 = swap(far2, 1)

    place = np.tile(np.arange(NF), 2)
    speeds = np.arange(2 * NF) < NF
    freq_pos = (lax.axis_index("bins") * NF + place).astype(F32)
    power = jnp.where(speeds, -freq_pos, freq_pos - (NFREQ - 1))
    table = jnp.power(jnp.where(speeds, 1.1, 1.03).astype(F32), power)
    table = table * jnp.where(speeds, COURANT_MAX, 1.0).astype(F32)
    trig = jnp.asarray(TRIG)

    own, mask, wind, metric = own_rows(
        spectral,
        table,
        trig,
        first_row,
        count * ROWS,
        sea,
        ice_mask,
        friction,
        wind_dir,
    )
    common = (table, trig, metric)
    out, acc, windows = finish(
        even, *common, mask, wind, own, far1, None, None, 0, 2, "finish_far1"
    )
    out, acc, _ = finish(
        odd, *common, mask, wind, own, near, acc, out, 0, 3, "finish_near"
    )
    out, acc = finish(
        even, *common, windows, wind, own, far2, acc, out, G1, 1, "finish_far2"
    )

    sent = pick_slots(ocean_owner, acc)
    got = lax.all_to_all(sent, "bins", 0, 0, tiled=True)
    total = got.sum(0)
    rest = total[4:].reshape(2, ROWS, 2, LANES // 2).transpose(0, 2, 1, 3)
    rest = rest.reshape(4, ROWS, LANES // 2)[:, :, : 2 * BLK - LANES]
    fields = jnp.concatenate([total[:4], rest], axis=2).reshape(4, ROWS, 2, BLK)
    return out.reshape(spectrum.shape), fields[:2], fields[2:]


def solution(mesh):
    field = P("tiles", None)
    blocks = P(None, "tiles", "bins", None)
    whole = P("bins", "tiles", None)
    return jax.shard_map(
        shards,
        mesh=mesh,
        in_specs=(whole, field, field, field, field, field),
        out_specs=(whole, blocks, blocks),
        check_vma=False,
    )
```

time: 73.4 us -> 73.1 us (level)
  starting transfers between devices: 13 us -> 6.55 us
  waiting for transfers between devices: 0.01 us -> 4.99 us
  Pallas kernels: 40.8 us -> 43.6 us
  local copies, waits for them, and re-layouts: 2.69 us -> 1.51 us
    ppermute x4 -> x3, starting transfers between devices: 13 us -> 6.55 us  [swap(): return lax.ppermute(x, 'tiles', pairs + [(j, i) for i, j in pairs])]
    ppermute x4 -> x3, waiting for transfers between devices: 0.01 us -> 4.99 us  [swap(): return lax.ppermute(x, 'tiles', pairs + [(j, i) for i, j in pairs])]
    pallas_call x5 -> x7, Pallas kernels: 39.8 us -> 42.6 us  [the longest x3 18.7 us: finish(): pl.pallas_call(kernel, grid_spec=pltpu.PrefetchScalarGridSpec(num_scalar_...]
    unnamed x12 -> x18, local copies, waits for them, and re-layouts: 0.83 us -> 0.06 us
  transfers between devices with their start and end apart: 4 -> 3, of which waited for: 0 -> 1; matrix products, arithmetic and copies ran while one was open for 1% -> 0% of each run, Pallas kernels for 41% -> 46%
where the time goes in v4:
time: 73.1 us; the launch traced here: 72.7 us
  Pallas kernels  43.6 us (60%)
  blocking collectives  15.1 us (21%)
  starting transfers between devices  6.55 us (9%)
  waiting for transfers between devices  4.99 us (7%)
  local copies, waits for them, and re-layouts  1.51 us (2%)
  between operations  0.87 us (1%)
    pallas_call x3, Pallas kernels, finish(): pl.pallas_call(kernel, grid_spec=pltpu.PrefetchScalarGridSpec(num_scalar_...  18.7 us
    pallas_call x1, Pallas kernels, own_rows(): pl.pallas_call(lambda *refs: own_kernel(lat_total, *refs), grid=(2 * GROU...  17.1 us
    all_to_all x1, blocking collectives, shards(): got = lax.all_to_all(sent, 'bins', 0, 0, tiled=True)  15.1 us
    pallas_call x3, Pallas kernels, pack(): pl.pallas_call(lambda *refs: pack_kernel(base, width, with_mask, *refs),...  6.76 us
    ppermute x3, starting transfers between devices, swap(): return lax.ppermute(x, 'tiles', pairs + [(j, i) for i, j in pairs])  6.55 us
    ppermute x3, waiting for transfers between devices, swap(): return lax.ppermute(x, 'tiles', pairs + [(j, i) for i, j in pairs])  4.99 us
  transfers between devices with their start and end apart: 3, of which 1 were waited for; matrix products, arithmetic and copies ran while one was open for 0% of the time, Pallas kernels for 46%

profile of v4, /device:TPU:32, one launch (start us, length us, event | category | flops | bytes accessed | tf_op | source)
XLA Modules:
  0.0 72.7 jit_solution(5308422698486222352)
XLA Ops:
  0.6 2.5 %far1.1 = f32[6,46,8,128]{3,2,1,0:T(8,128)S(1)} custom-call(s32[1]{0:T(128)} %bitcast.refs_0_, f32[4,36,8,1440]{3,2,1,0:T(8,128)} %bitcast.6, s32[8,1440]{1,0:T(8,128)} %refs_2_.6), custom_call_target="tpu_custom_call" | custom-call | tf_op jit(solution)/shard_map/far1/pallas_call | solution.py:98
  3.2 0.0 copy-start.5
  3.2 0.0 copy-start.6
  3.2 0.0 copy-start.7
  3.2 0.0 copy-start.8
  3.2 0.0 copy-start
  3.2 0.0 copy-start.1
  3.2 0.0 copy-start.3
  3.3 2.9 %near.1 = f32[9,46,8,128]{3,2,1,0:T(8,128)S(1)} custom-call(s32[1]{0:T(128)S(6)} %sub.6.refs_0_, f32[4,36,8,1440]{3,2,1,0:T(8,128)} %bitcast.7, s32[8,1440]{1,0:T(8,128)} %refs_2_.6), custom_call_target="tpu_custom_call" | custom-call | tf_op jit(solution)/shard_map/near/pallas_call | solution.py:98
  6.1 0.1 collective-permute-start.2
  6.2 3.0 %collective-permute-start = (f32[6,46,8,128]{3,2,1,0:T(8,128)S(1)}, f32[6,46,8,128]{3,2,1,0:T(8,128)}, u32[]{:S(2)}, u32[]{:S(2)}) collective-permute-start(f32[6,46,8,128]{3,2,1,0:T(8,128)S(1)} %far1.1), channel_id=1, source_target_pairs={{1,2},{3,4},{5,6},{7,8},{9,10},{11,12},{13,14},{2,1},{4,3},{6,5},{... | collective-permute-start | bytes 3391496 | tf_op jit(solution)/shard_map/ppermute | solution.py:616
  9.3 1.4 %far2.1 = f32[3,45,8,128]{3,2,1,0:T(8,128)S(1)} custom-call(s32[1]{0:T(128)} %bitcast.refs_0_, f32[4,36,8,1440]{3,2,1,0:T(8,128)} %bitcast.8, s32[8,1440]{1,0:T(8,128)} %refs_2_.6), custom_call_target="tpu_custom_call" | custom-call | tf_op jit(solution)/shard_map/far2/pallas_call | solution.py:98
  10.7 3.4 %collective-permute-start.1 = (f32[3,45,8,128]{3,2,1,0:T(8,128)S(1)}, f32[3,45,8,128]{3,2,1,0:T(8,128)}, u32[]{:S(2)}, u32[]{:S(2)}) collective-permute-start(f32[3,45,8,128]{3,2,1,0:T(8,128)S(1)} %far2.1), channel_id=1, source_target_pairs={{1,2},{3,4},{5,6},{7,8},{9,10},{11,12},{13,14},{2,1},{4,3},{6,5},{... | collective-permute-start | bytes 1658888 | tf_op jit(solution)/shard_map/ppermute | solution.py:616
  14.2 17.1 %own.1 = (f32[18,2,4,12,8,128]{5,4,3,2,1,0:T(8,128)S(1)}, f32[12,8,128]{2,1,0:T(8,128)S(1)}, f32[3,12,8,128]{3,2,1,0:T(8,128)S(1)}, f32[9,8,128]{2,1,0:T(8,128)S(1)}) custom-call(f32[8]{0:T(128)S(1)} %power_multiply_fusion.refs_0_.refs_1_, f32[72]{0:T(128)S(1)} %copy-done.3, s32[1]{0:T(128)} %bitcast.1.refs_2_, s32[8,1440]{1,0:T(8,128)} %refs_2_.6, ...), custom_call_target="tpu_custom_call" | custom-call | tf_op jit(solution)/shard_map/own/pallas_call | solution.py:254
  31.3 5.0 %collective-permute-done.refs_7_.refs_8_ = f32[6,46,8,128]{3,2,1,0:T(8,128)} collective-permute-done((f32[6,46,8,128]{3,2,1,0:T(8,128)S(1)}, f32[6,46,8,128]{3,2,1,0:T(8,128)}, u32[]{:S(2)}, u32[]{:S(2)}) %collective-permute-start) | collective-permute-done | bytes 1130528 | tf_op jit(solution)/shard_map/ppermute | solution.py:616
  36.3 6.2 %finish_far1.1 = (f32[4,36,8,1440]{3,2,1,0:T(8,128)}, f32[4,12,8,128]{3,2,1,0:T(8,128)S(1)}, f32[4,12,8,128]{3,2,1,0:T(8,128)S(1)}) custom-call(s32[1]{0:T(128)S(6)} %sub.6.refs_0_, f32[8]{0:T(128)S(1)} %power_multiply_fusion.refs_0_.refs_1_, f32[72]{0:T(128)S(1)} %copy-done.3, f32[9,8,128]{2,1,0:T(8,128)S(1)} %get-tuple-element.18.refs_3_, ...), custom_call_target="tpu_custom_call" | custom-call | tf_op jit(solution)/shard_map/finish_far1/pallas_call | solution.py:539
  42.5 8.5 %finish_near.1 = (f32[4,36,8,1440]{3,2,1,0:T(8,128)}, f32[4,12,8,128]{3,2,1,0:T(8,128)S(1)}, f32[4,12,8,128]{3,2,1,0:T(8,128)}) custom-call(s32[1]{0:T(128)} %bitcast.refs_0_, f32[8]{0:T(128)S(1)} %power_multiply_fusion.refs_0_.refs_1_, f32[72]{0:T(128)S(1)} %copy-done.3, ...), custom_call_target="tpu_custom_call", output_to_operand_aliasing={{0}: (10, {})} | custom-call | tf_op jit(solution)/shard_map/finish_near/pallas_call | solution.py:539
  51.0 0.0 copy-start.4
  51.0 4.1 %finish_far2.1 = (f32[4,36,8,1440]{3,2,1,0:T(8,128)}, f32[4,12,8,128]{3,2,1,0:T(8,128)S(1)}) custom-call(s32[1]{0:T(128)S(6)} %sub.6.refs_0_, f32[8]{0:T(128)S(1)} %power_multiply_fusion.refs_0_.refs_1_, f32[72]{0:T(128)S(1)} %copy-done.3, f32[9,8,128]{2,1,0:T(8,128)S(1)} %get-tuple-element.18.refs_3_, ...), custom_call_target="tpu_custom_call", output_to_operand_aliasing={{0}: (9, {})} | custom-call | tf_op jit(solution)/shard_map/finish_far2/pallas_call | solution.py:539
  55.1 1.0 %slots.1 = f32[8,6,8,128]{3,2,1,0:T(8,128)S(1)} custom-call(s32[1,16]{1,0:T(1,128)S(1)} %copy-done.4, f32[4,12,8,128]{3,2,1,0:T(8,128)S(1)} %get-tuple-element.28.acc_ref), custom_call_target="tpu_custom_call" | custom-call | tf_op jit(solution)/shard_map/slots/pallas_call | solution.py:588
  56.1 15.1 %all_to_all.5 = f32[8,6,8,128]{3,2,1,0:T(8,128)S(1)} all-to-all(f32[8,6,8,128]{3,2,1,0:T(8,128)S(1)} %slots.1), channel_id=1, replica_groups=mesh['bins'=8,'tiles'=16] {'bins'}, dimensions={0} | all-to-all | bytes 393216 | tf_op jit(solution)/shard_map/all_to_all | solution.py:658
  71.3 0.1 fusion.1
  71.4 0.7 slice.32
  72.1 0.7 slice.34
  (17 shorter events, 0.1 us)
Async XLA Ops:
  3.2 11.0 %copy-start.5 = (s32[8]{0:T(128)S(1)}, s32[8]{0:T(128)}, u32[]{:S(2)}) copy-start(s32[8]{0:T(128)} %constant.47.clone) | copy-start | bytes 100
  3.2 11.0 %copy-start.6 = (pred[8]{0:T(512)(128)(4,1)S(1)}, pred[8]{0:T(512)(128)(4,1)}, u32[]{:S(2)}) copy-start(pred[8]{0:T(512)(128)(4,1)} %constant.48.clone) | copy-start | bytes 28
  3.2 10.9 %copy-start.7 = (f32[8]{0:T(128)S(1)}, f32[8]{0:T(128)}, u32[]{:S(2)}) copy-start(f32[8]{0:T(128)} %constant.56) | copy-start | bytes 100
  3.2 10.9 %copy-start.8 = (f32[8]{0:T(128)S(1)}, f32[8]{0:T(128)}, u32[]{:S(2)}) copy-start(f32[8]{0:T(128)} %constant.57) | copy-start | bytes 100
  3.2 11.0 %copy-start = (s32[8,1440]{1,0:T(8,128)S(1)}, s32[8,1440]{1,0:T(8,128)}, u32[]{:S(2)}) copy-start(s32[8,1440]{1,0:T(8,128)} %refs_4_.1) | copy-start | bytes 138244
  3.2 11.0 %copy-start.1 = (f32[8,1440]{1,0:T(8,128)S(1)}, f32[8,1440]{1,0:T(8,128)}, u32[]{:S(2)}) copy-start(f32[8,1440]{1,0:T(8,128)} %refs_5_.1) | copy-start | bytes 138244
  3.2 11.0 %copy-start.2 = (f32[8,1440]{1,0:T(8,128)S(1)}, f32[8,1440]{1,0:T(8,128)}, u32[]{:S(2)}) copy-start(f32[8,1440]{1,0:T(8,128)} %refs_6_.1) | copy-start | bytes 138244
  3.2 11.0 %copy-start.3 = (f32[72]{0:T(128)S(1)}, f32[72]{0:T(128)}, u32[]{:S(2)}) copy-start(f32[72]{0:T(128)} %constant.49.clone.refs_1_.refs_2_) | copy-start | bytes 868
  6.1 36.3 %collective-permute-start.2 = (f32[9,46,8,128]{3,2,1,0:T(8,128)S(1)}, f32[9,46,8,128]{3,2,1,0:T(8,128)}, u32[]{:S(2)}, u32[]{:S(2)}) collective-permute-start(f32[9,46,8,128]{3,2,1,0:T(8,128)S(1)} %near.1), channel_id=1, source_target_pairs={{0,1},{2,3},{4,5},{6,7},{8,9},{10,11},{12,13},{14,15},{1,0},{3,2},... | collective-permute-start | bytes 5087240 | tf_op jit(solution)/shard_map/ppermute | solution.py:616
  6.2 30.1 %collective-permute-start = (f32[6,46,8,128]{3,2,1,0:T(8,128)S(1)}, f32[6,46,8,128]{3,2,1,0:T(8,128)}, u32[]{:S(2)}, u32[]{:S(2)}) collective-permute-start(f32[6,46,8,128]{3,2,1,0:T(8,128)S(1)} %far1.1), channel_id=1, source_target_pairs={{1,2},{3,4},{5,6},{7,8},{9,10},{11,12},{13,14},{2,1},{4,3},{6,5},{... | collective-permute-start | bytes 3391496 | tf_op jit(solution)/shard_map/ppermute | solution.py:616
  10.7 40.3 %collective-permute-start.1 = (f32[3,45,8,128]{3,2,1,0:T(8,128)S(1)}, f32[3,45,8,128]{3,2,1,0:T(8,128)}, u32[]{:S(2)}, u32[]{:S(2)}) collective-permute-start(f32[3,45,8,128]{3,2,1,0:T(8,128)S(1)} %far2.1), channel_id=1, source_target_pairs={{1,2},{3,4},{5,6},{7,8},{9,10},{11,12},{13,14},{2,1},{4,3},{6,5},{... | collective-permute-start | bytes 1658888 | tf_op jit(solution)/shard_map/ppermute | solution.py:616
  51.0 4.1 %copy-start.4 = (s32[1,16]{1,0:T(1,128)S(1)}, s32[1,16]{1,0:T(1,128)}, u32[]{:S(2)}) copy-start(s32[1,16]{1,0:T(1,128)} %owner_ref.1) | copy-start | bytes 196

commit v5 on v4

--- a/solution.py
+++ b/solution.py
@@ -23,7 +23,7 @@
 TAIL = NLON - (TILES - 1) * LANES
 NF = 4
 GROUPS = 9
-G1 = 6
+G1 = 7
 G2 = GROUPS - G1
 TPG = NF * (TILES - 1) + 1
 
@@ -615,13 +615,13 @@
         pairs = [(i, i + 1) for i in range(start, count - 1, 2)]
         return lax.ppermute(x, "tiles", pairs + [(j, i) for i, j in pairs])
 
-    far1 = pack(odd, spectral, sea, 0, G1, 2, True, "far1")
-    sea, _ = lax.optimization_barrier((sea, far1))
-    far1 = swap(far1, 1)
     near = pack(even, spectral, sea, 0, GROUPS, 3, True, "near")
     sea, _ = lax.optimization_barrier((sea, near))
     near = swap(near, 0)
-    far2 = pack(odd, spectral, sea, G1, G2, G2, False, "far2")
+    far1 = pack(odd, spectral, sea, 0, G1, 1, True, "far1")
+    sea, _ = lax.optimization_barrier((sea, far1))
+    far1 = swap(far1, 1)
+    far2 = pack(odd, spectral, sea, G1, G2, 1, False, "far2")
     far2 = swap(far2, 1)
 
     place = np.tile(np.arange(NF), 2)
@@ -644,11 +644,11 @@
         wind_dir,
     )
     common = (table, trig, metric)
+    out, acc, _ = finish(
+        odd, *common, mask, wind, own, near, None, None, 0, 3, "finish_near"
+    )
     out, acc, windows = finish(
-        even, *common, mask, wind, own, far1, None, None, 0, 2, "finish_far1"
-    )
-    out, acc, _ = finish(
-        odd, *common, mask, wind, own, near, acc, out, 0, 3, "finish_near"
+        even, *common, mask, wind, own, far1, acc, out, 0, 1, "finish_far1"
     )
     out, acc = finish(
         even, *common, windows, wind, own, far2, acc, out, G1, 1, "finish_far2"

time: 73.1 us -> 71.2 us (0.974)
  waiting for transfers between devices: 4.99 us -> 0.62 us
  Pallas kernels: 43.6 us -> 46 us
    ppermute x3, waiting for transfers between devices: 4.99 us -> 0.62 us  [swap(): return lax.ppermute(x, 'tiles', pairs + [(j, i) for i, j in pairs])]
    pallas_call x3, Pallas kernels: 6.76 us -> 8.49 us  [pack(): pl.pallas_call(lambda *refs: pack_kernel(base, width, with_mask, *refs),...]
  transfers between devices with their start and end apart: 3 -> 3, of which waited for: 1 -> 1; matrix products, arithmetic and copies ran while one was open for 0% -> 0% of each run, Pallas kernels for 46% -> 55%
where the time goes in v5:
time: 71.2 us; the launch traced here: 70.7 us
  Pallas kernels  46 us (65%)
  blocking collectives  15.2 us (21%)
  starting transfers between devices  6.53 us (9%)
  local copies, waits for them, and re-layouts  1.51 us (2%)
  between operations  0.85 us (1%)
    pallas_call x3, Pallas kernels, finish(): pl.pallas_call(kernel, grid_spec=pltpu.PrefetchScalarGridSpec(num_scalar_...  19.4 us
    pallas_call x1, Pallas kernels, own_rows(): pl.pallas_call(lambda *refs: own_kernel(lat_total, *refs), grid=(2 * GROU...  17.1 us
    all_to_all x1, blocking collectives, shards(): got = lax.all_to_all(sent, 'bins', 0, 0, tiled=True)  15.2 us
    pallas_call x3, Pallas kernels, pack(): pl.pallas_call(lambda *refs: pack_kernel(base, width, with_mask, *refs),...  8.49 us
    ppermute x3, starting transfers between devices, swap(): return lax.ppermute(x, 'tiles', pairs + [(j, i) for i, j in pairs])  6.53 us
  transfers between devices with their start and end apart: 3, of which 1 were waited for; matrix products, arithmetic and copies ran while one was open for 0% of the time, Pallas kernels for 55%

profile of v5, /device:TPU:32, one launch (start us, length us, event | category | flops | bytes accessed | tf_op | source)
XLA Modules:
  0.0 70.7 jit_solution(8720525182531787799)
XLA Ops:
  0.6 2.9 %near.1 = f32[9,46,8,128]{3,2,1,0:T(8,128)S(1)} custom-call(s32[1]{0:T(128)S(6)} %sub.6.refs_0_, f32[4,36,8,1440]{3,2,1,0:T(8,128)} %bitcast.6, s32[8,1440]{1,0:T(8,128)} %refs_2_.6), custom_call_target="tpu_custom_call" | custom-call | tf_op jit(solution)/shard_map/near/pallas_call | solution.py:98
  3.5 0.0 copy-start.5
  3.5 0.0 copy-start.6
  3.5 0.0 copy-start.7
  3.5 0.0 copy-start.8
  3.6 0.0 copy-start
  3.6 0.0 copy-start.1
  3.6 0.0 copy-start.2
  3.6 0.0 copy-start.3
  3.6 0.1 collective-permute-start.1
  3.7 4.4 %far1.1 = f32[7,46,8,128]{3,2,1,0:T(8,128)S(1)} custom-call(s32[1]{0:T(128)} %bitcast.refs_0_, f32[4,36,8,1440]{3,2,1,0:T(8,128)} %bitcast.7, s32[8,1440]{1,0:T(8,128)} %refs_2_.6), custom_call_target="tpu_custom_call" | custom-call | tf_op jit(solution)/shard_map/far1/pallas_call | solution.py:98
  8.1 3.0 %collective-permute-start = (f32[7,46,8,128]{3,2,1,0:T(8,128)S(1)}, f32[7,46,8,128]{3,2,1,0:T(8,128)}, u32[]{:S(2)}, u32[]{:S(2)}) collective-permute-start(f32[7,46,8,128]{3,2,1,0:T(8,128)S(1)} %far1.1), channel_id=1, source_target_pairs={{1,2},{3,4},{5,6},{7,8},{9,10},{11,12},{13,14},{2,1},{4,3},{6,5},{... | collective-permute-start | bytes 3956744 | tf_op jit(solution)/shard_map/ppermute | solution.py:616
  11.1 1.2 %far2.1 = f32[2,45,8,128]{3,2,1,0:T(8,128)S(1)} custom-call(s32[1]{0:T(128)} %bitcast.refs_0_, f32[4,36,8,1440]{3,2,1,0:T(8,128)} %bitcast.8, s32[8,1440]{1,0:T(8,128)} %refs_2_.6), custom_call_target="tpu_custom_call" | custom-call | tf_op jit(solution)/shard_map/far2/pallas_call | solution.py:98
  12.3 3.4 %collective-permute-start.2 = (f32[2,45,8,128]{3,2,1,0:T(8,128)S(1)}, f32[2,45,8,128]{3,2,1,0:T(8,128)}, u32[]{:S(2)}, u32[]{:S(2)}) collective-permute-start(f32[2,45,8,128]{3,2,1,0:T(8,128)S(1)} %far2.1), channel_id=1, source_target_pairs={{1,2},{3,4},{5,6},{7,8},{9,10},{11,12},{13,14},{2,1},{4,3},{6,5},{... | collective-permute-start | bytes 1105928 | tf_op jit(solution)/shard_map/ppermute | solution.py:616
  15.9 17.1 %own.1 = (f32[18,2,4,12,8,128]{5,4,3,2,1,0:T(8,128)S(1)}, f32[12,8,128]{2,1,0:T(8,128)S(1)}, f32[3,12,8,128]{3,2,1,0:T(8,128)S(1)}, f32[9,8,128]{2,1,0:T(8,128)S(1)}) custom-call(f32[8]{0:T(128)S(1)} %power_multiply_fusion.refs_0_.refs_1_, f32[72]{0:T(128)S(1)} %copy-done.3, s32[1]{0:T(128)} %bitcast.1.refs_2_, s32[8,1440]{1,0:T(8,128)} %refs_2_.6, ...), custom_call_target="tpu_custom_call" | custom-call | tf_op jit(solution)/shard_map/own/pallas_call | solution.py:254
  33.0 8.5 %finish_near.1 = (f32[4,36,8,1440]{3,2,1,0:T(8,128)}, f32[4,12,8,128]{3,2,1,0:T(8,128)S(1)}, f32[4,12,8,128]{3,2,1,0:T(8,128)}) custom-call(s32[1]{0:T(128)} %bitcast.refs_0_, f32[8]{0:T(128)S(1)} %power_multiply_fusion.refs_0_.refs_1_, f32[72]{0:T(128)S(1)} %copy-done.3, f32[9,8,128]{2,1,0:T(8,128)S(1)} %get-tuple-element.18.refs_3_, ...), custom_call_target="tpu_custom_call" | custom-call | tf_op jit(solution)/shard_map/finish_near/pallas_call | solution.py:539
  41.6 0.6 collective-permute-done.refs_7_.refs_8_
  42.2 7.8 %finish_far1.1 = (f32[4,36,8,1440]{3,2,1,0:T(8,128)}, f32[4,12,8,128]{3,2,1,0:T(8,128)S(1)}, f32[4,12,8,128]{3,2,1,0:T(8,128)S(1)}) custom-call(s32[1]{0:T(128)S(6)} %sub.6.refs_0_, f32[8]{0:T(128)S(1)} %power_multiply_fusion.refs_0_.refs_1_, f32[72]{0:T(128)S(1)} %copy-done.3, ...), custom_call_target="tpu_custom_call", output_to_operand_aliasing={{0}: (10, {})} | custom-call | tf_op jit(solution)/shard_map/finish_far1/pallas_call | solution.py:539
  50.0 3.0 %finish_far2.1 = (f32[4,36,8,1440]{3,2,1,0:T(8,128)}, f32[4,12,8,128]{3,2,1,0:T(8,128)S(1)}) custom-call(s32[1]{0:T(128)S(6)} %sub.6.refs_0_, f32[8]{0:T(128)S(1)} %power_multiply_fusion.refs_0_.refs_1_, f32[72]{0:T(128)S(1)} %copy-done.3, f32[9,8,128]{2,1,0:T(8,128)S(1)} %get-tuple-element.18.refs_3_, ...), custom_call_target="tpu_custom_call", output_to_operand_aliasing={{0}: (9, {})} | custom-call | tf_op jit(solution)/shard_map/finish_far2/pallas_call | solution.py:539
  53.1 1.0 %slots.1 = f32[8,6,8,128]{3,2,1,0:T(8,128)S(1)} custom-call(s32[1,16]{1,0:T(1,128)S(1)} %copy-done.4, f32[4,12,8,128]{3,2,1,0:T(8,128)S(1)} %get-tuple-element.28.acc_ref), custom_call_target="tpu_custom_call" | custom-call | tf_op jit(solution)/shard_map/slots/pallas_call | solution.py:588
  54.1 15.2 %all_to_all.5 = f32[8,6,8,128]{3,2,1,0:T(8,128)S(1)} all-to-all(f32[8,6,8,128]{3,2,1,0:T(8,128)S(1)} %slots.1), channel_id=1, replica_groups=mesh['bins'=8,'tiles'=16] {'bins'}, dimensions={0} | all-to-all | bytes 393216 | tf_op jit(solution)/shard_map/all_to_all | solution.py:658
  69.3 0.1 fusion.1
  69.3 0.7 slice.32
  70.0 0.7 slice.34
  (17 shorter events, 0.1 us)
Async XLA Ops:
  3.5 12.3 %copy-start.5 = (s32[8]{0:T(128)S(1)}, s32[8]{0:T(128)}, u32[]{:S(2)}) copy-start(s32[8]{0:T(128)} %constant.47.clone) | copy-start | bytes 100
  3.5 12.3 %copy-start.6 = (pred[8]{0:T(512)(128)(4,1)S(1)}, pred[8]{0:T(512)(128)(4,1)}, u32[]{:S(2)}) copy-start(pred[8]{0:T(512)(128)(4,1)} %constant.48.clone) | copy-start | bytes 28
  3.5 12.3 %copy-start.7 = (f32[8]{0:T(128)S(1)}, f32[8]{0:T(128)}, u32[]{:S(2)}) copy-start(f32[8]{0:T(128)} %constant.56) | copy-start | bytes 100
  3.5 12.3 %copy-start.8 = (f32[8]{0:T(128)S(1)}, f32[8]{0:T(128)}, u32[]{:S(2)}) copy-start(f32[8]{0:T(128)} %constant.57) | copy-start | bytes 100
  3.6 12.3 %copy-start = (s32[8,1440]{1,0:T(8,128)S(1)}, s32[8,1440]{1,0:T(8,128)}, u32[]{:S(2)}) copy-start(s32[8,1440]{1,0:T(8,128)} %refs_4_.1) | copy-start | bytes 138244
  3.6 12.3 %copy-start.1 = (f32[8,1440]{1,0:T(8,128)S(1)}, f32[8,1440]{1,0:T(8,128)}, u32[]{:S(2)}) copy-start(f32[8,1440]{1,0:T(8,128)} %refs_5_.1) | copy-start | bytes 138244
  3.6 12.3 %copy-start.2 = (f32[8,1440]{1,0:T(8,128)S(1)}, f32[8,1440]{1,0:T(8,128)}, u32[]{:S(2)}) copy-start(f32[8,1440]{1,0:T(8,128)} %refs_6_.1) | copy-start | bytes 138244
  3.6 12.3 %copy-start.3 = (f32[72]{0:T(128)S(1)}, f32[72]{0:T(128)}, u32[]{:S(2)}) copy-start(f32[72]{0:T(128)} %constant.49.clone.refs_1_.refs_2_) | copy-start | bytes 868
  3.6 29.4 %collective-permute-start.1 = (f32[9,46,8,128]{3,2,1,0:T(8,128)S(1)}, f32[9,46,8,128]{3,2,1,0:T(8,128)}, u32[]{:S(2)}, u32[]{:S(2)}) collective-permute-start(f32[9,46,8,128]{3,2,1,0:T(8,128)S(1)} %near.1), channel_id=1, source_target_pairs={{0,1},{2,3},{4,5},{6,7},{8,9},{10,11},{12,13},{14,15},{1,0},{3,2},... | collective-permute-start | bytes 5087240 | tf_op jit(solution)/shard_map/ppermute | solution.py:616
  8.1 34.1 %collective-permute-start = (f32[7,46,8,128]{3,2,1,0:T(8,128)S(1)}, f32[7,46,8,128]{3,2,1,0:T(8,128)}, u32[]{:S(2)}, u32[]{:S(2)}) collective-permute-start(f32[7,46,8,128]{3,2,1,0:T(8,128)S(1)} %far1.1), channel_id=1, source_target_pairs={{1,2},{3,4},{5,6},{7,8},{9,10},{11,12},{13,14},{2,1},{4,3},{6,5},{... | collective-permute-start | bytes 3956744 | tf_op jit(solution)/shard_map/ppermute | solution.py:616
  12.3 37.7 %collective-permute-start.2 = (f32[2,45,8,128]{3,2,1,0:T(8,128)S(1)}, f32[2,45,8,128]{3,2,1,0:T(8,128)}, u32[]{:S(2)}, u32[]{:S(2)}) collective-permute-start(f32[2,45,8,128]{3,2,1,0:T(8,128)S(1)} %far2.1), channel_id=1, source_target_pairs={{1,2},{3,4},{5,6},{7,8},{9,10},{11,12},{13,14},{2,1},{4,3},{6,5},{... | collective-permute-start | bytes 1105928 | tf_op jit(solution)/shard_map/ppermute | solution.py:616
  50.0 3.0 %copy-start.4 = (s32[1,16]{1,0:T(1,128)S(1)}, s32[1,16]{1,0:T(1,128)}, u32[]{:S(2)}) copy-start(s32[1,16]{1,0:T(1,128)} %owner_ref.1) | copy-start | bytes 196

commit v6 on v5

--- a/solution.py
+++ b/solution.py
@@ -28,7 +28,7 @@
 TPG = NF * (TILES - 1) + 1
 
 F32 = jnp.float32
-PER_STEP = 2
+PER_STEP = 3
 LIMIT = 16 << 20
 ANGLES = (np.arange(NDIR, dtype=np.float32) + 0.5) * np.float32(2.0 * math.pi / NDIR)
 TRIG = np.concatenate([np.cos(ANGLES), np.sin(ANGLES)]).astype(np.float32)
@@ -462,6 +462,38 @@
     lax.fori_loop(0, width, one, 0)
 
 
+def slots_kernel(owner_ref, acc_ref, out_ref, order_ref, count_ref):
+    lane = lane_iota()
+    for k in range(LON_BLOCKS // 2):
+        count_ref[k] = 0
+    for block in range(LON_BLOCKS):
+        owner = owner_ref[0, block]
+        seen = count_ref[owner]
+        order_ref[2 * owner + seen] = block
+        count_ref[owner] = seen + 1
+
+    for k in range(LON_BLOCKS // 2):
+        rests = []
+        for c in range(4):
+            parts = []
+            for s in range(2):
+                column = order_ref[2 * k + s] * BLK
+                tile = column // LANES
+                shift = column % LANES
+                back = (LANES - shift) % LANES
+                here = pltpu.roll(acc_ref[c, tile], back, 1)
+                after = pltpu.roll(acc_ref[c, jnp.minimum(tile + 1, TILES - 1)], back, 1)
+                parts.append(jnp.where(lane < LANES - shift, here, after))
+            moved = pltpu.roll(parts[1], BLK, 1)
+            out_ref[k, c] = jnp.where(lane < BLK, parts[0], moved)
+            rests.append(moved)
+        for c in range(2):
+            other = pltpu.roll(rests[2 * c + 1], LANES // 2, 1)
+            both = jnp.where(lane < LANES // 2, rests[2 * c], other)
+            used = lane % (LANES // 2) < 2 * BLK - LANES
+            out_ref[k, 4 + c] = jnp.where(used, both, 0.0)
+
+
 def in_vmem(x):
     return pltpu.with_memory_space_constraint(x, pltpu.VMEM)
 
@@ -470,7 +502,22 @@
     return pltpu.with_memory_space_constraint(x, pltpu.HBM)
 
 
-def finish(south, table, trig, metric, mask, wind, own, halo, prev, old, base, width, name):
+def finish(
+    south,
+    table,
+    trig,
+    metric,
+    mask,
+    wind,
+    own,
+    halo,
+    prev,
+    old,
+    owner,
+    base,
+    width,
+    name,
+):
     groups, tiles = halo.shape[:2]
     whole = pl.BlockSpec(memory_space=pltpu.VMEM)
     block = lambda i, s: block_of(base, width, i, s[0])
@@ -492,13 +539,18 @@
     out_specs = [
         pl.BlockSpec(
             (NF, 2 * width, ROWS, TILES * LANES), lambda i, s: (0, block(i, s), 0, 0)
-        ),
-        whole,
+        )
     ]
-    out_shape = [
-        jax.ShapeDtypeStruct((NF, NDIR, ROWS, NLON), F32),
-        pltpu.VMEM((4, TILES, ROWS, LANES), F32),
-    ]
+    out_shape = [jax.ShapeDtypeStruct((NF, NDIR, ROWS, NLON), F32)]
+    acc_type = pltpu.VMEM((4, TILES, ROWS, LANES), F32)
+    window_type = pltpu.VMEM((STEPS, TILES, ROWS, LANES), F32)
+    scratch = [pltpu.VMEM((NF, TILES, ROWS, LANES), F32)]
+    with_slots = owner is not None
+    if with_slots:
+        scratch.append(acc_type)
+    else:
+        out_specs.append(whole)
+        out_shape.append(acc_type)
     with_edge = tiles > TPG
     with_prev = prev is not None
     aliases = {}
@@ -507,12 +559,25 @@
             pl.BlockSpec((TILES // 2, 1, ROWS, LANES), lambda i, s: (0, TPG, 0, 0))
         )
         args.append(halo)
-        out_specs.append(whole)
-        out_shape.append(pltpu.VMEM((STEPS, TILES, ROWS, LANES), F32))
+        if with_prev:
+            out_specs.append(whole)
+            out_shape.append(window_type)
+        else:
+            scratch.append(window_type)
     if with_prev:
         in_specs += [whole, pl.BlockSpec(memory_space=pl.ANY)]
         args += [in_vmem(prev), old]
         aliases = {len(args) - 1: 0}
+    if with_slots:
+        in_specs.append(pl.BlockSpec(memory_space=pltpu.SMEM))
+        args.append(owner)
+        out_specs.append(whole)
+        out_shape.append(pltpu.VMEM((LON_BLOCKS // 2, 6, ROWS, LANES), F32))
+        scratch += [
+            pltpu.SMEM((LON_BLOCKS,), jnp.int32),
+            pltpu.SMEM((LON_BLOCKS // 2,), jnp.int32),
+        ]
+    steps = groups // width
 
     def kernel(*refs):
         refs = list(refs)
@@ -520,8 +585,16 @@
         edge = refs.pop(0) if with_edge else None
         before = refs.pop(0) if with_prev else None
         former = refs.pop(0) if with_prev else None
-        result, acc = refs.pop(0), refs.pop(0)
-        windows = refs.pop(0) if with_edge else None
+        owners = refs.pop(0) if with_slots else None
+        result = refs.pop(0)
+        acc = None if with_slots else refs.pop(0)
+        windows = refs.pop(0) if with_edge and with_prev else None
+        sent = refs.pop(0) if with_slots else None
+        parts = refs.pop(0)
+        if with_slots:
+            acc = refs.pop(0)
+        if with_edge and not with_prev:
+            windows = refs.pop(0)
         finish_kernel(
             base,
             groups,
@@ -533,73 +606,28 @@
             result,
             acc,
             windows,
-            *refs,
+            parts,
         )
+        if with_slots:
+
+            @pl.when(pl.program_id(0) == steps - 1)
+            def _():
+                slots_kernel(owners, acc, sent, *refs)
 
     return pl.pallas_call(
         kernel,
         grid_spec=pltpu.PrefetchScalarGridSpec(
             num_scalar_prefetch=1,
-            grid=(groups // width,),
+            grid=(steps,),
             in_specs=in_specs,
             out_specs=out_specs,
-            scratch_shapes=[pltpu.VMEM((NF, TILES, ROWS, LANES), F32)],
+            scratch_shapes=scratch,
         ),
         out_shape=out_shape,
         input_output_aliases=aliases,
         compiler_params=pltpu.CompilerParams(vmem_limit_bytes=LIMIT),
         name=name,
     )(*args)
-
-
-def slots_kernel(owner_ref, acc_ref, out_ref, order_ref, count_ref):
-    lane = lane_iota()
-    for k in range(LON_BLOCKS // 2):
-        count_ref[k] = 0
-    for block in range(LON_BLOCKS):
-        owner = owner_ref[0, block]
-        seen = count_ref[owner]
-        order_ref[2 * owner + seen] = block
-        count_ref[owner] = seen + 1
-
-    for k in range(LON_BLOCKS // 2):
-        rests = []
-        for c in range(4):
-            parts = []
-            for s in range(2):
-                column = order_ref[2 * k + s] * BLK
-                tile = column // LANES
-                shift = column % LANES
-                back = (LANES - shift) % LANES
-                here = pltpu.roll(acc_ref[c, tile], back, 1)
-                after = pltpu.roll(acc_ref[c, jnp.minimum(tile + 1, TILES - 1)], back, 1)
-                parts.append(jnp.where(lane < LANES - shift, here, after))
-            moved = pltpu.roll(parts[1], BLK, 1)
-            out_ref[k, c] = jnp.where(lane < BLK, parts[0], moved)
-            rests.append(moved)
-        for c in range(2):
-            other = pltpu.roll(rests[2 * c + 1], LANES // 2, 1)
-            both = jnp.where(lane < LANES // 2, rests[2 * c], other)
-            used = lane % (LANES // 2) < 2 * BLK - LANES
-            out_ref[k, 4 + c] = jnp.where(used, both, 0.0)
-
-
-def pick_slots(owner, acc):
-    return pl.pallas_call(
-        slots_kernel,
-        in_specs=[
-            pl.BlockSpec(memory_space=pltpu.SMEM),
-            pl.BlockSpec(memory_space=pltpu.VMEM),
-        ],
-        out_specs=pl.BlockSpec(memory_space=pltpu.VMEM),
-        out_shape=pltpu.VMEM((LON_BLOCKS // 2, 6, ROWS, LANES), F32),
-        scratch_shapes=[
-            pltpu.SMEM((LON_BLOCKS,), jnp.int32),
-            pltpu.SMEM((LON_BLOCKS // 2,), jnp.int32),
-        ],
-        compiler_params=pltpu.CompilerParams(vmem_limit_bytes=LIMIT),
-        name="slots",
-    )(owner, acc)
 
 
 def shards(spectrum, sea_mask, ice_mask, friction, wind_dir, ocean_owner):
@@ -644,17 +672,27 @@
         wind_dir,
     )
     common = (table, trig, metric)
-    out, acc, _ = finish(
-        odd, *common, mask, wind, own, near, None, None, 0, 3, "finish_near"
+    out, acc = finish(
+        odd, *common, mask, wind, own, near, None, None, None, 0, 3, "finish_near"
     )
     out, acc, windows = finish(
-        even, *common, mask, wind, own, far1, acc, out, 0, 1, "finish_far1"
+        even, *common, mask, wind, own, far1, acc, out, None, 0, 1, "finish_far1"
     )
-    out, acc = finish(
-        even, *common, windows, wind, own, far2, acc, out, G1, 1, "finish_far2"
+    out, sent = finish(
+        even,
+        *common,
+        windows,
+        wind,
+        own,
+        far2,
+        acc,
+        out,
+        ocean_owner,
+        G1,
+        1,
+        "finish_far2",
     )
 
-    sent = pick_slots(ocean_owner, acc)
     got = lax.all_to_all(sent, "bins", 0, 0, tiled=True)
     total = got.sum(0)
     rest = total[4:].reshape(2, ROWS, 2, LANES // 2).transpose(0, 2, 1, 3)

time: 71.2 us -> 70.7 us (level)
    pallas_call x1 -> x0, Pallas kernels: 1.02 us -> none  [pick_slots(): pl.pallas_call(slots_kernel, in_specs=[pl.BlockSpec(memory_space=pltpu.SM...]
  transfers between devices with their start and end apart: 3 -> 3, of which waited for: 1 -> 1; matrix products, arithmetic and copies ran while one was open for 0% -> 0% of each run, Pallas kernels for 55% -> 56%
where the time goes in v6:
time: 70.7 us; the launch traced here: 70.2 us
  Pallas kernels  45.5 us (64%)
  blocking collectives  15.1 us (21%)
  starting transfers between devices  6.53 us (9%)
  local copies, waits for them, and re-layouts  1.51 us (2%)
  between operations  0.85 us (1%)
    pallas_call x3, Pallas kernels, finish(): pl.pallas_call(kernel, grid_spec=pltpu.PrefetchScalarGridSpec(num_scalar_...  19.8 us
    pallas_call x1, Pallas kernels, own_rows(): pl.pallas_call(lambda *refs: own_kernel(lat_total, *refs), grid=(2 * GROU...  17.2 us
    all_to_all x1, blocking collectives, shards(): got = lax.all_to_all(sent, 'bins', 0, 0, tiled=True)  15.1 us
    pallas_call x3, Pallas kernels, pack(): pl.pallas_call(lambda *refs: pack_kernel(base, width, with_mask, *refs),...  8.49 us
    ppermute x3, starting transfers between devices, swap(): return lax.ppermute(x, 'tiles', pairs + [(j, i) for i, j in pairs])  6.53 us
  transfers between devices with their start and end apart: 3, of which 1 were waited for; matrix products, arithmetic and copies ran while one was open for 0% of the time, Pallas kernels for 56%

profile of v6, /device:TPU:32, one launch (start us, length us, event | category | flops | bytes accessed | tf_op | source)
XLA Modules:
  0.0 70.2 jit_solution(18137678487838691328)
XLA Ops:
  0.6 2.9 %near.1 = f32[9,46,8,128]{3,2,1,0:T(8,128)S(1)} custom-call(s32[1]{0:T(128)S(6)} %sub.6.refs_0_, f32[4,36,8,1440]{3,2,1,0:T(8,128)} %bitcast.6, s32[8,1440]{1,0:T(8,128)} %refs_2_.6), custom_call_target="tpu_custom_call" | custom-call | tf_op jit(solution)/shard_map/near/pallas_call | solution.py:98
  3.5 0.0 copy-start.5
  3.5 0.0 copy-start.6
  3.5 0.0 copy-start.7
  3.5 0.0 copy-start.8
  3.6 0.0 copy-start
  3.6 0.0 copy-start.1
  3.6 0.0 copy-start.2
  3.6 0.0 copy-start.3
  3.6 0.1 collective-permute-start.1
  3.7 4.4 %far1.1 = f32[7,46,8,128]{3,2,1,0:T(8,128)S(1)} custom-call(s32[1]{0:T(128)} %bitcast.refs_0_, f32[4,36,8,1440]{3,2,1,0:T(8,128)} %bitcast.7, s32[8,1440]{1,0:T(8,128)} %refs_2_.6), custom_call_target="tpu_custom_call" | custom-call | tf_op jit(solution)/shard_map/far1/pallas_call | solution.py:98
  8.1 3.0 %collective-permute-start = (f32[7,46,8,128]{3,2,1,0:T(8,128)S(1)}, f32[7,46,8,128]{3,2,1,0:T(8,128)}, u32[]{:S(2)}, u32[]{:S(2)}) collective-permute-start(f32[7,46,8,128]{3,2,1,0:T(8,128)S(1)} %far1.1), channel_id=1, source_target_pairs={{1,2},{3,4},{5,6},{7,8},{9,10},{11,12},{13,14},{2,1},{4,3},{6,5},{... | collective-permute-start | bytes 3956744 | tf_op jit(solution)/shard_map/ppermute | solution.py:644
  11.1 1.2 %far2.1 = f32[2,45,8,128]{3,2,1,0:T(8,128)S(1)} custom-call(s32[1]{0:T(128)} %bitcast.refs_0_, f32[4,36,8,1440]{3,2,1,0:T(8,128)} %bitcast.8, s32[8,1440]{1,0:T(8,128)} %refs_2_.6), custom_call_target="tpu_custom_call" | custom-call | tf_op jit(solution)/shard_map/far2/pallas_call | solution.py:98
  12.3 3.4 %collective-permute-start.2 = (f32[2,45,8,128]{3,2,1,0:T(8,128)S(1)}, f32[2,45,8,128]{3,2,1,0:T(8,128)}, u32[]{:S(2)}, u32[]{:S(2)}) collective-permute-start(f32[2,45,8,128]{3,2,1,0:T(8,128)S(1)} %far2.1), channel_id=1, source_target_pairs={{1,2},{3,4},{5,6},{7,8},{9,10},{11,12},{13,14},{2,1},{4,3},{6,5},{... | collective-permute-start | bytes 1105928 | tf_op jit(solution)/shard_map/ppermute | solution.py:644
  15.9 17.2 %own.1 = (f32[18,2,4,12,8,128]{5,4,3,2,1,0:T(8,128)S(1)}, f32[12,8,128]{2,1,0:T(8,128)S(1)}, f32[3,12,8,128]{3,2,1,0:T(8,128)S(1)}, f32[9,8,128]{2,1,0:T(8,128)S(1)}) custom-call(f32[8]{0:T(128)S(1)} %power_multiply_fusion.refs_0_.refs_1_, f32[72]{0:T(128)S(1)} %copy-done.3, s32[1]{0:T(128)} %bitcast.1.refs_2_, s32[8,1440]{1,0:T(8,128)} %refs_2_.6, ...), custom_call_target="tpu_custom_call" | custom-call | tf_op jit(solution)/shard_map/own/pallas_call | solution.py:254
  33.1 0.0 collective-permute-done.1.refs_7_.refs_8_
  33.1 8.5 %finish_near.1 = (f32[4,36,8,1440]{3,2,1,0:T(8,128)}, f32[4,12,8,128]{3,2,1,0:T(8,128)S(1)}) custom-call(s32[1]{0:T(128)} %bitcast.refs_0_, f32[8]{0:T(128)S(1)} %power_multiply_fusion.refs_0_.refs_1_, f32[72]{0:T(128)S(1)} %copy-done.3, f32[9,8,128]{2,1,0:T(8,128)S(1)} %get-tuple-element.18.refs_3_, f32[12,8,128]{2,1,0:T(8,128)S(1)} %get-tuple-element.19.refs_4_, ...), custom_call_target="tpu_custom_call" | custom-call | tf_op jit(solution)/shard_map/finish_near/pallas_call | solution.py:617
  41.5 0.6 collective-permute-done.refs_7_.refs_8_
  42.2 7.8 %finish_far1.1 = (f32[4,36,8,1440]{3,2,1,0:T(8,128)}, f32[4,12,8,128]{3,2,1,0:T(8,128)S(1)}, f32[4,12,8,128]{3,2,1,0:T(8,128)S(1)}) custom-call(s32[1]{0:T(128)S(6)} %sub.6.refs_0_, f32[8]{0:T(128)S(1)} %power_multiply_fusion.refs_0_.refs_1_, f32[72]{0:T(128)S(1)} %copy-done.3, ...), custom_call_target="tpu_custom_call", output_to_operand_aliasing={{0}: (10, {})} | custom-call | tf_op jit(solution)/shard_map/finish_far1/pallas_call | solution.py:617
  50.0 3.5 %finish_far2.1 = (f32[4,36,8,1440]{3,2,1,0:T(8,128)}, f32[8,6,8,128]{3,2,1,0:T(8,128)S(1)}) custom-call(s32[1]{0:T(128)S(6)} %sub.6.refs_0_, f32[8]{0:T(128)S(1)} %power_multiply_fusion.refs_0_.refs_1_, f32[72]{0:T(128)S(1)} %copy-done.3, f32[9,8,128]{2,1,0:T(8,128)S(1)} %get-tuple-element.18.refs_3_, ...), custom_call_target="tpu_custom_call", output_to_operand_aliasing={{0}: (9, {})} | custom-call | tf_op jit(solution)/shard_map/finish_far2/pallas_call | solution.py:617
  53.6 15.1 %all_to_all.5 = f32[8,6,8,128]{3,2,1,0:T(8,128)S(1)} all-to-all(f32[8,6,8,128]{3,2,1,0:T(8,128)S(1)} %get-tuple-element.28), channel_id=1, replica_groups=mesh['bins'=8,'tiles'=16] {'bins'}, dimensions={0} | all-to-all | bytes 393216 | tf_op jit(solution)/shard_map/all_to_all | solution.py:696
  68.7 0.1 fusion.1
  68.8 0.7 slice.32
  69.5 0.7 slice.34
  (16 shorter events, 0.1 us)
Async XLA Ops:
  3.5 12.3 %copy-start.5 = (s32[8]{0:T(128)S(1)}, s32[8]{0:T(128)}, u32[]{:S(2)}) copy-start(s32[8]{0:T(128)} %constant.47.clone) | copy-start | bytes 100
  3.5 12.3 %copy-start.6 = (pred[8]{0:T(512)(128)(4,1)S(1)}, pred[8]{0:T(512)(128)(4,1)}, u32[]{:S(2)}) copy-start(pred[8]{0:T(512)(128)(4,1)} %constant.48.clone) | copy-start | bytes 28
  3.5 12.3 %copy-start.7 = (f32[8]{0:T(128)S(1)}, f32[8]{0:T(128)}, u32[]{:S(2)}) copy-start(f32[8]{0:T(128)} %constant.56) | copy-start | bytes 100
  3.5 12.3 %copy-start.8 = (f32[8]{0:T(128)S(1)}, f32[8]{0:T(128)}, u32[]{:S(2)}) copy-start(f32[8]{0:T(128)} %constant.57) | copy-start | bytes 100
  3.6 12.3 %copy-start = (s32[8,1440]{1,0:T(8,128)S(1)}, s32[8,1440]{1,0:T(8,128)}, u32[]{:S(2)}) copy-start(s32[8,1440]{1,0:T(8,128)} %refs_4_.1) | copy-start | bytes 138244
  3.6 12.3 %copy-start.1 = (f32[8,1440]{1,0:T(8,128)S(1)}, f32[8,1440]{1,0:T(8,128)}, u32[]{:S(2)}) copy-start(f32[8,1440]{1,0:T(8,128)} %refs_5_.1) | copy-start | bytes 138244
  3.6 12.3 %copy-start.2 = (f32[8,1440]{1,0:T(8,128)S(1)}, f32[8,1440]{1,0:T(8,128)}, u32[]{:S(2)}) copy-start(f32[8,1440]{1,0:T(8,128)} %refs_6_.1) | copy-start | bytes 138244
  3.6 12.3 %copy-start.3 = (f32[72]{0:T(128)S(1)}, f32[72]{0:T(128)}, u32[]{:S(2)}) copy-start(f32[72]{0:T(128)} %constant.49.clone.refs_1_.refs_2_) | copy-start | bytes 868
  3.6 29.5 %collective-permute-start.1 = (f32[9,46,8,128]{3,2,1,0:T(8,128)S(1)}, f32[9,46,8,128]{3,2,1,0:T(8,128)}, u32[]{:S(2)}, u32[]{:S(2)}) collective-permute-start(f32[9,46,8,128]{3,2,1,0:T(8,128)S(1)} %near.1), channel_id=1, source_target_pairs={{0,1},{2,3},{4,5},{6,7},{8,9},{10,11},{12,13},{14,15},{1,0},{3,2},... | collective-permute-start | bytes 5087240 | tf_op jit(solution)/shard_map/ppermute | solution.py:644
  8.1 34.1 %collective-permute-start = (f32[7,46,8,128]{3,2,1,0:T(8,128)S(1)}, f32[7,46,8,128]{3,2,1,0:T(8,128)}, u32[]{:S(2)}, u32[]{:S(2)}) collective-permute-start(f32[7,46,8,128]{3,2,1,0:T(8,128)S(1)} %far1.1), channel_id=1, source_target_pairs={{1,2},{3,4},{5,6},{7,8},{9,10},{11,12},{13,14},{2,1},{4,3},{6,5},{... | collective-permute-start | bytes 3956744 | tf_op jit(solution)/shard_map/ppermute | solution.py:644
  12.3 37.7 %collective-permute-start.2 = (f32[2,45,8,128]{3,2,1,0:T(8,128)S(1)}, f32[2,45,8,128]{3,2,1,0:T(8,128)}, u32[]{:S(2)}, u32[]{:S(2)}) collective-permute-start(f32[2,45,8,128]{3,2,1,0:T(8,128)S(1)} %far2.1), channel_id=1, source_target_pairs={{1,2},{3,4},{5,6},{7,8},{9,10},{11,12},{13,14},{2,1},{4,3},{6,5},{... | collective-permute-start | bytes 1105928 | tf_op jit(solution)/shard_map/ppermute | solution.py:644
  42.2 7.8 %copy-start.4 = (s32[1,16]{1,0:T(1,128)S(1)}, s32[1,16]{1,0:T(1,128)}, u32[]{:S(2)}) copy-start(s32[1,16]{1,0:T(1,128)} %refs_10_.1) | copy-start | bytes 196

commit v7 on v6

--- a/solution.py
+++ b/solution.py
@@ -23,12 +23,12 @@
 TAIL = NLON - (TILES - 1) * LANES
 NF = 4
 GROUPS = 9
-G1 = 7
+G1 = 6
 G2 = GROUPS - G1
 TPG = NF * (TILES - 1) + 1
 
 F32 = jnp.float32
-PER_STEP = 3
+PER_STEP = 2
 LIMIT = 16 << 20
 ANGLES = (np.arange(NDIR, dtype=np.float32) + 0.5) * np.float32(2.0 * math.pi / NDIR)
 TRIG = np.concatenate([np.cos(ANGLES), np.sin(ANGLES)]).astype(np.float32)
@@ -646,10 +646,10 @@
     near = pack(even, spectral, sea, 0, GROUPS, 3, True, "near")
     sea, _ = lax.optimization_barrier((sea, near))
     near = swap(near, 0)
-    far1 = pack(odd, spectral, sea, 0, G1, 1, True, "far1")
+    far1 = pack(odd, spectral, sea, 0, G1, 2, True, "far1")
     sea, _ = lax.optimization_barrier((sea, far1))
     far1 = swap(far1, 1)
-    far2 = pack(odd, spectral, sea, G1, G2, 1, False, "far2")
+    far2 = pack(odd, spectral, sea, G1, G2, 3, False, "far2")
     far2 = swap(far2, 1)
 
     place = np.tile(np.arange(NF), 2)
@@ -676,7 +676,7 @@
         odd, *common, mask, wind, own, near, None, None, None, 0, 3, "finish_near"
     )
     out, acc, windows = finish(
-        even, *common, mask, wind, own, far1, acc, out, None, 0, 1, "finish_far1"
+        even, *common, mask, wind, own, far1, acc, out, None, 0, 2, "finish_far1"
     )
     out, sent = finish(
         even,

time: 70.7 us -> 69.4 us (0.982)
  Pallas kernels: 45.5 us -> 43 us
  waiting for transfers between devices: 0.65 us -> 1.44 us
    pallas_call x3, Pallas kernels: 8.49 us -> 6.73 us  [pack(): pl.pallas_call(lambda *refs: pack_kernel(base, width, with_mask, *refs),...]
    ppermute x3, waiting for transfers between devices: 0.65 us -> 1.44 us  [swap(): return lax.ppermute(x, 'tiles', pairs + [(j, i) for i, j in pairs])]
  transfers between devices with their start and end apart: 3 -> 3, of which waited for: 1 -> 1; matrix products, arithmetic and copies ran while one was open for 0% -> 0% of each run, Pallas kernels for 56% -> 52%
where the time goes in v7:
time: 69.4 us; the launch traced here: 68.7 us
  Pallas kernels  43 us (62%)
  blocking collectives  15.2 us (22%)
  starting transfers between devices  6.55 us (9%)
  local copies, waits for them, and re-layouts  1.51 us (2%)
  waiting for transfers between devices  1.44 us (2%)
  between operations  0.86 us (1%)
    pallas_call x3, Pallas kernels, finish(): pl.pallas_call(kernel, grid_spec=pltpu.PrefetchScalarGridSpec(num_scalar_...  19.2 us
    pallas_call x1, Pallas kernels, own_rows(): pl.pallas_call(lambda *refs: own_kernel(lat_total, *refs), grid=(2 * GROU...  17.1 us
    all_to_all x1, blocking collectives, shards(): got = lax.all_to_all(sent, 'bins', 0, 0, tiled=True)  15.2 us
    pallas_call x3, Pallas kernels, pack(): pl.pallas_call(lambda *refs: pack_kernel(base, width, with_mask, *refs),...  6.73 us
    ppermute x3, starting transfers between devices, swap(): return lax.ppermute(x, 'tiles', pairs + [(j, i) for i, j in pairs])  6.55 us
    ppermute x3, waiting for transfers between devices, swap(): return lax.ppermute(x, 'tiles', pairs + [(j, i) for i, j in pairs])  1.44 us
  transfers between devices with their start and end apart: 3, of which 1 were waited for; matrix products, arithmetic and copies ran while one was open for 0% of the time, Pallas kernels for 52%

profile of v7, /device:TPU:32, one launch (start us, length us, event | category | flops | bytes accessed | tf_op | source)
XLA Modules:
  0.0 68.7 jit_solution(8826481742247768087)
XLA Ops:
  0.6 2.9 %near.1 = f32[9,46,8,128]{3,2,1,0:T(8,128)S(1)} custom-call(s32[1]{0:T(128)S(6)} %sub.6.refs_0_, f32[4,36,8,1440]{3,2,1,0:T(8,128)} %bitcast.6, s32[8,1440]{1,0:T(8,128)} %refs_2_.6), custom_call_target="tpu_custom_call" | custom-call | tf_op jit(solution)/shard_map/near/pallas_call | solution.py:98
  3.5 0.0 copy-start.5
  3.5 0.0 copy-start.6
  3.5 0.0 copy-start.7
  3.5 0.0 copy-start.8
  3.6 0.0 copy-start
  3.6 0.0 copy-start.1
  3.6 0.0 copy-start.2
  3.6 0.0 copy-start.3
  3.6 0.1 collective-permute-start.1
  3.7 2.5 %far1.1 = f32[6,46,8,128]{3,2,1,0:T(8,128)S(1)} custom-call(s32[1]{0:T(128)} %bitcast.refs_0_, f32[4,36,8,1440]{3,2,1,0:T(8,128)} %bitcast.7, s32[8,1440]{1,0:T(8,128)} %refs_2_.6), custom_call_target="tpu_custom_call" | custom-call | tf_op jit(solution)/shard_map/far1/pallas_call | solution.py:98
  6.2 3.0 %collective-permute-start = (f32[6,46,8,128]{3,2,1,0:T(8,128)S(1)}, f32[6,46,8,128]{3,2,1,0:T(8,128)}, u32[]{:S(2)}, u32[]{:S(2)}) collective-permute-start(f32[6,46,8,128]{3,2,1,0:T(8,128)S(1)} %far1.1), channel_id=1, source_target_pairs={{1,2},{3,4},{5,6},{7,8},{9,10},{11,12},{13,14},{2,1},{4,3},{6,5},{... | collective-permute-start | bytes 3391496 | tf_op jit(solution)/shard_map/ppermute | solution.py:644
  9.3 1.4 %far2.1 = f32[3,45,8,128]{3,2,1,0:T(8,128)S(1)} custom-call(s32[1]{0:T(128)} %bitcast.refs_0_, f32[4,36,8,1440]{3,2,1,0:T(8,128)} %bitcast.8, s32[8,1440]{1,0:T(8,128)} %refs_2_.6), custom_call_target="tpu_custom_call" | custom-call | tf_op jit(solution)/shard_map/far2/pallas_call | solution.py:98
  10.6 3.4 %collective-permute-start.2 = (f32[3,45,8,128]{3,2,1,0:T(8,128)S(1)}, f32[3,45,8,128]{3,2,1,0:T(8,128)}, u32[]{:S(2)}, u32[]{:S(2)}) collective-permute-start(f32[3,45,8,128]{3,2,1,0:T(8,128)S(1)} %far2.1), channel_id=1, source_target_pairs={{1,2},{3,4},{5,6},{7,8},{9,10},{11,12},{13,14},{2,1},{4,3},{6,5},{... | collective-permute-start | bytes 1658888 | tf_op jit(solution)/shard_map/ppermute | solution.py:644
  14.2 17.1 %own.1 = (f32[18,2,4,12,8,128]{5,4,3,2,1,0:T(8,128)S(1)}, f32[12,8,128]{2,1,0:T(8,128)S(1)}, f32[3,12,8,128]{3,2,1,0:T(8,128)S(1)}, f32[9,8,128]{2,1,0:T(8,128)S(1)}) custom-call(f32[8]{0:T(128)S(1)} %power_multiply_fusion.refs_0_.refs_1_, f32[72]{0:T(128)S(1)} %copy-done.3, s32[1]{0:T(128)} %bitcast.1.refs_2_, s32[8,1440]{1,0:T(8,128)} %refs_2_.6, ...), custom_call_target="tpu_custom_call" | custom-call | tf_op jit(solution)/shard_map/own/pallas_call | solution.py:254
  31.3 8.5 %finish_near.1 = (f32[4,36,8,1440]{3,2,1,0:T(8,128)}, f32[4,12,8,128]{3,2,1,0:T(8,128)S(1)}) custom-call(s32[1]{0:T(128)} %bitcast.refs_0_, f32[8]{0:T(128)S(1)} %power_multiply_fusion.refs_0_.refs_1_, f32[72]{0:T(128)S(1)} %copy-done.3, f32[9,8,128]{2,1,0:T(8,128)S(1)} %get-tuple-element.18.refs_3_, f32[12,8,128]{2,1,0:T(8,128)S(1)} %get-tuple-element.19.refs_4_, ...), custom_call_target="tpu_custom_call" | custom-call | tf_op jit(solution)/shard_map/finish_near/pallas_call | solution.py:617
  39.8 0.0 collective-permute-done.refs_7_.refs_8_
  39.8 6.2 %finish_far1.1 = (f32[4,36,8,1440]{3,2,1,0:T(8,128)}, f32[4,12,8,128]{3,2,1,0:T(8,128)S(1)}, f32[4,12,8,128]{3,2,1,0:T(8,128)S(1)}) custom-call(s32[1]{0:T(128)S(6)} %sub.6.refs_0_, f32[8]{0:T(128)S(1)} %power_multiply_fusion.refs_0_.refs_1_, f32[72]{0:T(128)S(1)} %copy-done.3, ...), custom_call_target="tpu_custom_call", output_to_operand_aliasing={{0}: (10, {})} | custom-call | tf_op jit(solution)/shard_map/finish_far1/pallas_call | solution.py:617
  46.0 1.4 %collective-permute-done.2.refs_7_ = f32[3,45,8,128]{3,2,1,0:T(8,128)} collective-permute-done((f32[3,45,8,128]{3,2,1,0:T(8,128)S(1)}, f32[3,45,8,128]{3,2,1,0:T(8,128)}, u32[]{:S(2)}, u32[]{:S(2)}) %collective-permute-start.2) | collective-permute-done | bytes 552992 | tf_op jit(solution)/shard_map/ppermute | solution.py:644
  47.4 4.6 %finish_far2.1 = (f32[4,36,8,1440]{3,2,1,0:T(8,128)}, f32[8,6,8,128]{3,2,1,0:T(8,128)S(1)}) custom-call(s32[1]{0:T(128)S(6)} %sub.6.refs_0_, f32[8]{0:T(128)S(1)} %power_multiply_fusion.refs_0_.refs_1_, f32[72]{0:T(128)S(1)} %copy-done.3, f32[9,8,128]{2,1,0:T(8,128)S(1)} %get-tuple-element.18.refs_3_, ...), custom_call_target="tpu_custom_call", output_to_operand_aliasing={{0}: (9, {})} | custom-call | tf_op jit(solution)/shard_map/finish_far2/pallas_call | solution.py:617
  52.0 15.2 %all_to_all.5 = f32[8,6,8,128]{3,2,1,0:T(8,128)S(1)} all-to-all(f32[8,6,8,128]{3,2,1,0:T(8,128)S(1)} %get-tuple-element.28), channel_id=1, replica_groups=mesh['bins'=8,'tiles'=16] {'bins'}, dimensions={0} | all-to-all | bytes 393216 | tf_op jit(solution)/shard_map/all_to_all | solution.py:696
  67.2 0.1 fusion.1
  67.3 0.7 %slice.32 = f32[2,8,2,90]{3,2,1,0:T(2,128)} reshape(f32[2,8,180]{2,1,0:T(8,128)S(1)} %get-tuple-element.30) | data formatting | bytes 23040 | tf_op jit(solution)/shard_map/slice | solution.py:701
  68.0 0.7 %slice.34 = f32[2,8,2,90]{3,2,1,0:T(2,128)} reshape(f32[2,8,180]{2,1,0:T(8,128)S(1)} %get-tuple-element.29) | data formatting | bytes 23040 | tf_op jit(solution)/shard_map/slice | solution.py:701
  (16 shorter events, 0.1 us)
Async XLA Ops:
  3.5 10.6 %copy-start.5 = (s32[8]{0:T(128)S(1)}, s32[8]{0:T(128)}, u32[]{:S(2)}) copy-start(s32[8]{0:T(128)} %constant.47.clone) | copy-start | bytes 100
  3.5 10.6 %copy-start.6 = (pred[8]{0:T(512)(128)(4,1)S(1)}, pred[8]{0:T(512)(128)(4,1)}, u32[]{:S(2)}) copy-start(pred[8]{0:T(512)(128)(4,1)} %constant.48.clone) | copy-start | bytes 28
  3.5 10.6 %copy-start.7 = (f32[8]{0:T(128)S(1)}, f32[8]{0:T(128)}, u32[]{:S(2)}) copy-start(f32[8]{0:T(128)} %constant.56) | copy-start | bytes 100
  3.5 10.6 %copy-start.8 = (f32[8]{0:T(128)S(1)}, f32[8]{0:T(128)}, u32[]{:S(2)}) copy-start(f32[8]{0:T(128)} %constant.57) | copy-start | bytes 100
  3.6 10.6 %copy-start = (s32[8,1440]{1,0:T(8,128)S(1)}, s32[8,1440]{1,0:T(8,128)}, u32[]{:S(2)}) copy-start(s32[8,1440]{1,0:T(8,128)} %refs_4_.1) | copy-start | bytes 138244
  3.6 10.6 %copy-start.1 = (f32[8,1440]{1,0:T(8,128)S(1)}, f32[8,1440]{1,0:T(8,128)}, u32[]{:S(2)}) copy-start(f32[8,1440]{1,0:T(8,128)} %refs_5_.1) | copy-start | bytes 138244
  3.6 10.6 %copy-start.2 = (f32[8,1440]{1,0:T(8,128)S(1)}, f32[8,1440]{1,0:T(8,128)}, u32[]{:S(2)}) copy-start(f32[8,1440]{1,0:T(8,128)} %refs_6_.1) | copy-start | bytes 138244
  3.6 10.6 %copy-start.3 = (f32[72]{0:T(128)S(1)}, f32[72]{0:T(128)}, u32[]{:S(2)}) copy-start(f32[72]{0:T(128)} %constant.49.clone.refs_1_.refs_2_) | copy-start | bytes 868
  3.6 27.7 %collective-permute-start.1 = (f32[9,46,8,128]{3,2,1,0:T(8,128)S(1)}, f32[9,46,8,128]{3,2,1,0:T(8,128)}, u32[]{:S(2)}, u32[]{:S(2)}) collective-permute-start(f32[9,46,8,128]{3,2,1,0:T(8,128)S(1)} %near.1), channel_id=1, source_target_pairs={{0,1},{2,3},{4,5},{6,7},{8,9},{10,11},{12,13},{14,15},{1,0},{3,2},... | collective-permute-start | bytes 5087240 | tf_op jit(solution)/shard_map/ppermute | solution.py:644
  6.2 33.6 %collective-permute-start = (f32[6,46,8,128]{3,2,1,0:T(8,128)S(1)}, f32[6,46,8,128]{3,2,1,0:T(8,128)}, u32[]{:S(2)}, u32[]{:S(2)}) collective-permute-start(f32[6,46,8,128]{3,2,1,0:T(8,128)S(1)} %far1.1), channel_id=1, source_target_pairs={{1,2},{3,4},{5,6},{7,8},{9,10},{11,12},{13,14},{2,1},{4,3},{6,5},{... | collective-permute-start | bytes 3391496 | tf_op jit(solution)/shard_map/ppermute | solution.py:644
  10.6 36.8 %collective-permute-start.2 = (f32[3,45,8,128]{3,2,1,0:T(8,128)S(1)}, f32[3,45,8,128]{3,2,1,0:T(8,128)}, u32[]{:S(2)}, u32[]{:S(2)}) collective-permute-start(f32[3,45,8,128]{3,2,1,0:T(8,128)S(1)} %far2.1), channel_id=1, source_target_pairs={{1,2},{3,4},{5,6},{7,8},{9,10},{11,12},{13,14},{2,1},{4,3},{6,5},{... | collective-permute-start | bytes 1658888 | tf_op jit(solution)/shard_map/ppermute | solution.py:644
  39.8 7.6 %copy-start.4 = (s32[1,16]{1,0:T(1,128)S(1)}, s32[1,16]{1,0:T(1,128)}, u32[]{:S(2)}) copy-start(s32[1,16]{1,0:T(1,128)} %refs_10_.1) | copy-start | bytes 196

commit v8 on v7

--- a/solution.py
+++ b/solution.py
@@ -646,7 +646,7 @@
     near = pack(even, spectral, sea, 0, GROUPS, 3, True, "near")
     sea, _ = lax.optimization_barrier((sea, near))
     near = swap(near, 0)
-    far1 = pack(odd, spectral, sea, 0, G1, 2, True, "far1")
+    far1 = pack(odd, spectral, sea, 0, G1, 3, True, "far1")
     sea, _ = lax.optimization_barrier((sea, far1))
     far1 = swap(far1, 1)
     far2 = pack(odd, spectral, sea, G1, G2, 3, False, "far2")
@@ -676,7 +676,7 @@
         odd, *common, mask, wind, own, near, None, None, None, 0, 3, "finish_near"
     )
     out, acc, windows = finish(
-        even, *common, mask, wind, own, far1, acc, out, None, 0, 2, "finish_far1"
+        even, *common, mask, wind, own, far1, acc, out, None, 0, 3, "finish_far1"
     )
     out, sent = finish(
         even,

time: 69.4 us -> 68.6 us (0.988)
    pallas_call x3, Pallas kernels: 6.73 us -> 6.01 us  [pack(): pl.pallas_call(lambda *refs: pack_kernel(base, width, with_mask, *refs),...]
where the time goes in v8:
time: 68.6 us; the launch traced here: 68 us
  Pallas kernels  42.5 us (62%)
  blocking collectives  15.2 us (22%)
  starting transfers between devices  6.55 us (10%)
  local copies, waits for them, and re-layouts  1.51 us (2%)
  waiting for transfers between devices  1.3 us (2%)
  between operations  0.86 us (1%)
    pallas_call x3, Pallas kernels, finish(): pl.pallas_call(kernel, grid_spec=pltpu.PrefetchScalarGridSpec(num_scalar_...  19.3 us
    pallas_call x1, Pallas kernels, own_rows(): pl.pallas_call(lambda *refs: own_kernel(lat_total, *refs), grid=(2 * GROU...  17.1 us
    all_to_all x1, blocking collectives, shards(): got = lax.all_to_all(sent, 'bins', 0, 0, tiled=True)  15.2 us
    ppermute x3, starting transfers between devices, swap(): return lax.ppermute(x, 'tiles', pairs + [(j, i) for i, j in pairs])  6.55 us
    pallas_call x3, Pallas kernels, pack(): pl.pallas_call(lambda *refs: pack_kernel(base, width, with_mask, *refs),...  6.01 us
    slice x2, local copies, waits for them, and re-layouts, shards(): return (out.reshape(spectrum.shape), fields[:2], fields[2:])  1.38 us
  transfers between devices with their start and end apart: 3, of which 1 were waited for; matrix products, arithmetic and copies ran while one was open for 0% of the time, Pallas kernels for 52%

profile of v8, /device:TPU:32, one launch (start us, length us, event | category | flops | bytes accessed | tf_op | source)
XLA Modules:
  0.0 68.0 jit_solution(1782757471303787958)
XLA Ops:
  0.6 2.9 %near.1 = f32[9,46,8,128]{3,2,1,0:T(8,128)S(1)} custom-call(s32[1]{0:T(128)S(6)} %sub.6.refs_0_, f32[4,36,8,1440]{3,2,1,0:T(8,128)} %bitcast.6, s32[8,1440]{1,0:T(8,128)} %refs_2_.6), custom_call_target="tpu_custom_call" | custom-call | tf_op jit(solution)/shard_map/near/pallas_call | solution.py:98
  3.5 0.0 copy-start.5
  3.5 0.0 copy-start.6
  3.5 0.0 copy-start.7
  3.5 0.0 copy-start.8
  3.6 0.0 copy-start
  3.6 0.0 copy-start.1
  3.6 0.0 copy-start.2
  3.6 0.0 copy-start.3
  3.6 0.1 collective-permute-start.1
  3.7 1.8 %far1.1 = f32[6,46,8,128]{3,2,1,0:T(8,128)S(1)} custom-call(s32[1]{0:T(128)} %bitcast.refs_0_, f32[4,36,8,1440]{3,2,1,0:T(8,128)} %bitcast.7, s32[8,1440]{1,0:T(8,128)} %refs_2_.6), custom_call_target="tpu_custom_call" | custom-call | tf_op jit(solution)/shard_map/far1/pallas_call | solution.py:98
  5.5 3.0 %collective-permute-start = (f32[6,46,8,128]{3,2,1,0:T(8,128)S(1)}, f32[6,46,8,128]{3,2,1,0:T(8,128)}, u32[]{:S(2)}, u32[]{:S(2)}) collective-permute-start(f32[6,46,8,128]{3,2,1,0:T(8,128)S(1)} %far1.1), channel_id=1, source_target_pairs={{1,2},{3,4},{5,6},{7,8},{9,10},{11,12},{13,14},{2,1},{4,3},{6,5},{... | collective-permute-start | bytes 3391496 | tf_op jit(solution)/shard_map/ppermute | solution.py:644
  8.5 1.4 %far2.1 = f32[3,45,8,128]{3,2,1,0:T(8,128)S(1)} custom-call(s32[1]{0:T(128)} %bitcast.refs_0_, f32[4,36,8,1440]{3,2,1,0:T(8,128)} %bitcast.8, s32[8,1440]{1,0:T(8,128)} %refs_2_.6), custom_call_target="tpu_custom_call" | custom-call | tf_op jit(solution)/shard_map/far2/pallas_call | solution.py:98
  9.9 3.4 %collective-permute-start.2 = (f32[3,45,8,128]{3,2,1,0:T(8,128)S(1)}, f32[3,45,8,128]{3,2,1,0:T(8,128)}, u32[]{:S(2)}, u32[]{:S(2)}) collective-permute-start(f32[3,45,8,128]{3,2,1,0:T(8,128)S(1)} %far2.1), channel_id=1, source_target_pairs={{1,2},{3,4},{5,6},{7,8},{9,10},{11,12},{13,14},{2,1},{4,3},{6,5},{... | collective-permute-start | bytes 1658888 | tf_op jit(solution)/shard_map/ppermute | solution.py:644
  13.5 17.1 %own.1 = (f32[18,2,4,12,8,128]{5,4,3,2,1,0:T(8,128)S(1)}, f32[12,8,128]{2,1,0:T(8,128)S(1)}, f32[3,12,8,128]{3,2,1,0:T(8,128)S(1)}, f32[9,8,128]{2,1,0:T(8,128)S(1)}) custom-call(f32[8]{0:T(128)S(1)} %power_multiply_fusion.refs_0_.refs_1_, f32[72]{0:T(128)S(1)} %copy-done.3, s32[1]{0:T(128)} %bitcast.1.refs_2_, s32[8,1440]{1,0:T(8,128)} %refs_2_.6, ...), custom_call_target="tpu_custom_call" | custom-call | tf_op jit(solution)/shard_map/own/pallas_call | solution.py:254
  30.6 0.0 collective-permute-done.1.refs_7_.refs_8_
  30.6 8.5 %finish_near.1 = (f32[4,36,8,1440]{3,2,1,0:T(8,128)}, f32[4,12,8,128]{3,2,1,0:T(8,128)S(1)}) custom-call(s32[1]{0:T(128)} %bitcast.refs_0_, f32[8]{0:T(128)S(1)} %power_multiply_fusion.refs_0_.refs_1_, f32[72]{0:T(128)S(1)} %copy-done.3, f32[9,8,128]{2,1,0:T(8,128)S(1)} %get-tuple-element.18.refs_3_, f32[12,8,128]{2,1,0:T(8,128)S(1)} %get-tuple-element.19.refs_4_, ...), custom_call_target="tpu_custom_call" | custom-call | tf_op jit(solution)/shard_map/finish_near/pallas_call | solution.py:617
  39.1 6.3 %finish_far1.1 = (f32[4,36,8,1440]{3,2,1,0:T(8,128)}, f32[4,12,8,128]{3,2,1,0:T(8,128)S(1)}, f32[4,12,8,128]{3,2,1,0:T(8,128)S(1)}) custom-call(s32[1]{0:T(128)S(6)} %sub.6.refs_0_, f32[8]{0:T(128)S(1)} %power_multiply_fusion.refs_0_.refs_1_, f32[72]{0:T(128)S(1)} %copy-done.3, ...), custom_call_target="tpu_custom_call", output_to_operand_aliasing={{0}: (10, {})} | custom-call | tf_op jit(solution)/shard_map/finish_far1/pallas_call | solution.py:617
  45.4 1.3 %collective-permute-done.2.refs_7_ = f32[3,45,8,128]{3,2,1,0:T(8,128)} collective-permute-done((f32[3,45,8,128]{3,2,1,0:T(8,128)S(1)}, f32[3,45,8,128]{3,2,1,0:T(8,128)}, u32[]{:S(2)}, u32[]{:S(2)}) %collective-permute-start.2) | collective-permute-done | bytes 552992 | tf_op jit(solution)/shard_map/ppermute | solution.py:644
  46.7 4.6 %finish_far2.1 = (f32[4,36,8,1440]{3,2,1,0:T(8,128)}, f32[8,6,8,128]{3,2,1,0:T(8,128)S(1)}) custom-call(s32[1]{0:T(128)S(6)} %sub.6.refs_0_, f32[8]{0:T(128)S(1)} %power_multiply_fusion.refs_0_.refs_1_, f32[72]{0:T(128)S(1)} %copy-done.3, f32[9,8,128]{2,1,0:T(8,128)S(1)} %get-tuple-element.18.refs_3_, ...), custom_call_target="tpu_custom_call", output_to_operand_aliasing={{0}: (9, {})} | custom-call | tf_op jit(solution)/shard_map/finish_far2/pallas_call | solution.py:617
  51.2 15.2 %all_to_all.5 = f32[8,6,8,128]{3,2,1,0:T(8,128)S(1)} all-to-all(f32[8,6,8,128]{3,2,1,0:T(8,128)S(1)} %get-tuple-element.28), channel_id=1, replica_groups=mesh['bins'=8,'tiles'=16] {'bins'}, dimensions={0} | all-to-all | bytes 393216 | tf_op jit(solution)/shard_map/all_to_all | solution.py:696
  66.5 0.1 fusion.1
  66.6 0.7 %slice.32 = f32[2,8,2,90]{3,2,1,0:T(2,128)} reshape(f32[2,8,180]{2,1,0:T(8,128)S(1)} %get-tuple-element.30) | data formatting | bytes 23040 | tf_op jit(solution)/shard_map/slice | solution.py:701
  67.3 0.7 %slice.34 = f32[2,8,2,90]{3,2,1,0:T(2,128)} reshape(f32[2,8,180]{2,1,0:T(8,128)S(1)} %get-tuple-element.29) | data formatting | bytes 23040 | tf_op jit(solution)/shard_map/slice | solution.py:701
  (16 shorter events, 0.1 us)
Async XLA Ops:
  3.5 9.8 %copy-start.5 = (s32[8]{0:T(128)S(1)}, s32[8]{0:T(128)}, u32[]{:S(2)}) copy-start(s32[8]{0:T(128)} %constant.47.clone) | copy-start | bytes 100
  3.5 9.8 %copy-start.6 = (pred[8]{0:T(512)(128)(4,1)S(1)}, pred[8]{0:T(512)(128)(4,1)}, u32[]{:S(2)}) copy-start(pred[8]{0:T(512)(128)(4,1)} %constant.48.clone) | copy-start | bytes 28
  3.5 9.8 %copy-start.7 = (f32[8]{0:T(128)S(1)}, f32[8]{0:T(128)}, u32[]{:S(2)}) copy-start(f32[8]{0:T(128)} %constant.56) | copy-start | bytes 100
  3.5 9.8 %copy-start.8 = (f32[8]{0:T(128)S(1)}, f32[8]{0:T(128)}, u32[]{:S(2)}) copy-start(f32[8]{0:T(128)} %constant.57) | copy-start | bytes 100
  3.6 9.9 %copy-start = (s32[8,1440]{1,0:T(8,128)S(1)}, s32[8,1440]{1,0:T(8,128)}, u32[]{:S(2)}) copy-start(s32[8,1440]{1,0:T(8,128)} %refs_4_.1) | copy-start | bytes 138244
  3.6 9.9 %copy-start.1 = (f32[8,1440]{1,0:T(8,128)S(1)}, f32[8,1440]{1,0:T(8,128)}, u32[]{:S(2)}) copy-start(f32[8,1440]{1,0:T(8,128)} %refs_5_.1) | copy-start | bytes 138244
  3.6 9.9 %copy-start.2 = (f32[8,1440]{1,0:T(8,128)S(1)}, f32[8,1440]{1,0:T(8,128)}, u32[]{:S(2)}) copy-start(f32[8,1440]{1,0:T(8,128)} %refs_6_.1) | copy-start | bytes 138244
  3.6 9.9 %copy-start.3 = (f32[72]{0:T(128)S(1)}, f32[72]{0:T(128)}, u32[]{:S(2)}) copy-start(f32[72]{0:T(128)} %constant.49.clone.refs_1_.refs_2_) | copy-start | bytes 868
  3.6 27.0 %collective-permute-start.1 = (f32[9,46,8,128]{3,2,1,0:T(8,128)S(1)}, f32[9,46,8,128]{3,2,1,0:T(8,128)}, u32[]{:S(2)}, u32[]{:S(2)}) collective-permute-start(f32[9,46,8,128]{3,2,1,0:T(8,128)S(1)} %near.1), channel_id=1, source_target_pairs={{0,1},{2,3},{4,5},{6,7},{8,9},{10,11},{12,13},{14,15},{1,0},{3,2},... | collective-permute-start | bytes 5087240 | tf_op jit(solution)/shard_map/ppermute | solution.py:644
  5.5 33.6 %collective-permute-start = (f32[6,46,8,128]{3,2,1,0:T(8,128)S(1)}, f32[6,46,8,128]{3,2,1,0:T(8,128)}, u32[]{:S(2)}, u32[]{:S(2)}) collective-permute-start(f32[6,46,8,128]{3,2,1,0:T(8,128)S(1)} %far1.1), channel_id=1, source_target_pairs={{1,2},{3,4},{5,6},{7,8},{9,10},{11,12},{13,14},{2,1},{4,3},{6,5},{... | collective-permute-start | bytes 3391496 | tf_op jit(solution)/shard_map/ppermute | solution.py:644
  9.9 36.8 %collective-permute-start.2 = (f32[3,45,8,128]{3,2,1,0:T(8,128)S(1)}, f32[3,45,8,128]{3,2,1,0:T(8,128)}, u32[]{:S(2)}, u32[]{:S(2)}) collective-permute-start(f32[3,45,8,128]{3,2,1,0:T(8,128)S(1)} %far2.1), channel_id=1, source_target_pairs={{1,2},{3,4},{5,6},{7,8},{9,10},{11,12},{13,14},{2,1},{4,3},{6,5},{... | collective-permute-start | bytes 1658888 | tf_op jit(solution)/shard_map/ppermute | solution.py:644
  39.1 7.6 %copy-start.4 = (s32[1,16]{1,0:T(1,128)S(1)}, s32[1,16]{1,0:T(1,128)}, u32[]{:S(2)}) copy-start(s32[1,16]{1,0:T(1,128)} %refs_10_.1) | copy-start | bytes 196
